TPU v7x, 32 devices: a whole 2x2x4 slice. The times are simulated.
32 devices in a mesh: grp: 2 (over x), tmpl: 16 (over z, y, core).
Axes of the slice: x: 2, y: 2, z: 4, core: 2. Of those that a mesh axis runs over, the one named last changes fastest.
Arguments:
- strain: float32 [16, 512, 1024], P('grp', None, 'tmpl'), parts along dimension 0, may hold values from -6 to 6
- analysis: float32 [1024, 1024], P('grp', 'tmpl'), parts along dimension 0, may hold values from -6 to 6
- bank: bfloat16 [2, 16, 512, 512], P(None, None, 'tmpl'), may hold values from -6 to 6
- cutoff: int32 [16], replicated, may hold values from 65536 to 262144
- order: int32 [16], replicated, may hold values from 0 to 15, each once
Outputs:
- snr: bfloat16 [32, 512, 1024], P(('grp', 'tmpl')), parts along dimension 0
There are 2 independent parts, one for each index of `grp`. A program takes and returns all parts, laid end to end along the dimension named above; an argument that names none is the same for every part. Nothing has to cross between parts.
Inputs may be any that keep to these rules, and one draw needn't show every extreme that they name: `order`: a permutation of the bank's templates.
All inputs are finite; a program needn't handle non-finite values.
Results may differ from a plain program's by a relative error of at most 0.013.
Values may be sent and summed in bfloat16 or wider, within the bound.
No kernel may reach another device: no remote copies, remote signals or barrier semaphores. Data moves between devices by JAX's collectives and lax.ppermute only.
A program may use at most 64 MiB of HBM per device.

v0:
```python
import functools
import math

import jax
import jax.numpy as jnp
import numpy as np
from jax import lax
from jax.experimental import pallas as pl
from jax.experimental.pallas import tpu as pltpu
from jax.sharding import PartitionSpec as P

BF16 = jnp.bfloat16
F32 = jnp.float32
STEP = 16
NEAR = (0, 2, 4, 12, 6, 14, 8, 10)


def turns(product, period):
    angle = (product % period) * (2.0 * math.pi / period)
    return np.cos(angle).astype(np.float32), np.sin(angle).astype(np.float32)


def matmul(left, right):
    return jnp.dot(left, right, preferred_element_type=F32)


def matmul_nt(left, right):
    return lax.dot_general(left, right, (((1,), (1,)), ((), ())), preferred_element_type=F32)


def vmem(shape, dtype=BF16):
    return pltpu.VMEM(shape, dtype)


def whole():
    return pl.BlockSpec(memory_space=pltpu.VMEM)


def outside():
    return pl.BlockSpec(memory_space=pltpu.HBM)


def in_hbm(*arrays):
    return [pltpu.with_memory_space_constraint(jnp.asarray(array), pltpu.HBM) for array in arrays]


def position():
    return lax.axis_index("tmpl"), lax.axis_index("grp")


def start_copies(pairs, sems):
    copies = [
        pltpu.make_async_copy(source, target, sems.at[at]) for at, (source, target) in enumerate(pairs)
    ]
    for copy in copies:
        copy.start()
    return copies


def params(mib):
    return pltpu.CompilerParams(vmem_limit_bytes=mib << 20)


def halves(count):
    return np.concatenate([np.arange(0, count, 2), np.arange(1, count, 2)])


def aligned(start, size):
    return pl.ds(pl.multiple_of(start, size), size)


def stage_one_kernel(
    order, strain_hbm, analysis_hbm, spin_hbm, win_c_hbm, win_s_hbm, cos_hbm, sin_hbm, bank, out,
    strain, analysis, spin, win_c, win_s, cos, sin, packed, sems, bank_sems,
):
    segs, cols, _ = strain.shape
    tail = segs * cols
    templates, half_len = bank.shape[1], bank.shape[3]
    rows = out.shape[0] // templates
    place, group = position()
    sources = [
        (spin_hbm.at[place], spin),
        (win_c_hbm, win_c),
        (win_s_hbm, win_s),
        *[(strain_hbm.at[seg], strain.at[seg]) for seg in range(segs)],
        (analysis_hbm, analysis),
        (cos_hbm, cos),
        (sin_hbm, sin),
    ]
    copies = start_copies(sources, sems)
    lane = 2 * (tail + cols)
    bank_pairs = []
    for row in range(templates):
        for part in range(2):
            bank_pairs.append(
                (
                    bank.at[part, order[row], aligned(group * rows, rows), :],
                    out.at[
                        row * rows : (row + 1) * rows,
                        lane + part * half_len : lane + (part + 1) * half_len,
                    ],
                )
            )
    bank_copies = start_copies(bank_pairs, bank_sems)
    for copy in copies[:3]:
        copy.wait()
    scale = 0.5 * math.sqrt(8.0 / 3.0)
    window = scale - scale * (win_c[...] * spin[0:1, :] - win_s[...] * spin[1:2, :])
    for seg in range(segs):
        copies[3 + seg].wait()
        packed[seg * cols : (seg + 1) * cols, :] = (strain[seg] * window).astype(BF16)
    for copy in copies[3 + segs :]:
        copy.wait()
    packed[tail:, :] = analysis[...].astype(BF16)
    real = matmul_nt(cos[...], packed[...])
    imag = -matmul_nt(sin[...], packed[...])
    out[:, 0:tail] = real[:, :tail].astype(BF16)
    out[:, tail : 2 * tail] = imag[:, :tail].astype(BF16)
    joined = jnp.concatenate([real[:, tail:], imag[:, tail:]], 1)
    out[:, 2 * tail : lane] = joined.astype(BF16)
    for copy in bank_copies:
        copy.wait()


def tables_kernel(
    fore_c, fore_s, fore_rc, fore_rs, even_c, even_s, odd_c, odd_s, rows_rc, rows_rs,
    lift_c, lift_s, lift_rc, lift_rs, mid_c, mid_s,
    forward_hbm, even_hbm, odd_hbm, lift_c_hbm, lift_s_hbm,
    forward, even_out, odd_out, lift_out_c, lift_out_s, sems,
):
    half_len = fore_c.shape[1]
    second_len = 2 * half_len

    def turn(cos, sin, by_cos, by_sin):
        return cos * by_cos - sin * by_sin, sin * by_cos + cos * by_sin

    first_lane = lax.broadcasted_iota(jnp.int32, fore_c.shape, 1) == 0
    sign = 1.0 - 2.0 * (lax.broadcasted_iota(jnp.int32, fore_c.shape, 0) % 2).astype(F32)

    def fore(step, carry):
        cos, sin = carry
        forward[aligned(step * STEP, STEP), 0:half_len] = cos.astype(BF16)
        forward[aligned(step * STEP, STEP), half_len:] = jnp.where(first_lane, sign, sin).astype(BF16)
        return turn(cos, sin, fore_rc[...], fore_rs[...])

    lax.fori_loop(0, second_len // STEP, fore, (fore_c[...], fore_s[...]))
    quarter = half_len // 2

    def spread(out, cos, sin):
        def body(step, carry):
            cos, sin = carry
            upper = aligned(step * STEP, STEP)
            lower = aligned(quarter + step * STEP, STEP)
            out[upper, 0:half_len] = cos.astype(BF16)
            out[upper, half_len:] = sin.astype(BF16)
            out[lower, 0:half_len] = (-sin).astype(BF16)
            out[lower, half_len:] = cos.astype(BF16)
            return turn(cos, sin, rows_rc[...], rows_rs[...])

        lax.fori_loop(0, quarter // STEP, body, (cos, sin))

    spread(even_out, even_c[...], even_s[...])
    spread(odd_out, odd_c[...], odd_s[...])
    per = lift_out_c.shape[0] // 2

    for parity in range(2):

        def lifts(step, carry, parity=parity):
            cos, sin = carry
            at = aligned(parity * per + step * STEP, STEP)
            lift_out_c[at, :] = cos.astype(BF16)
            lift_out_s[at, :] = sin.astype(BF16)
            return turn(cos, sin, lift_rc[...], lift_rs[...])

        lax.fori_loop(0, per // STEP, lifts, (lift_c[parity], lift_s[parity]))
    lift_out_c[0:STEP, :] = mid_c[...].astype(BF16)
    lift_out_s[0:STEP, :] = mid_s[...].astype(BF16)
    made = [forward, even_out, odd_out, lift_out_c, lift_out_s]
    kept = [forward_hbm, even_hbm, odd_hbm, lift_c_hbm, lift_s_hbm]
    for copy in start_copies(list(zip(made, kept)), sems):
        copy.wait()


def stage_two_kernel(
    segs, cols, moved, near_c_hbm, near_s_hbm, base_c_hbm, base_s_hbm, mid_c_hbm, mid_s_hbm, forward_hbm, out,
    near_c, near_s, base_c, base_s, mid_c, mid_s, forward, stacked, middle, sems,
):
    place, _ = position()
    pairs = [
        (near_c_hbm, near_c),
        (near_s_hbm, near_s),
        (base_c_hbm.at[place], base_c),
        (base_s_hbm.at[place], base_s),
        (mid_c_hbm, mid_c),
        (mid_s_hbm, mid_s),
        (forward_hbm, forward),
    ]
    copies = start_copies(pairs, sems)
    sources, rows, _ = moved.shape
    second_len = forward.shape[0]
    half_len = second_len // 2
    quarter = half_len // 2
    tail = segs * cols
    all_rows = (segs + 1) * rows
    width = 2 * cols
    low = lax.broadcasted_iota(jnp.int32, (rows, width), 1) < cols
    own_first = place == 0
    packed_row = lax.broadcasted_iota(jnp.int32, (rows, width), 0) == 0
    drop = jnp.logical_and(packed_row, own_first)

    def pair(left, right):
        return (
            jnp.where(low, left, pltpu.roll(right, cols, 1)),
            jnp.where(low, pltpu.roll(left, cols, 1), right),
        )

    middle[...] = jnp.zeros_like(middle)
    for copy in copies[:-1]:
        copy.wait()
    for tile in range(sources // 2):
        lane = slice(tile * width, (tile + 1) * width)
        by_cos, by_sin = base_c[:, lane], base_s[:, lane]
        cos = near_c[:, lane] * by_cos - near_s[:, lane] * by_sin
        sin = near_s[:, lane] * by_cos + near_c[:, lane] * by_sin

        def piece(lo, tile=tile):
            hi = lo + width
            return pair(
                moved[2 * tile, :, lo:hi].astype(F32), moved[2 * tile + 1, :, lo:hi].astype(F32)
            )

        def put(seg, real, imag, lane=lane, cos=cos, sin=sin):
            middle[seg : seg + 1, lane] = imag[0:1, :] * mid_c[:, lane]
            middle[rows + seg : rows + seg + 1, lane] = -imag[0:1, :] * mid_s[:, lane]
            imag = jnp.where(drop, 0.0, imag)
            at = seg * rows
            stacked[at : at + rows, lane] = (real * cos + imag * sin).astype(BF16)
            at += all_rows
            stacked[at : at + rows, lane] = (imag * cos - real * sin).astype(BF16)

        for twin in range(segs // 2):
            real_one, real_two = piece(twin * width)
            imag_one, imag_two = piece(tail + twin * width)
            put(2 * twin, real_one, imag_one)
            put(2 * twin + 1, real_two, imag_two)
        real, imag = piece(2 * tail)
        put(segs, real, imag)
    stacked[2 * all_rows :, :] = middle[...].astype(BF16)

    copies[-1].wait()
    first_lane = lax.broadcasted_iota(jnp.int32, (rows, half_len), 1) == 0

    def both(at, lower_at):
        upper = matmul(stacked[at : at + rows, :], forward[...])
        lower = matmul(stacked[lower_at : lower_at + rows, :], forward[...])
        rc, rs = upper[:, :half_len], upper[:, half_len:]
        ic, imag_s = lower[:, :half_len], lower[:, half_len:]
        rz, iz = jnp.where(first_lane, 0.0, rs), jnp.where(first_lane, 0.0, imag_s)
        direct = (rc + iz, ic - rz)
        mirror = (jnp.where(first_lane, rs, rc - iz), -jnp.where(first_lane, imag_s, ic + rz))
        return direct, mirror

    zero = jnp.zeros((rows, half_len), F32)
    level, mirror_level = zero, zero
    for seg in range(segs):
        (real, imag), (mirror_real, mirror_imag) = both(seg * rows, all_rows + seg * rows)
        level = level + (real * real + imag * imag)
        mirror_level = mirror_level + (mirror_real * mirror_real + mirror_imag * mirror_imag)
    direct, mirror = both(segs * rows, all_rows + segs * rows)
    _, (mid_real, mid_imag) = both(2 * all_rows, 2 * all_rows + rows)
    mid_level = jnp.sum((mid_real * mid_real + mid_imag * mid_imag)[:segs], 0, keepdims=True)
    swap = jnp.logical_and(lax.broadcasted_iota(jnp.int32, (rows, half_len), 0) == 0, own_first)
    mirror_level = jnp.where(swap, mid_level, mirror_level)
    mirror_real = jnp.where(swap, mid_real[segs : segs + 1], mirror[0])
    mirror_imag = jnp.where(swap, mid_imag[segs : segs + 1], mirror[1])
    floor = 0.2 * (second_len * 2 * sources * rows)

    def whiten(level, real, imag):
        level = jnp.maximum(level * (1.0 / segs), floor)
        return real / level, imag / level, 1.0 / level

    def ordered(table):
        return jnp.concatenate([table[:, quarter:], pltpu.roll(table[:, :quarter], quarter - 1, 1)], 1)

    upper = whiten(level, *direct)
    lower = [ordered(table) for table in whiten(mirror_level, mirror_real, mirror_imag)]
    eighth = rows // 2
    for part in range(3):
        lane = slice(part * half_len, (part + 1) * half_len)
        for parity in range(2):
            at = slice(parity * eighth, (parity + 1) * eighth)
            block = jnp.concatenate([upper[part][at], lower[part][at]], 0)
            out[parity * rows : (parity + 1) * rows, lane] = block.astype(BF16)


def choose_kernel(order, cuts, own, other, out, held, bins):
    place, group = position()
    rows, sources = own.shape[1], own.shape[0]
    per = sources * rows
    first_len, half_len = 2 * per, own.shape[2] // 2
    for source in range(sources):
        held[source * rows : (source + 1) * rows, :] = own[source]
        held[per + source * rows : per + (source + 1) * rows, :] = other[source]
    cut = cuts[order[place]]

    def bin_of(lane):
        return jnp.where(lane < half_len // 2, 2 * lane, 2 * lane - half_len + 1)

    def one_hot(mask):
        return jnp.where(mask, 1.0, 0.0).astype(BF16)

    deep = 128
    wide_row = lax.broadcasted_iota(jnp.int32, (deep, half_len), 0)
    wide_lane = lax.broadcasted_iota(jnp.int32, (deep, half_len), 1)
    for block in range(half_len // deep):
        bins[block * deep : (block + 1) * deep, :] = one_hot(wide_row + block * deep == bin_of(wide_lane))

    def body(step, carry):
        at = step * deep + wide_row
        inner = at % per
        packed = (inner // rows) * rows + 2 * (at % (rows // 2)) + at // per
        mirrored = (at % rows) >= rows // 2
        turned = jnp.where(packed == 0, first_len // 2, first_len - packed)
        row = jnp.where(mirrored, turned, packed)
        share = (row // rows) % 2
        column = (row // (2 * rows)) * rows + row % rows + jnp.where(share == group, 0, per)
        picked = matmul(one_hot(column == wide_lane), held[...]).astype(BF16)
        in_band = row + first_len * bin_of(wide_lane) < cut
        for part in range(2):
            lane = slice(part * half_len, (part + 1) * half_len)
            moved = matmul(picked[:, lane], bins[...])
            out[aligned(step * deep, deep), lane] = jnp.where(in_band, moved, 0.0).astype(BF16)
        return carry

    lax.fori_loop(0, first_len // deep, body, 0)


def inverse_kernel(
    near, far, chosen, even_table, odd_table, lift_c, lift_s, cols_table, out, filtered, lifted
):
    place, _ = position()
    half_len = even_table.shape[0]
    second_len = 2 * half_len
    first_len = filtered.shape[0]
    per = first_len // 2
    quarter = half_len // 2
    rows = near.shape[1] // 2
    norm = jnp.zeros((rows, half_len), F32)
    for blocks, turned in ((near, 0), (far, 1)):
        for block, offset in enumerate(NEAR):
            device = jnp.bitwise_xor(place, offset ^ turned)
            for parity in range(2):
                row = slice(parity * rows, (parity + 1) * rows)
                at = aligned(parity * per + device * rows, rows)
                white_real = blocks[block, row, :half_len].astype(F32)
                white_imag = blocks[block, row, half_len : 2 * half_len].astype(F32)
                weight = blocks[block, row, 2 * half_len :].astype(F32)
                real = chosen[at, :half_len].astype(F32)
                imag = chosen[at, half_len:].astype(F32)
                norm = norm + (real * real + imag * imag) * weight
                filt_real = (white_real * real + white_imag * imag).astype(BF16)
                filt_imag = (white_imag * real - white_real * imag).astype(BF16)
                filtered[at, 0:quarter] = filt_real[:, :quarter]
                filtered[at, quarter:half_len] = filt_imag[:, :quarter]
                filtered[at, half_len : half_len + quarter] = filt_real[:, quarter:]
                filtered[at, half_len + quarter :] = filt_imag[:, quarter:]
    scale = lax.rsqrt(jnp.sum(norm, keepdims=True))
    deep = 128

    def lift(step, carry):
        at = aligned(step * deep, deep)
        even = matmul(filtered[at, :half_len], even_table[...])
        odd = matmul(filtered[at, half_len:], odd_table[...])
        parity = step // (per // deep)
        target = parity * first_len + (step - parity * (per // deep)) * deep
        for upper in range(2):
            lane = slice(upper * half_len, (upper + 1) * half_len)
            total = even - odd if upper else even + odd
            real, imag = total[:, :half_len], total[:, half_len:]
            cos, sin = lift_c[at, lane].astype(F32), lift_s[at, lane].astype(F32)
            lifted[aligned(target, deep), lane] = (real * cos - imag * sin).astype(BF16)
            lifted[aligned(target + per, deep), lane] = (real * sin + imag * cos).astype(BF16)
        return carry

    lax.fori_loop(0, first_len // deep, lift, 0)
    tall = 64
    wide = 512

    def field(step, carry):
        upper = aligned(step * tall, tall)
        lower = aligned(per + step * tall, tall)
        for lane in range(0, second_len, wide):
            at = slice(lane, lane + wide)
            even, odd = lifted[:first_len, at], lifted[first_len:, at]
            even_real = matmul(cols_table[upper, :first_len], even)
            even_imag = matmul(cols_table[lower, :first_len], even)
            odd_real = matmul(cols_table[upper, first_len:], odd)
            odd_imag = matmul(cols_table[lower, first_len:], odd)
            real, imag = even_real + odd_real, even_imag + odd_imag
            out[0, upper, at] = (jnp.sqrt(real * real + imag * imag) * scale).astype(BF16)
            real, imag = even_real - odd_real, even_imag - odd_imag
            out[0, lower, at] = (jnp.sqrt(real * real + imag * imag) * scale).astype(BF16)
        return carry

    lax.fori_loop(0, per // tall, field, 0)


def swap_with(array, flip):
    pairs = [(at, at ^ flip) for at in range(lax.axis_size("tmpl"))]
    return lax.ppermute(array, "tmpl", pairs)


def tiled_local(strain, analysis, bank, cutoff, order):
    dev_count = lax.axis_size("tmpl")
    segs, first_len, cols = strain.shape
    second_len = cols * dev_count
    length = first_len * second_len
    half_len = second_len // 2
    rows = first_len // dev_count // 2
    templates = order.shape[0]
    lanes = 2 * (segs + 1) * cols

    first, second, half = np.arange(first_len), np.arange(second_len), np.arange(half_len)
    devices, step = np.arange(dev_count), np.arange(STEP)
    near = halves(rows)
    packed = (devices[:, None] * rows + near[None, :]).reshape(-1, 1)
    cos_one, sin_one = turns(packed * first[None, :], first_len)
    sin_one[0] = 2 * (first % 2) - 1.0
    win_c, win_s = turns(np.arange(cols)[:, None] + second_len * first[None, :], length)
    spin = np.stack(turns(cols * devices, length), 1)[:, :, None] * np.ones((1, 1, first_len), np.float32)

    sent = pl.pallas_call(
        stage_one_kernel,
        grid_spec=pltpu.PrefetchScalarGridSpec(
            num_scalar_prefetch=1,
            grid=(),
            in_specs=[outside()] * 8,
            out_specs=whole(),
            scratch_shapes=[
                vmem((segs, cols, first_len), F32),
                vmem((cols, first_len), F32),
                vmem((2, first_len), F32),
                vmem((cols, first_len), F32),
                vmem((cols, first_len), F32),
                vmem((dev_count * rows, first_len)),
                vmem((dev_count * rows, first_len)),
                vmem(((segs + 1) * cols, first_len)),
                pltpu.SemaphoreType.DMA((segs + 6,)),
                pltpu.SemaphoreType.DMA((2 * templates,)),
            ],
        ),
        out_shape=jax.ShapeDtypeStruct((dev_count * rows, lanes + 2 * half_len), BF16),
        compiler_params=params(16),
        name="stage_one",
    )(
        order,
        *in_hbm(
            jnp.swapaxes(strain, 1, 2), jnp.swapaxes(analysis, 0, 1), spin, win_c, win_s,
            cos_one.astype(BF16), sin_one.astype(BF16), bank,
        ),
    )
    moved = lax.all_to_all(
        sent.reshape(dev_count, rows, lanes + 2 * half_len), "tmpl", split_axis=0, concat_axis=0, tiled=True
    )
    own = moved[:, :, lanes:]
    other = lax.ppermute(own, "grp", [(0, 1), (1, 0)])

    split = halves(half_len)
    low = 2 * np.arange(rows // 2)
    lift_rows = [np.concatenate([low + odd, first_len - low - odd]) for odd in range(2)]
    lift_init = [turns(at[:, None] * second[None, :], length) for at in lift_rows]
    mid_rows = lift_rows[0].copy()
    mid_rows[rows // 2] = first_len // 2
    step_sign = np.where(np.arange(rows) < rows // 2, rows, -rows)
    tables = [
        *turns(step[:, None] * split[None, :], second_len),
        *turns(STEP * split[None, :], second_len),
        *turns(2 * step[:, None] * half[None, :], second_len),
        *turns((2 * step[:, None] + 1) * half[None, :], second_len),
        *turns(2 * STEP * half[None, :], second_len),
        np.stack([lift_init[0][0], lift_init[1][0]]),
        np.stack([lift_init[0][1], lift_init[1][1]]),
        *turns(step_sign[:, None] * second[None, :], length),
        *turns(mid_rows[:, None] * second[None, :], length),
    ]
    shapes = [(second_len, second_len)] + [(half_len, second_len)] * 2 + [(first_len, second_len)] * 2
    forward, even_table, odd_table, lift_c, lift_s = pl.pallas_call(
        tables_kernel,
        out_shape=[pltpu.HBM(shape, BF16) for shape in shapes],
        in_specs=[whole()] * len(tables),
        out_specs=[outside()] * len(shapes),
        scratch_shapes=[*[vmem(shape) for shape in shapes], pltpu.SemaphoreType.DMA((len(shapes),))],
        compiler_params=params(24),
        cost_estimate=pl.CostEstimate(flops=10**7, bytes_accessed=2 * 10**7, transcendentals=0),
        name="tables",
    )(*in_hbm(*tables))

    near_c, near_s = turns(near[:, None] * second[None, :], length)
    base_c, base_s = turns(rows * devices[:, None, None] * second[None, None, :], length)
    mid_c, mid_s = turns(first_len // 2 * second[None, :], length)
    all_rows = 2 * (segs + 2) * rows
    stage_two = pl.pallas_call(
        functools.partial(stage_two_kernel, segs, cols),
        out_shape=jax.ShapeDtypeStruct((2 * rows, 3 * half_len), BF16),
        in_specs=[whole()] + [outside()] * 7,
        out_specs=whole(),
        scratch_shapes=[
            vmem((rows, second_len), F32),
            vmem((rows, second_len), F32),
            *[vmem((1, second_len), F32)] * 4,
            vmem(forward.shape),
            vmem((all_rows, second_len)),
            vmem((2 * rows, second_len), F32),
            pltpu.SemaphoreType.DMA((7,)),
        ],
        compiler_params=params(24),
        cost_estimate=pl.CostEstimate(flops=10**9, bytes_accessed=4 * 10**6, transcendentals=0),
        name="stage_two",
    )
    block = stage_two(moved, *in_hbm(near_c, near_s, base_c, base_s, mid_c, mid_s, forward))

    beside, one, two = swap_with(block, 2), swap_with(block, 4), swap_with(block, 12)
    both = swap_with(jnp.stack([one, two]), 2)
    far = swap_with(two, 4)
    last = swap_with(far, 2)
    mine = jnp.stack([block, beside, one, two, both[0], both[1], far, last])
    theirs = swap_with(mine, 1)

    choose = pl.pallas_call(
        choose_kernel,
        grid_spec=pltpu.PrefetchScalarGridSpec(
            num_scalar_prefetch=2,
            grid=(),
            in_specs=[whole()] * 2,
            out_specs=whole(),
            scratch_shapes=[vmem((first_len, 2 * half_len)), vmem((half_len, half_len))],
        ),
        out_shape=jax.ShapeDtypeStruct((first_len, 2 * half_len), BF16),
        compiler_params=params(16),
        cost_estimate=pl.CostEstimate(flops=10**9, bytes_accessed=4 * 10**6, transcendentals=0),
        name="choose",
    )
    chosen = choose(order, cutoff, own, other)

    per = first_len // 2
    cols_parts = []
    for odd in range(2):
        straight = devices[:, None] * rows + low[None, :] + odd
        turned = first_len - straight
        turned[straight == 0] = first_len // 2
        at = np.concatenate([straight, turned], 1).reshape(-1)
        cos, sin = turns(np.arange(per)[:, None] * at[None, :], first_len)
        cols_parts.append(np.block([[cos, -sin], [sin, cos]]))
    cols_table = jnp.asarray(np.concatenate(cols_parts, 1), BF16)
    return pl.pallas_call(
        inverse_kernel,
        out_shape=jax.ShapeDtypeStruct((1, first_len, second_len), BF16),
        in_specs=[whole()] * 8,
        out_specs=whole(),
        scratch_shapes=[vmem((first_len, 2 * half_len)), vmem((2 * first_len, second_len))],
        compiler_params=params(24),
        name="inverse",
    )(mine, theirs, chosen, even_table, odd_table, lift_c, lift_s, cols_table)


def angles(left_idx, right_idx, period):
    product = left_idx[:, None] * right_idx[None, :] % period
    phase_angle = product.astype(jnp.float32) * (2.0 * math.pi / period)
    return (jnp.cos(phase_angle), jnp.sin(phase_angle))


def filtered(white_pair, tmpl_pair, cut_bins, freq_bin):
    white_real = white_pair[0].astype(jnp.float32)
    white_imag = white_pair[1].astype(jnp.float32)
    tmpl_real = tmpl_pair[0].astype(jnp.float32)
    tmpl_imag = tmpl_pair[1].astype(jnp.float32)
    in_band = freq_bin[None] < cut_bins[:, None, None]
    filt_real = jnp.where(in_band, white_real * tmpl_real + white_imag * tmpl_imag, 0.0)
    filt_imag = jnp.where(in_band, white_imag * tmpl_real - white_real * tmpl_imag, 0.0)
    return jnp.concatenate([filt_real, filt_imag], -1).astype(jnp.bfloat16)


def inverse_rows(stacked, row_bins, second_len, length):
    half_len = second_len // 2
    cosine, sine = angles(
        jnp.arange(half_len, dtype=jnp.int32), jnp.arange(second_len, dtype=jnp.int32), second_len
    )
    dft_table = jnp.concatenate(
        [jnp.concatenate([cosine, sine], 1), jnp.concatenate([-sine, cosine], 1)], 0
    ).astype(jnp.bfloat16)
    spread = jnp.einsum("tkf,fg->tkg", stacked, dft_table, preferred_element_type=jnp.float32)
    spread_real = spread[..., :second_len]
    spread_imag = spread[..., second_len:]
    cos_twist, sin_twist = angles(row_bins, jnp.arange(second_len, dtype=jnp.int32), length)
    lift_real = spread_real * cos_twist - spread_imag * sin_twist
    lift_imag = spread_real * sin_twist + spread_imag * cos_twist
    return jnp.concatenate([lift_real, lift_imag], -1).astype(jnp.bfloat16)


def inverse_cols(lifted, first_len, second_len):
    row_idx = jnp.arange(first_len, dtype=jnp.int32)
    cosine, sine = angles(row_idx, row_idx, first_len)
    cosine = cosine.astype(jnp.bfloat16)
    sine = sine.astype(jnp.bfloat16)
    lift_real = lifted[..., :second_len]
    lift_imag = lifted[..., second_len:]
    field_real = jnp.einsum(
        "ak,tkb->tab", cosine, lift_real, preferred_element_type=jnp.float32
    ) - jnp.einsum("ak,tkb->tab", sine, lift_imag, preferred_element_type=jnp.float32)
    field_imag = jnp.einsum(
        "ak,tkb->tab", sine, lift_real, preferred_element_type=jnp.float32
    ) + jnp.einsum("ak,tkb->tab", cosine, lift_imag, preferred_element_type=jnp.float32)
    return (field_real, field_imag)


def plain_local(strain, analysis, bank, cutoff, order):
    highest = lax.Precision.HIGHEST
    dev_count = lax.axis_size("tmpl")
    my_index = lax.axis_index("tmpl")
    seg_count = strain.shape[0]
    first_len = strain.shape[1]
    col_count = strain.shape[2]
    second_len = col_count * dev_count
    length = first_len * second_len
    half_len = second_len // 2
    row_count = first_len // dev_count
    row_idx = jnp.arange(first_len, dtype=jnp.int32)
    col_index = my_index * col_count + jnp.arange(col_count, dtype=jnp.int32)
    sample_idx = row_idx[:, None] * second_len + col_index[None, :]
    window = (
        math.sqrt(8.0 / 3.0) * jnp.sin(sample_idx.astype(jnp.float32) * (math.pi / length)) ** 2
    )
    series = jnp.concatenate([strain * window, analysis[None]], 0)
    cos_one, sin_one = angles(row_idx, row_idx, first_len)
    part_real = jnp.einsum("ka,sab->skb", cos_one, series, precision=highest)
    part_imag = -jnp.einsum("ka,sab->skb", sin_one, series, precision=highest)
    cos_twist, sin_twist = angles(row_idx, col_index, length)
    twist_real = part_real * cos_twist + part_imag * sin_twist
    twist_imag = part_imag * cos_twist - part_real * sin_twist
    moved = lax.all_to_all(
        jnp.stack([twist_real, twist_imag]).astype(jnp.bfloat16),
        "tmpl",
        split_axis=2,
        concat_axis=3,
        tiled=True,
    ).astype(jnp.float32)
    cos_two, sin_two = angles(
        jnp.arange(second_len, dtype=jnp.int32), jnp.arange(half_len, dtype=jnp.int32), second_len
    )
    spec_real = jnp.einsum("skb,bf->skf", moved[0], cos_two, precision=highest) + jnp.einsum(
        "skb,bf->skf", moved[1], sin_two, precision=highest
    )
    spec_imag = jnp.einsum("skb,bf->skf", moved[1], cos_two, precision=highest) - jnp.einsum(
        "skb,bf->skf", moved[0], sin_two, precision=highest
    )
    power_spec = jnp.maximum(
        jnp.mean(spec_real[:seg_count] ** 2 + spec_imag[:seg_count] ** 2, axis=0), 0.2 * length
    )
    whitened = jnp.stack(
        [spec_real[seg_count] / power_spec, spec_imag[seg_count] / power_spec]
    ).astype(jnp.bfloat16)
    own_rows = my_index * row_count + jnp.arange(row_count, dtype=jnp.int32)
    half_idx = jnp.arange(half_len, dtype=jnp.int32)
    freq_local = own_rows[:, None] + first_len * half_idx[None, :]
    chosen = jnp.take(bank, order, axis=1)
    cuts = jnp.take(cutoff, order)
    bank_real = chosen[0].astype(jnp.float32)
    bank_imag = chosen[1].astype(jnp.float32)
    in_band = freq_local[None] < cuts[:, None, None]
    local_norm = jnp.sum(
        jnp.where(in_band, (bank_real**2 + bank_imag**2) / power_spec, 0.0), axis=(1, 2)
    )
    norm_sq = lax.psum(local_norm, "tmpl")
    per_device = cuts.shape[0] // dev_count
    own_norm = lax.dynamic_slice_in_dim(norm_sq, my_index * per_device, per_device)
    stacked = filtered(whitened, chosen, cuts, freq_local)
    lifted = lax.all_to_all(
        inverse_rows(stacked, own_rows, second_len, length),
        "tmpl",
        split_axis=0,
        concat_axis=1,
        tiled=True,
    )
    field_real, field_imag = inverse_cols(lifted, first_len, second_len)
    magnitude = jnp.sqrt(field_real**2 + field_imag**2)
    return (magnitude / jnp.sqrt(own_norm)[:, None, None]).astype(jnp.bfloat16)


def local(strain, analysis, bank, cutoff, order):
    dev_count, segs, cols = lax.axis_size("tmpl"), strain.shape[0], strain.shape[2]
    rows = strain.shape[1] // dev_count // 2
    fits = rows == STEP and cols == 64 and segs % 2 == 0 and dev_count == 2 * len(NEAR)
    if fits and order.shape[0] == dev_count and lax.axis_size("grp") == 2:
        return tiled_local(strain, analysis, bank, cutoff, order)
    return plain_local(strain, analysis, bank, cutoff, order)


def solution(mesh):
    return jax.shard_map(
        local,
        mesh=mesh,
        in_specs=(P("grp", None, "tmpl"), P("grp", "tmpl"), P(None, None, "tmpl", None), P(), P()),
        out_specs=P(("grp", "tmpl"), None, None),
        check_vma=False,
    )
```

profile of v0, /device:TPU:0, one launch (start us, length us, event | category | flops | bytes accessed | tf_op | source)
XLA Modules:
  0.0 92.1 jit_solution(9782602680214691360)
XLA Ops:
  0.0 0.0 copy-start.5
  0.0 0.7 copy-done.5
  0.7 4.5 %stage_one.1 = bf16[256,2176]{1,0:T(8,128)(2,1)} custom-call(s32[16]{0:T(128)S(1)} %copy-done.5, f32[8,64,512]{2,1,0:T(8,128)} %bitcast.15, f32[64,512]{1,0:T(8,128)} %bitcast.18, f32[16,2,512]{2,1,0:T(2,128)} %constant.56.clone.spin_hbm, f32[64,512]{1,0:T(8,128)} %constant.57.clone.win_c_hbm, f32[64,512]{1,0:T(8,128)} %constant.58.clone.win_s_hbm, ...), custom_call_target="tpu_custom_call" | custom-call | tf_op jit(solution)/shard_map/stage_one/pallas_call | solution.py:432
  5.1 7.4 %all-to-all-start = ((bf16[16,16,2176]{2,1,0:T(8,128)(2,1)}), bf16[16,16,2176]{2,1,0:T(8,128)(2,1)S(1)}, u32[]{:S(2)}, u32[]{:S(2)}) async-start(bf16[16,16,2176]{2,1,0:T(8,128)(2,1)} %bitcast.2), calls=%async_computation | async-start | bytes 2228224 | tf_op jit(solution)/shard_map/all_to_all | solution.py:462
  12.6 5.6 %tables.1 = (bf16[1024,1024]{1,0:T(8,128)(2,1)}, bf16[512,1024]{1,0:T(8,128)(2,1)}, bf16[512,1024]{1,0:T(8,128)(2,1)}, bf16[512,1024]{1,0:T(8,128)(2,1)}, bf16[512,1024]{1,0:T(8,128)(2,1)}) custom-call(f32[16,512]{1,0:T(8,128)} %constant.61.clone.fore_c, f32[16,512]{1,0:T(8,128)} %constant.62.clone.fore_s, f32[1,512]{1,0:T(1,128)} %constant.63.clone.fore_rc, ...), custom_call_target="tpu_custom_call" | custom-call | flops 10000000 | bytes 20000000 | tf_op jit(solution)/shard_map/tables/pallas_call | solution.py:487
  18.1 18.4 %all-to-all-done.moved = bf16[16,16,2176]{2,1,0:T(8,128)(2,1)S(1)} async-done(((bf16[16,16,2176]{2,1,0:T(8,128)(2,1)}), bf16[16,16,2176]{2,1,0:T(8,128)(2,1)S(1)}, u32[]{:S(2)}, u32[]{:S(2)}) %all-to-all-start) | async-done | bytes 1114144 | tf_op jit(solution)/shard_map/all_to_all | solution.py:462
  36.5 7.5 %stage_two.1 = bf16[32,1536]{1,0:T(8,128)(2,1)S(1)} custom-call(bf16[16,16,2176]{2,1,0:T(8,128)(2,1)S(1)} %all-to-all-done.moved, f32[16,1024]{1,0:T(8,128)} %constant.77.clone.near_c_hbm, f32[16,1024]{1,0:T(8,128)} %constant.78.clone.near_s_hbm, f32[16,1,1024]{2,1,0:T(1,128)} %constant.79.clone.base_c_hbm, f32[16,1,1024]{2,1,0:T(1,128)} %constant.80.clone.base_s_hbm, ...), custom_call_target="tpu_custom_call" | custom-call | flops 1000000000 | bytes 4000000 | tf_op jit(solution)/shard_map/stage_two/pallas_call | solution.py:520
  44.0 3.4 %collective-permute-start.1 = (bf16[32,1536]{1,0:T(8,128)(2,1)S(1)}, bf16[32,1536]{1,0:T(8,128)(2,1)S(1)}, u32[]{:S(2)}, u32[]{:S(2)}) collective-permute-start(bf16[32,1536]{1,0:T(8,128)(2,1)S(1)} %stage_two.1), channel_id=1, source_target_pairs={{0,4},{1,5},{2,6},{3,7},{4,0},{5,1},{6,2},{7,3},{8,12},{9,13},{10,... | collective-permute-start | bytes 294920 | tf_op jit(solution)/shard_map/ppermute | solution.py:410
  47.4 3.5 %collective-permute-start.2 = (bf16[32,1536]{1,0:T(8,128)(2,1)S(1)}, bf16[32,1536]{1,0:T(8,128)(2,1)S(1)}, u32[]{:S(2)}, u32[]{:S(2)}) collective-permute-start(bf16[32,1536]{1,0:T(8,128)(2,1)S(1)} %stage_two.1), channel_id=1, source_target_pairs={{0,12},{1,13},{2,14},{3,15},{4,8},{5,9},{6,10},{7,11},{8,4},{9,5},... | collective-permute-start | bytes 294920 | tf_op jit(solution)/shard_map/ppermute | solution.py:410
  50.9 0.1 collective-permute-start
  51.0 0.0 collective-permute-done.1
  51.0 4.6 %collective-permute-done.2 = bf16[32,1536]{1,0:T(8,128)(2,1)S(1)} collective-permute-done((bf16[32,1536]{1,0:T(8,128)(2,1)S(1)}, bf16[32,1536]{1,0:T(8,128)(2,1)S(1)}, u32[]{:S(2)}, u32[]{:S(2)}) %collective-permute-start.2) | collective-permute-done | bytes 98336 | tf_op jit(solution)/shard_map/ppermute | solution.py:410
  55.6 0.6 collective-permute-start.3
  56.3 0.0 collective-permute-start.4
  56.3 0.0 collective-permute-done
  56.3 0.0 copy-start.6
  56.3 0.0 copy-start.7
  56.4 4.5 %collective-permute-done.4 = bf16[32,1536]{1,0:T(8,128)(2,1)S(1)} collective-permute-done((bf16[32,1536]{1,0:T(8,128)(2,1)S(1)}, bf16[32,1536]{1,0:T(8,128)(2,1)S(1)}, u32[]{:S(2)}, u32[]{:S(2)}) %collective-permute-start.4) | collective-permute-done | bytes 98336 | tf_op jit(solution)/shard_map/ppermute | solution.py:410
  60.9 1.5 %collective-permute-start.5 = (bf16[32,1536]{1,0:T(8,128)(2,1)S(1)}, bf16[32,1536]{1,0:T(8,128)(2,1)S(1)}, u32[]{:S(2)}, u32[]{:S(2)}) collective-permute-start(bf16[32,1536]{1,0:T(8,128)(2,1)S(1)} %collective-permute-done.4), channel_id=1, source_target_pairs={{0,2},{1,3},{2,0},{3,1},{4,6},{5,7},{6,4},{7,5},{8,10},{9,11},{10,... | collective-permute-start | bytes 294920 | tf_op jit(solution)/shard_map/ppermute | solution.py:410
  62.4 0.0 collective-permute-done.3
  62.4 0.0 copy-start.4
  62.4 3.1 %collective-permute-done.5 = bf16[32,1536]{1,0:T(8,128)(2,1)S(1)} collective-permute-done((bf16[32,1536]{1,0:T(8,128)(2,1)S(1)}, bf16[32,1536]{1,0:T(8,128)(2,1)S(1)}, u32[]{:S(2)}, u32[]{:S(2)}) %collective-permute-start.5) | collective-permute-done | bytes 98336 | tf_op jit(solution)/shard_map/ppermute | solution.py:410
  65.5 0.1 collective-permute-start.6
  65.6 0.0 copy-start.3
  65.6 0.1 slice.7.own
  65.7 0.0 copy-start
  65.7 0.0 copy-start.1
  65.7 0.0 copy-start.2
  65.7 1.6 %collective-permute-start.7 = (bf16[16,16,1024]{2,1,0:T(8,128)(2,1)S(1)}, bf16[16,16,1024]{2,1,0:T(8,128)(2,1)S(1)}, u32[]{:S(2)}, u32[]{:S(2)}) collective-permute-start(bf16[16,16,1024]{2,1,0:T(8,128)(2,1)S(1)} %slice.7.own), channel_id=1, source_target_pairs={{0,16},{16,0},{1,17},{17,1},{2,18},{18,2},{3,19},{19,3},{4,20},{20... | collective-permute-start | bytes 1572872 | tf_op jit(solution)/shard_map/ppermute | solution.py:466
  67.3 12.8 %collective-permute-done.7.other = bf16[16,16,1024]{2,1,0:T(8,128)(2,1)S(1)} collective-permute-done((bf16[16,16,1024]{2,1,0:T(8,128)(2,1)S(1)}, bf16[16,16,1024]{2,1,0:T(8,128)(2,1)S(1)}, u32[]{:S(2)}, u32[]{:S(2)}) %collective-permute-start.7) | collective-permute-done | bytes 524320 | tf_op jit(solution)/shard_map/ppermute | solution.py:466
  80.1 0.0 copy-done.6
  80.1 0.0 copy-done.7
  80.1 3.4 %choose.1.chosen = bf16[512,1024]{1,0:T(8,128)(2,1)S(1)} custom-call(s32[16]{0:T(128)S(1)} %copy-done.6, s32[16]{0:T(128)S(1)} %copy-done.7, bf16[16,16,1024]{2,1,0:T(8,128)(2,1)S(1)} %slice.7.own, bf16[16,16,1024]{2,1,0:T(8,128)(2,1)S(1)} %collective-permute-done.7.other), custom_call_target="tpu_custom_call" | custom-call | flops 1000000000 | bytes 4000000 | tf_op jit(solution)/shard_map/choose/pallas_call | solution.py:543
  83.5 0.0 collective-permute-done.6.far
  83.5 0.0 copy-done.4
  83.5 0.0 copy-done.3
  83.6 0.0 copy-done
  83.6 0.0 copy-done.1
  83.6 0.0 copy-done.2
  83.6 8.5 %inverse.1 = bf16[1,512,1024]{2,1,0:T(8,128)(2,1)} custom-call(bf16[8,32,1536]{2,1,0:T(8,128)(2,1)S(1)} %bitcast_dynamic-update-slice_fusion.near, bf16[8,32,1536]{2,1,0:T(8,128)(2,1)S(1)} %collective-permute-done.6.far, bf16[512,1024]{1,0:T(8,128)(2,1)S(1)} %choose.1.chosen, bf16[512,1024]{1,0:T(8,128)(2,1)S(1)} %copy-done.1, ...), custom_call_target="tpu_custom_call" | custom-call | tf_op jit(solution)/shard_map/inverse/pallas_call | solution.py:555
  (8 shorter events, 0.1 us)
Async XLA Ops:
  0.0 0.7 copy-start.5
  5.1 31.4 %all-to-all-start = ((bf16[16,16,2176]{2,1,0:T(8,128)(2,1)}), bf16[16,16,2176]{2,1,0:T(8,128)(2,1)S(1)}, u32[]{:S(2)}, u32[]{:S(2)}) async-start(bf16[16,16,2176]{2,1,0:T(8,128)(2,1)} %bitcast.2), calls=%async_computation | async-start | bytes 2228224 | tf_op jit(solution)/shard_map/all_to_all | solution.py:462
  44.0 7.0 %collective-permute-start.1 = (bf16[32,1536]{1,0:T(8,128)(2,1)S(1)}, bf16[32,1536]{1,0:T(8,128)(2,1)S(1)}, u32[]{:S(2)}, u32[]{:S(2)}) collective-permute-start(bf16[32,1536]{1,0:T(8,128)(2,1)S(1)} %stage_two.1), channel_id=1, source_target_pairs={{0,4},{1,5},{2,6},{3,7},{4,0},{5,1},{6,2},{7,3},{8,12},{9,13},{10,... | collective-permute-start | bytes 294920 | tf_op jit(solution)/shard_map/ppermute | solution.py:410
  47.4 8.2 %collective-permute-start.2 = (bf16[32,1536]{1,0:T(8,128)(2,1)S(1)}, bf16[32,1536]{1,0:T(8,128)(2,1)S(1)}, u32[]{:S(2)}, u32[]{:S(2)}) collective-permute-start(bf16[32,1536]{1,0:T(8,128)(2,1)S(1)} %stage_two.1), channel_id=1, source_target_pairs={{0,12},{1,13},{2,14},{3,15},{4,8},{5,9},{6,10},{7,11},{8,4},{9,5},... | collective-permute-start | bytes 294920 | tf_op jit(solution)/shard_map/ppermute | solution.py:410
  50.9 5.3 %collective-permute-start = (bf16[32,1536]{1,0:T(8,128)(2,1)S(1)}, bf16[32,1536]{1,0:T(8,128)(2,1)S(1)}, u32[]{:S(2)}, u32[]{:S(2)}) collective-permute-start(bf16[32,1536]{1,0:T(8,128)(2,1)S(1)} %stage_two.1), channel_id=1, source_target_pairs={{0,2},{1,3},{2,0},{3,1},{4,6},{5,7},{6,4},{7,5},{8,10},{9,11},{10,... | collective-permute-start | bytes 294920 | tf_op jit(solution)/shard_map/ppermute | solution.py:410
  55.6 6.7 %collective-permute-start.3 = (bf16[2,32,1536]{2,1,0:T(8,128)(2,1)S(1)}, bf16[2,32,1536]{2,1,0:T(8,128)(2,1)S(1)}, u32[]{:S(2)}, u32[]{:S(2)}) collective-permute-start(bf16[2,32,1536]{2,1,0:T(8,128)(2,1)S(1)} %pad_maximum_fusion), channel_id=1, source_target_pairs={{0,2},{1,3},{2,0},{3,1},{4,6},{5,7},{6,4},{7,5},{8,10},{9,11},{10,... | collective-permute-start | bytes 589832 | tf_op jit(solution)/shard_map/ppermute | solution.py:410
  56.3 4.6 %collective-permute-start.4 = (bf16[32,1536]{1,0:T(8,128)(2,1)S(1)}, bf16[32,1536]{1,0:T(8,128)(2,1)S(1)}, u32[]{:S(2)}, u32[]{:S(2)}) collective-permute-start(bf16[32,1536]{1,0:T(8,128)(2,1)S(1)} %collective-permute-done.2), channel_id=1, source_target_pairs={{0,4},{1,5},{2,6},{3,7},{4,0},{5,1},{6,2},{7,3},{8,12},{9,13},{10,... | collective-permute-start | bytes 294920 | tf_op jit(solution)/shard_map/ppermute | solution.py:410
  56.3 23.8 %copy-start.6 = (s32[16]{0:T(128)S(1)}, s32[16]{0:T(128)}, u32[]{:S(2)}) copy-start(s32[16]{0:T(128)} %order.3) | copy-start | bytes 196
  56.3 23.8 %copy-start.7 = (s32[16]{0:T(128)S(1)}, s32[16]{0:T(128)}, u32[]{:S(2)}) copy-start(s32[16]{0:T(128)} %cuts.1) | copy-start | bytes 196
  60.9 4.6 %collective-permute-start.5 = (bf16[32,1536]{1,0:T(8,128)(2,1)S(1)}, bf16[32,1536]{1,0:T(8,128)(2,1)S(1)}, u32[]{:S(2)}, u32[]{:S(2)}) collective-permute-start(bf16[32,1536]{1,0:T(8,128)(2,1)S(1)} %collective-permute-done.4), channel_id=1, source_target_pairs={{0,2},{1,3},{2,0},{3,1},{4,6},{5,7},{6,4},{7,5},{8,10},{9,11},{10,... | collective-permute-start | bytes 294920 | tf_op jit(solution)/shard_map/ppermute | solution.py:410
  62.4 21.2 %copy-start.4 = (bf16[512,1024]{1,0:T(8,128)(2,1)S(1)}, bf16[512,1024]{1,0:T(8,128)(2,1)}, u32[]{:S(2)}) copy-start(bf16[512,1024]{1,0:T(8,128)(2,1)} %get-tuple-element.14.lift_s) | copy-start | bytes 3145732
  65.5 18.0 %collective-permute-start.6 = (bf16[8,32,1536]{2,1,0:T(8,128)(2,1)S(1)}, bf16[8,32,1536]{2,1,0:T(8,128)(2,1)S(1)}, u32[]{:S(2)}, u32[]{:S(2)}) collective-permute-start(bf16[8,32,1536]{2,1,0:T(8,128)(2,1)S(1)} %bitcast_dynamic-update-slice_fusion.near), channel_id=1, source_target_pairs={{0,1},{1,0},{2,3},{3,2},{4,5},{5,4},{6,7},{7,6},{8,9},{9,8},{10,11... | collective-permute-start | bytes 2359304 | tf_op jit(solution)/shard_map/ppermute | solution.py:410
  65.6 17.9 %copy-start.3 = (bf16[512,1024]{1,0:T(8,128)(2,1)S(1)}, bf16[512,1024]{1,0:T(8,128)(2,1)}, u32[]{:S(2)}) copy-start(bf16[512,1024]{1,0:T(8,128)(2,1)} %get-tuple-element.13.lift_c) | copy-start | bytes 3145732
  65.7 17.9 %copy-start = (bf16[512,1024]{1,0:T(8,128)(2,1)S(1)}, bf16[512,1024]{1,0:T(8,128)(2,1)}, u32[]{:S(2)}) copy-start(bf16[512,1024]{1,0:T(8,128)(2,1)} %constant.83.clone.cols_table) | copy-start | bytes 3145732
  65.7 17.9 %copy-start.1 = (bf16[512,1024]{1,0:T(8,128)(2,1)S(1)}, bf16[512,1024]{1,0:T(8,128)(2,1)}, u32[]{:S(2)}) copy-start(bf16[512,1024]{1,0:T(8,128)(2,1)} %get-tuple-element.11.even_table) | copy-start | bytes 3145732
  65.7 17.9 %copy-start.2 = (bf16[512,1024]{1,0:T(8,128)(2,1)S(1)}, bf16[512,1024]{1,0:T(8,128)(2,1)}, u32[]{:S(2)}) copy-start(bf16[512,1024]{1,0:T(8,128)(2,1)} %get-tuple-element.12.odd_table) | copy-start | bytes 3145732
  65.7 14.4 %collective-permute-start.7 = (bf16[16,16,1024]{2,1,0:T(8,128)(2,1)S(1)}, bf16[16,16,1024]{2,1,0:T(8,128)(2,1)S(1)}, u32[]{:S(2)}, u32[]{:S(2)}) collective-permute-start(bf16[16,16,1024]{2,1,0:T(8,128)(2,1)S(1)} %slice.7.own), channel_id=1, source_target_pairs={{0,16},{16,0},{1,17},{17,1},{2,18},{18,2},{3,19},{19,3},{4,20},{20... | collective-permute-start | bytes 1572872 | tf_op jit(solution)/shard_map/ppermute | solution.py:466
where the time goes:
time: 92.4 us; the launch traced here: 92.1 us
  waiting for transfers between devices  43.4 us (47%)
  Pallas kernels  29.4 us (32%)
  starting transfers between devices  18.2 us (20%)
    all_to_all x1, waiting for transfers between devices, tiled_local(): lax.all_to_all(sent.reshape(dev_count, rows, lanes + 2 * half_len), 'tmpl...  18.4 us
    ppermute x1, waiting for transfers between devices, tiled_local(): other = lax.ppermute(own, 'grp', [(0, 1), (1, 0)])  12.8 us
    ppermute x7, waiting for transfers between devices, swap_with(): return lax.ppermute(array, 'tmpl', pairs)  12.3 us
    ppermute x7, starting transfers between devices, swap_with(): return lax.ppermute(array, 'tmpl', pairs)  9.18 us
    pallas_call x1, Pallas kernels, tiled_local(): pl.pallas_call(inverse_kernel, out_shape=jax.ShapeDtypeStruct((1, first_l...  8.52 us
    pallas_call x1, Pallas kernels, tiled_local(): stage_two(moved, *in_hbm(near_c, near_s, base_c, base_s, mid_c, mid_s, fo...  7.46 us
    all_to_all x1, starting transfers between devices, tiled_local(): lax.all_to_all(sent.reshape(dev_count, rows, lanes + 2 * half_len), 'tmpl...  7.43 us
    pallas_call x1, Pallas kernels, tiled_local(): pl.pallas_call(tables_kernel, out_shape=[pltpu.HBM(shape, BF16) for shape...  5.59 us
  transfers between devices with their start and end apart: 9, of which 5 were waited for; matrix products, arithmetic and copies ran while one was open for 0% of the time, Pallas kernels for 10%

commit v1 on v0

v1 whole, which is shorter than its diff:
```python
import functools
import math

import jax
import jax.numpy as jnp
import numpy as np
from jax import lax
from jax.experimental import pallas as pl
from jax.experimental.pallas import tpu as pltpu
from jax.sharding import PartitionSpec as P

BF16 = jnp.bfloat16
F32 = jnp.float32
STEP = 16
PIECE = 128
EARLY = (0, 2, 4, 8, 1, 3, 5, 9, 6, 10, 12)
LATE = (14, 7, 11, 13, 15)


def turns(product, period):
    angle = (product % period) * (2.0 * math.pi / period)
    return np.cos(angle).astype(np.float32), np.sin(angle).astype(np.float32)


def matmul(left, right):
    return jnp.dot(left, right, preferred_element_type=F32)


def matmul_nt(left, right):
    return lax.dot_general(left, right, (((1,), (1,)), ((), ())), preferred_element_type=F32)


def vmem(shape, dtype=BF16):
    return pltpu.VMEM(shape, dtype)


def whole():
    return pl.BlockSpec(memory_space=pltpu.VMEM)


def outside():
    return pl.BlockSpec(memory_space=pltpu.HBM)


def in_hbm(*arrays):
    return [pltpu.with_memory_space_constraint(jnp.asarray(array), pltpu.HBM) for array in arrays]


def in_vmem(*arrays):
    return [pltpu.with_memory_space_constraint(array, pltpu.VMEM) for array in arrays]


def position():
    return lax.axis_index("tmpl"), lax.axis_index("grp")


def start_copies(pairs, sems):
    copies = [
        pltpu.make_async_copy(source, target, sems.at[at]) for at, (source, target) in enumerate(pairs)
    ]
    for copy in copies:
        copy.start()
    return copies


def params(mib):
    return pltpu.CompilerParams(vmem_limit_bytes=mib << 20)


def halves(count):
    return np.concatenate([np.arange(0, count, 2), np.arange(1, count, 2)])


def aligned(start, size):
    return pl.ds(pl.multiple_of(start, size), size)


def stage_one_kernel(
    order_hbm, strain_hbm, analysis_hbm, spin_hbm, win_c_hbm, win_s_hbm, cos_hbm, sin_hbm, bank, out,
    order, strain, analysis, spin, win_c, win_s, cos, sin, packed, sems, bank_sems,
):
    segs, cols, _ = strain.shape
    tail = segs * cols
    templates, half_len = bank.shape[1], bank.shape[3]
    rows = out.shape[0] // templates
    place, group = position()
    sources = [
        (spin_hbm.at[place], spin),
        (win_c_hbm, win_c),
        (win_s_hbm, win_s),
        *[(strain_hbm.at[seg], strain.at[seg]) for seg in range(segs)],
        (analysis_hbm, analysis),
        (cos_hbm, cos),
        (sin_hbm, sin),
        (order_hbm, order),
    ]
    copies = start_copies(sources, sems)
    copies.pop().wait()
    lane = 2 * (tail + cols)
    bank_pairs = []
    for row in range(templates):
        for part in range(2):
            bank_pairs.append(
                (
                    bank.at[part, order[row], aligned(group * rows, rows), :],
                    out.at[
                        row * rows : (row + 1) * rows,
                        lane + part * half_len : lane + (part + 1) * half_len,
                    ],
                )
            )
    bank_copies = start_copies(bank_pairs, bank_sems)
    for copy in copies[:3]:
        copy.wait()
    scale = 0.5 * math.sqrt(8.0 / 3.0)
    window = scale - scale * (win_c[...] * spin[0:1, :] - win_s[...] * spin[1:2, :])
    for seg in range(segs):
        copies[3 + seg].wait()
        packed[seg * cols : (seg + 1) * cols, :] = (strain[seg] * window).astype(BF16)
    for copy in copies[3 + segs :]:
        copy.wait()
    packed[tail:, :] = analysis[...].astype(BF16)
    real = matmul_nt(cos[...], packed[...])
    imag = -matmul_nt(sin[...], packed[...])
    out[:, 0:tail] = real[:, :tail].astype(BF16)
    out[:, tail : 2 * tail] = imag[:, :tail].astype(BF16)
    joined = jnp.concatenate([real[:, tail:], imag[:, tail:]], 1)
    out[:, 2 * tail : lane] = joined.astype(BF16)
    for copy in bank_copies:
        copy.wait()


def turn(cos, sin, by_cos, by_sin):
    return cos * by_cos - sin * by_sin, sin * by_cos + cos * by_sin


def forward_kernel(
    fore_c, fore_s, fore_rc, fore_rs, near_c, near_s, base_c, base_s,
    forward_hbm, near_out_c, near_out_s, forward, sem,
):
    half_len = fore_c.shape[1]
    quarter = half_len // 2
    place, _ = position()
    first_lane = lax.broadcasted_iota(jnp.int32, fore_c.shape, 1) == 0
    sign = 1.0 - 2.0 * (lax.broadcasted_iota(jnp.int32, fore_c.shape, 0) % 2).astype(F32)

    def fore(step, carry):
        cos, sin = carry
        for part, table in enumerate((cos, jnp.where(first_lane, sign, sin))):
            for odd in range(2):
                lane = slice(odd * quarter, (odd + 1) * quarter)
                to = slice(part * quarter, (part + 1) * quarter)
                forward[odd, aligned(step * STEP, STEP), to] = table[:, lane].astype(BF16)
        return turn(cos, sin, fore_rc[...], fore_rs[...])

    lax.fori_loop(0, forward.shape[1] // STEP, fore, (fore_c[...], fore_s[...]))
    copy = pltpu.make_async_copy(forward, forward_hbm, sem)
    copy.start()
    near_out_c[...], near_out_s[...] = turn(near_c[...], near_s[...], base_c[place], base_s[place])
    copy.wait()


def inverse_tables_kernel(
    even_c, even_s, odd_c, odd_s, rows_rc, rows_rs, lift_c, lift_s, lift_rc, lift_rs, mid_c, mid_s,
    cols_c, cols_s, cols_rc, cols_rs,
    even_out, odd_out, lift_out_c, lift_out_s, cols_out, rows_out, bins_out,
):
    half_len = even_c.shape[1]
    quarter = half_len // 2
    first_len = cols_c.shape[1]
    per = first_len // 2

    def spread(out, cos, sin):
        def body(step, carry):
            cos, sin = carry
            upper = aligned(step * STEP, STEP)
            lower = aligned(quarter + step * STEP, STEP)
            for lane in range(0, half_len, PIECE):
                real, imag = slice(2 * lane, 2 * lane + PIECE), slice(2 * lane + PIECE, 2 * (lane + PIECE))
                cos_at, sin_at = cos[:, lane : lane + PIECE], sin[:, lane : lane + PIECE]
                out[upper, real] = cos_at.astype(BF16)
                out[upper, imag] = sin_at.astype(BF16)
                out[lower, real] = (-sin_at).astype(BF16)
                out[lower, imag] = cos_at.astype(BF16)
            return turn(cos, sin, rows_rc[...], rows_rs[...])

        lax.fori_loop(0, quarter // STEP, body, (cos, sin))

    spread(even_out, even_c[...], even_s[...])
    spread(odd_out, odd_c[...], odd_s[...])

    for parity in range(2):

        def lifts(step, carry, parity=parity):
            cos, sin = carry
            at = aligned(parity * per + step * STEP, STEP)
            lift_out_c[at, :] = cos
            lift_out_s[at, :] = sin
            return turn(cos, sin, lift_rc[...], lift_rs[...])

        lax.fori_loop(0, per // STEP, lifts, (lift_c[parity], lift_s[parity]))
    lift_out_c[0:STEP, :] = mid_c[...]
    lift_out_s[0:STEP, :] = mid_s[...]

    def columns(step, carry):
        cos, sin = carry
        upper = aligned(step * STEP, STEP)
        lower = aligned(per + step * STEP, STEP)
        for parity in range(2):
            at = slice(parity * per, (parity + 1) * per)
            left = slice(parity * first_len, parity * first_len + per)
            right = slice(parity * first_len + per, (parity + 1) * first_len)
            cols_out[upper, left] = cos[:, at].astype(BF16)
            cols_out[upper, right] = (-sin[:, at]).astype(BF16)
            cols_out[lower, left] = sin[:, at].astype(BF16)
            cols_out[lower, right] = cos[:, at].astype(BF16)
        return turn(cos, sin, cols_rc[...], cols_rs[...])

    lax.fori_loop(0, per // STEP, columns, (cols_c[...], cols_s[...]))
    sort_tables(lift_c.shape[1], rows_out, bins_out)


def stage_two_kernel(
    segs, cols, moved, near_c, near_s, mid_c_hbm, mid_s_hbm, forward_hbm, out,
    mid_c, mid_s, forward, stacked, middle, product, sems,
):
    place, _ = position()
    _, second_len, half_len = forward.shape
    quarter = half_len // 2
    pieces = [(forward_hbm.at[odd], forward.at[odd]) for odd in range(2)]
    pieces += [(mid_c_hbm, mid_c), (mid_s_hbm, mid_s)]
    copies = start_copies(pieces, sems)
    sources, rows, _ = moved.shape
    tail = segs * cols
    all_rows = (segs + 1) * rows
    width = 2 * cols
    low = lax.broadcasted_iota(jnp.int32, (rows, width), 1) < cols
    own_first = place == 0
    packed_row = lax.broadcasted_iota(jnp.int32, (rows, width), 0) == 0
    drop = jnp.logical_and(packed_row, own_first)

    def pair(left, right):
        return (
            jnp.where(low, left, pltpu.roll(right, cols, 1)),
            jnp.where(low, pltpu.roll(left, cols, 1), right),
        )

    middle[...] = jnp.zeros_like(middle)
    for tile in range(sources // 2):
        lane = slice(tile * width, (tile + 1) * width)
        cos, sin = near_c[:, lane], near_s[:, lane]

        def piece(lo, tile=tile):
            hi = lo + width
            return pair(
                moved[2 * tile, :, lo:hi].astype(F32), moved[2 * tile + 1, :, lo:hi].astype(F32)
            )

        def put(seg, real, imag, lane=lane, cos=cos, sin=sin):
            middle[seg : seg + 1, lane] = imag[0:1, :]
            imag = jnp.where(drop, 0.0, imag)
            at = seg * rows
            stacked[at : at + rows, lane] = (real * cos + imag * sin).astype(BF16)
            at += all_rows
            stacked[at : at + rows, lane] = (imag * cos - real * sin).astype(BF16)

        for twin in range(segs // 2):
            real_one, real_two = piece(twin * width)
            imag_one, imag_two = piece(tail + twin * width)
            put(2 * twin, real_one, imag_one)
            put(2 * twin + 1, real_two, imag_two)
        real, imag = piece(2 * tail)
        put(segs, real, imag)
    for copy in copies[2:]:
        copy.wait()
    stacked[2 * all_rows : 2 * all_rows + rows, :] = (middle[...] * mid_c[...]).astype(BF16)
    stacked[2 * all_rows + rows :, :] = (middle[...] * -mid_s[...]).astype(BF16)

    first_lane = lax.broadcasted_iota(jnp.int32, (rows, quarter), 1) == 0
    swap = jnp.logical_and(lax.broadcasted_iota(jnp.int32, (rows, quarter), 0) == 0, own_first)
    floor = 0.2 * (second_len * 2 * sources * rows)
    upper, lower = [], []
    for odd in range(2):
        cos_at = slice(odd * half_len, odd * half_len + quarter)
        sin_at = slice(odd * half_len + quarter, (odd + 1) * half_len)
        copies[odd].wait()
        product[:, odd * half_len : (odd + 1) * half_len] = matmul(stacked[...], forward[odd])

        def parts(at, lower_at, cos_at=cos_at, sin_at=sin_at):
            return (
                product[at : at + rows, cos_at],
                product[at : at + rows, sin_at],
                product[lower_at : lower_at + rows, cos_at],
                product[lower_at : lower_at + rows, sin_at],
            )

        def direct_of(rc, rs, ic, imag_s, odd=odd):
            if not odd:
                rs, imag_s = jnp.where(first_lane, 0.0, rs), jnp.where(first_lane, 0.0, imag_s)
            return rc + imag_s, ic - rs

        def mirror_of(rc, rs, ic, imag_s, odd=odd):
            real, imag = rc - imag_s, ic + rs
            if not odd:
                real, imag = jnp.where(first_lane, rs, real), jnp.where(first_lane, imag_s, imag)
            return real, imag

        level = jnp.zeros((rows, quarter), F32)
        mirror_level = level
        for seg in range(segs):
            four = parts(seg * rows, all_rows + seg * rows)
            real, imag = direct_of(*four)
            level = level + (real * real + imag * imag)
            real, imag = mirror_of(*four)
            mirror_level = mirror_level + (real * real + imag * imag)
        four = parts(segs * rows, all_rows + segs * rows)
        real, imag = direct_of(*four)
        mirror_real, mirror_imag = mirror_of(*four)
        mid_real, mid_imag = mirror_of(*parts(2 * all_rows, 2 * all_rows + rows))
        mid_level = jnp.sum((mid_real * mid_real + mid_imag * mid_imag)[:segs], 0, keepdims=True)
        mirror_level = jnp.where(swap, mid_level, mirror_level)
        mirror_real = jnp.where(swap, mid_real[segs : segs + 1], mirror_real)
        mirror_imag = jnp.where(swap, mid_imag[segs : segs + 1], mirror_imag)
        level = jnp.maximum(level * (1.0 / segs), floor)
        mirror_level = jnp.maximum(mirror_level * (1.0 / segs), floor)
        upper.append((real / level, imag / level, 1.0 / level))
        lower.append((mirror_real / mirror_level, -mirror_imag / mirror_level, 1.0 / mirror_level))
    eighth = rows // 2
    for part in range(3):
        mirrored = (lower[1][part], pltpu.roll(lower[0][part], quarter - 1, 1))
        for odd in range(2):
            lane = slice(part * half_len + odd * quarter, part * half_len + (odd + 1) * quarter)
            for parity in range(2):
                at = slice(parity * eighth, (parity + 1) * eighth)
                block = jnp.concatenate([upper[odd][part][at], mirrored[odd][at]], 0)
                out[parity * rows : (parity + 1) * rows, lane] = block.astype(BF16)


def sort_tables(rows, rows_out, bins_out):
    first_len, half_len = rows_out.shape[0], bins_out.shape[0]
    per = first_len // 2
    _, group = position()
    deep = 128

    def one_hot(mask):
        return jnp.where(mask, 1.0, 0.0).astype(BF16)

    def body(step, carry):
        at = aligned(step * deep, deep)
        row = packed_row_of(step * deep + lax.broadcasted_iota(jnp.int32, (deep, first_len), 0), first_len, rows)
        share = (row // rows) % 2
        column = (row // (2 * rows)) * rows + row % rows + jnp.where(share == group, 0, per)
        rows_out[at, :] = one_hot(column == lax.broadcasted_iota(jnp.int32, (deep, first_len), 1))
        return carry

    lax.fori_loop(0, first_len // deep, body, 0)

    def bins(step, carry):
        row = step * deep + lax.broadcasted_iota(jnp.int32, (deep, half_len), 0)
        lane = lax.broadcasted_iota(jnp.int32, (deep, half_len), 1)
        bins_out[aligned(step * deep, deep), :] = one_hot(row == bin_of(lane, half_len))
        return carry

    lax.fori_loop(0, half_len // deep, bins, 0)


def bin_of(lane, half_len):
    return jnp.where(lane < half_len // 2, 2 * lane, 2 * lane - half_len + 1)


def packed_row_of(at, first_len, rows):
    per = first_len // 2
    packed = (at % per) // rows * rows + 2 * (at % (rows // 2)) + at // per
    turned = jnp.where(packed == 0, first_len // 2, first_len - packed)
    return jnp.where(at % rows >= rows // 2, turned, packed)


def choose_kernel(order, cuts, own, other, by_rows, by_bins, out, held):
    place, _ = position()
    rows, sources = own.shape[1], own.shape[0]
    per = sources * rows
    first_len, half_len = 2 * per, own.shape[2] // 2
    for source in range(sources):
        held[source * rows : (source + 1) * rows, :] = own[source]
        held[per + source * rows : per + (source + 1) * rows, :] = other[source]
    picked = matmul(by_rows[...], held[...]).astype(BF16)
    at = lax.broadcasted_iota(jnp.int32, (first_len, 128), 0)
    room = cuts[order[place]] - packed_row_of(at, first_len, rows)
    for part in range(2):
        moved = matmul(picked[:, part * half_len : (part + 1) * half_len], by_bins[...])
        for lane in range(0, half_len, 128):
            bins = bin_of(lane + lax.broadcasted_iota(jnp.int32, (1, 128), 1), half_len)
            kept = jnp.where(first_len * bins < room, moved[:, lane : lane + 128], 0.0)
            out[:, part * half_len + lane : part * half_len + lane + 128] = kept.astype(BF16)


def filter_blocks(offsets, blocks, chosen, tables, norm, filtered, lifted):
    place, _ = position()
    even_table, odd_table, lift_c, lift_s = tables
    half_len = even_table.shape[0]
    quarter = half_len // 2
    first_len = chosen.shape[0]
    per = first_len // 2
    rows = blocks[0].shape[0] // 2
    groups = []
    for block, offset in zip(blocks, offsets):
        device = jnp.bitwise_xor(place, offset)
        for parity in range(2):
            row = slice(parity * rows, (parity + 1) * rows)
            at = aligned(parity * per + device * rows, rows)
            white_real = block[row, :half_len].astype(F32)
            white_imag = block[row, half_len : 2 * half_len].astype(F32)
            weight = block[row, 2 * half_len :].astype(F32)
            real = chosen[at, :half_len].astype(F32)
            imag = chosen[at, half_len:].astype(F32)
            norm = norm + (real * real + imag * imag) * weight
            filt_real = (white_real * real + white_imag * imag).astype(BF16)
            filt_imag = (white_imag * real - white_real * imag).astype(BF16)
            to = slice(len(groups) * rows, (len(groups) + 1) * rows)
            filtered[to, 0:quarter] = filt_real[:, :quarter]
            filtered[to, quarter:half_len] = filt_imag[:, :quarter]
            filtered[to, half_len : half_len + quarter] = filt_real[:, quarter:]
            filtered[to, half_len + quarter :] = filt_imag[:, quarter:]
            groups.append((to, at, parity * first_len + device * rows))
    for lane in range(0, half_len, PIECE):
        both = slice(2 * lane, 2 * (lane + PIECE))
        even = matmul(filtered[:, :half_len], even_table[:, both])
        odd = matmul(filtered[:, half_len:], odd_table[:, both])
        for upper in range(2):
            lanes = slice(upper * half_len + lane, upper * half_len + lane + PIECE)
            total = even - odd if upper else even + odd
            for row, at, target in groups:
                real, imag = total[row, :PIECE], total[row, PIECE:]
                cos, sin = lift_c[at, lanes], lift_s[at, lanes]
                lifted[aligned(target, rows), lanes] = (real * cos - imag * sin).astype(BF16)
                lifted[aligned(target + per, rows), lanes] = (real * sin + imag * cos).astype(BF16)
    return norm


def early_kernel(near, theirs, both, far, chosen, *refs):
    tables, (lifted, norm, filtered) = refs[:4], refs[4:]
    blocks = [*[near.at[at] for at in range(4)], *[theirs.at[at] for at in range(4)], both.at[0], both.at[1], far]
    zero = jnp.zeros(norm.shape, F32)
    norm[...] = filter_blocks(EARLY, blocks, chosen, tables, zero, filtered, lifted)


def late_kernel(last, theirs, early, early_norm, chosen, *refs):
    tables, (cols_table, out, lifted, filtered) = refs[:4], refs[4:]
    blocks = [last, *[theirs.at[at] for at in range(4)]]
    norm = filter_blocks(LATE, blocks, chosen, tables, early_norm[...], filtered, lifted)
    scale = lax.rsqrt(jnp.sum(norm, keepdims=True))
    first_len = chosen.shape[0]
    per = first_len // 2
    wide = 256
    for lane in range(0, lifted.shape[1], wide):
        at = slice(lane, lane + wide)
        even = matmul(cols_table[:, :first_len], lifted[:first_len, at])
        odd = matmul(cols_table[:, first_len:], lifted[first_len:, at])
        for upper in range(2):
            total = even - odd if upper else even + odd
            power = total[:per] * total[:per] + total[per:] * total[per:]
            size = power * lax.rsqrt(jnp.maximum(power, 1e-37))
            out[0, upper * per : (upper + 1) * per, at] = (size * scale).astype(BF16)


def swap_with(array, flip):
    pairs = [(at, at ^ flip) for at in range(lax.axis_size("tmpl"))]
    return lax.ppermute(array, "tmpl", pairs)


def tiled_local(strain, analysis, bank, cutoff, order):
    dev_count = lax.axis_size("tmpl")
    segs, first_len, cols = strain.shape
    second_len = cols * dev_count
    length = first_len * second_len
    half_len = second_len // 2
    rows = first_len // dev_count // 2
    templates = order.shape[0]
    lanes = 2 * (segs + 1) * cols

    first, second, half = np.arange(first_len), np.arange(second_len), np.arange(half_len)
    devices, step = np.arange(dev_count), np.arange(STEP)
    near = halves(rows)
    packed = (devices[:, None] * rows + near[None, :]).reshape(-1, 1)
    cos_one, sin_one = turns(packed * first[None, :], first_len)
    sin_one[0] = 2 * (first % 2) - 1.0
    win_c, win_s = turns(np.arange(cols)[:, None] + second_len * first[None, :], length)
    spin = np.stack(turns(cols * devices, length), 1)[:, :, None] * np.ones((1, 1, first_len), np.float32)

    sent = pl.pallas_call(
        stage_one_kernel,
        in_specs=[outside()] * 9,
        out_specs=whole(),
        scratch_shapes=[
            pltpu.SMEM((templates,), jnp.int32),
            vmem((segs, cols, first_len), F32),
            vmem((cols, first_len), F32),
            vmem((2, first_len), F32),
            vmem((cols, first_len), F32),
            vmem((cols, first_len), F32),
            vmem((dev_count * rows, first_len)),
            vmem((dev_count * rows, first_len)),
            vmem(((segs + 1) * cols, first_len)),
            pltpu.SemaphoreType.DMA((segs + 7,)),
            pltpu.SemaphoreType.DMA((2 * templates,)),
        ],
        out_shape=pltpu.VMEM((dev_count * rows, lanes + 2 * half_len), BF16),
        compiler_params=params(16),
        name="stage_one",
    )(
        *in_hbm(
            order, jnp.swapaxes(strain, 1, 2), jnp.swapaxes(analysis, 0, 1), spin, win_c, win_s,
            cos_one.astype(BF16), sin_one.astype(BF16), bank,
        ),
    )
    moved = lax.all_to_all(
        sent.reshape(dev_count, rows, lanes + 2 * half_len), "tmpl", split_axis=0, concat_axis=0, tiled=True
    )
    own = moved[:, :, lanes:]
    other = lax.ppermute(own, "grp", [(0, 1), (1, 0)])

    split = halves(half_len)
    low = 2 * np.arange(rows // 2)
    lift_rows = [np.concatenate([low + odd, first_len - low - odd]) for odd in range(2)]
    lift_init = [turns(at[:, None] * second[None, :], length) for at in lift_rows]
    cols_parts = []
    for odd in range(2):
        straight = devices[:, None] * rows + low[None, :] + odd
        turned = np.where(straight == 0, first_len // 2, first_len - straight)
        cols_parts.append(np.concatenate([straight, turned], 1).reshape(-1))
    cols_rows = np.concatenate(cols_parts)
    mid_rows = lift_rows[0].copy()
    mid_rows[rows // 2] = first_len // 2
    step_sign = np.where(np.arange(rows) < rows // 2, rows, -rows)
    fore = [
        *turns(step[:, None] * split[None, :], second_len),
        *turns(STEP * split[None, :], second_len),
        *turns(near[:, None] * second[None, :], length),
        *turns(rows * devices[:, None, None] * second[None, None, :], length),
    ]
    forward, near_c, near_s = pl.pallas_call(
        forward_kernel,
        out_shape=[
            pltpu.HBM((2, second_len, half_len), BF16),
            *[pltpu.VMEM((rows, second_len), F32)] * 2,
        ],
        in_specs=[whole()] * len(fore),
        out_specs=[outside()] + [whole()] * 2,
        scratch_shapes=[vmem((2, second_len, half_len)), pltpu.SemaphoreType.DMA],
        compiler_params=params(16),
        cost_estimate=pl.CostEstimate(flops=10**7, bytes_accessed=2 * 10**7, transcendentals=0),
        name="forward_tables",
    )(*in_hbm(*fore))
    back = [
        *turns(2 * step[:, None] * half[None, :], second_len),
        *turns((2 * step[:, None] + 1) * half[None, :], second_len),
        *turns(2 * STEP * half[None, :], second_len),
        np.stack([lift_init[0][0], lift_init[1][0]]),
        np.stack([lift_init[0][1], lift_init[1][1]]),
        *turns(step_sign[:, None] * second[None, :], length),
        *turns(mid_rows[:, None] * second[None, :], length),
        *turns(step[:, None] * cols_rows[None, :], first_len),
        *turns(STEP * cols_rows[None, :], first_len),
    ]
    shapes = [
        ((half_len, second_len), BF16),
        ((half_len, second_len), BF16),
        ((first_len, second_len), F32),
        ((first_len, second_len), F32),
        ((first_len, 2 * first_len), BF16),
        ((first_len, first_len), BF16),
        ((half_len, half_len), BF16),
    ]
    inverse_tables = pl.pallas_call(
        inverse_tables_kernel,
        out_shape=[pltpu.VMEM(*shape) for shape in shapes],
        in_specs=[whole()] * len(back),
        out_specs=[whole()] * len(shapes),
        compiler_params=params(8),
        cost_estimate=pl.CostEstimate(flops=10**7, bytes_accessed=2 * 10**7, transcendentals=0),
        name="inverse_tables",
    )
    even_table, odd_table, lift_c, lift_s, cols_table, by_rows, by_bins = inverse_tables(*in_hbm(*back))

    mid_c, mid_s = turns(first_len // 2 * second[None, :], length)
    all_rows = 2 * (segs + 2) * rows
    stage_two = pl.pallas_call(
        functools.partial(stage_two_kernel, segs, cols),
        out_shape=jax.ShapeDtypeStruct((2 * rows, 3 * half_len), BF16),
        in_specs=[whole()] * 3 + [outside()] * 3,
        out_specs=whole(),
        scratch_shapes=[
            *[vmem((1, second_len), F32)] * 2,
            vmem(forward.shape),
            vmem((all_rows, second_len)),
            vmem((rows, second_len), F32),
            vmem((all_rows, second_len), F32),
            pltpu.SemaphoreType.DMA((4,)),
        ],
        compiler_params=params(24),
        cost_estimate=pl.CostEstimate(flops=10**9, bytes_accessed=4 * 10**6, transcendentals=0),
        name="stage_two",
    )
    block = stage_two(moved, *in_vmem(near_c, near_s), *in_hbm(mid_c, mid_s, forward))

    two = swap_with(block, 8)
    one = swap_with(block, 4)
    beside = swap_with(block, 2)
    both = swap_with(jnp.stack([one, two]), 2)
    far = swap_with(two, 4)
    near = jnp.stack([block, beside, one, two])
    theirs = swap_with(near, 1)
    last = swap_with(far, 2)
    late = swap_with(jnp.stack([both[0], both[1], far, last]), 1)

    choose = pl.pallas_call(
        choose_kernel,
        grid_spec=pltpu.PrefetchScalarGridSpec(
            num_scalar_prefetch=2,
            grid=(),
            in_specs=[whole()] * 4,
            out_specs=whole(),
            scratch_shapes=[vmem((first_len, 2 * half_len))],
        ),
        out_shape=jax.ShapeDtypeStruct((first_len, 2 * half_len), BF16),
        compiler_params=params(16),
        cost_estimate=pl.CostEstimate(flops=10**9, bytes_accessed=4 * 10**6, transcendentals=0),
        name="choose",
    )
    chosen = choose(order, cutoff, own, other, *in_vmem(by_rows, by_bins))

    spread = [(2 * first_len, second_len), BF16]
    tables = in_vmem(even_table, odd_table, lift_c, lift_s)
    early = pl.pallas_call(
        early_kernel,
        out_shape=[pltpu.VMEM(*spread), pltpu.VMEM((rows, half_len), F32)],
        in_specs=[whole()] * 9,
        out_specs=[whole()] * 2,
        scratch_shapes=[vmem((len(EARLY) * 2 * rows, 2 * half_len))],
        compiler_params=params(16),
        cost_estimate=pl.CostEstimate(flops=10**9, bytes_accessed=4 * 10**6, transcendentals=0),
        name="early",
    )
    lifted, norm = early(near, theirs, both, far, chosen, *tables)
    result, _ = pl.pallas_call(
        late_kernel,
        out_shape=[jax.ShapeDtypeStruct((1, first_len, second_len), BF16), pltpu.VMEM(*spread)],
        in_specs=[whole()] * 10,
        out_specs=[whole()] * 2,
        scratch_shapes=[vmem((len(LATE) * 2 * rows, 2 * half_len))],
        input_output_aliases={2: 1},
        compiler_params=params(16),
        name="late",
    )(last, late, *in_vmem(lifted, norm), chosen, *tables, *in_vmem(cols_table))
    return result


def angles(left_idx, right_idx, period):
    product = left_idx[:, None] * right_idx[None, :] % period
    phase_angle = product.astype(jnp.float32) * (2.0 * math.pi / period)
    return (jnp.cos(phase_angle), jnp.sin(phase_angle))


def filtered(white_pair, tmpl_pair, cut_bins, freq_bin):
    white_real = white_pair[0].astype(jnp.float32)
    white_imag = white_pair[1].astype(jnp.float32)
    tmpl_real = tmpl_pair[0].astype(jnp.float32)
    tmpl_imag = tmpl_pair[1].astype(jnp.float32)
    in_band = freq_bin[None] < cut_bins[:, None, None]
    filt_real = jnp.where(in_band, white_real * tmpl_real + white_imag * tmpl_imag, 0.0)
    filt_imag = jnp.where(in_band, white_imag * tmpl_real - white_real * tmpl_imag, 0.0)
    return jnp.concatenate([filt_real, filt_imag], -1).astype(jnp.bfloat16)


def inverse_rows(stacked, row_bins, second_len, length):
    half_len = second_len // 2
    cosine, sine = angles(
        jnp.arange(half_len, dtype=jnp.int32), jnp.arange(second_len, dtype=jnp.int32), second_len
    )
    dft_table = jnp.concatenate(
        [jnp.concatenate([cosine, sine], 1), jnp.concatenate([-sine, cosine], 1)], 0
    ).astype(jnp.bfloat16)
    spread = jnp.einsum("tkf,fg->tkg", stacked, dft_table, preferred_element_type=jnp.float32)
    spread_real = spread[..., :second_len]
    spread_imag = spread[..., second_len:]
    cos_twist, sin_twist = angles(row_bins, jnp.arange(second_len, dtype=jnp.int32), length)
    lift_real = spread_real * cos_twist - spread_imag * sin_twist
    lift_imag = spread_real * sin_twist + spread_imag * cos_twist
    return jnp.concatenate([lift_real, lift_imag], -1).astype(jnp.bfloat16)


def inverse_cols(lifted, first_len, second_len):
    row_idx = jnp.arange(first_len, dtype=jnp.int32)
    cosine, sine = angles(row_idx, row_idx, first_len)
    cosine = cosine.astype(jnp.bfloat16)
    sine = sine.astype(jnp.bfloat16)
    lift_real = lifted[..., :second_len]
    lift_imag = lifted[..., second_len:]
    field_real = jnp.einsum(
        "ak,tkb->tab", cosine, lift_real, preferred_element_type=jnp.float32
    ) - jnp.einsum("ak,tkb->tab", sine, lift_imag, preferred_element_type=jnp.float32)
    field_imag = jnp.einsum(
        "ak,tkb->tab", sine, lift_real, preferred_element_type=jnp.float32
    ) + jnp.einsum("ak,tkb->tab", cosine, lift_imag, preferred_element_type=jnp.float32)
    return (field_real, field_imag)


def plain_local(strain, analysis, bank, cutoff, order):
    highest = lax.Precision.HIGHEST
    dev_count = lax.axis_size("tmpl")
    my_index = lax.axis_index("tmpl")
    seg_count = strain.shape[0]
    first_len = strain.shape[1]
    col_count = strain.shape[2]
    second_len = col_count * dev_count
    length = first_len * second_len
    half_len = second_len // 2
    row_count = first_len // dev_count
    row_idx = jnp.arange(first_len, dtype=jnp.int32)
    col_index = my_index * col_count + jnp.arange(col_count, dtype=jnp.int32)
    sample_idx = row_idx[:, None] * second_len + col_index[None, :]
    window = (
        math.sqrt(8.0 / 3.0) * jnp.sin(sample_idx.astype(jnp.float32) * (math.pi / length)) ** 2
    )
    series = jnp.concatenate([strain * window, analysis[None]], 0)
    cos_one, sin_one = angles(row_idx, row_idx, first_len)
    part_real = jnp.einsum("ka,sab->skb", cos_one, series, precision=highest)
    part_imag = -jnp.einsum("ka,sab->skb", sin_one, series, precision=highest)
    cos_twist, sin_twist = angles(row_idx, col_index, length)
    twist_real = part_real * cos_twist + part_imag * sin_twist
    twist_imag = part_imag * cos_twist - part_real * sin_twist
    moved = lax.all_to_all(
        jnp.stack([twist_real, twist_imag]).astype(jnp.bfloat16),
        "tmpl",
        split_axis=2,
        concat_axis=3,
        tiled=True,
    ).astype(jnp.float32)
    cos_two, sin_two = angles(
        jnp.arange(second_len, dtype=jnp.int32), jnp.arange(half_len, dtype=jnp.int32), second_len
    )
    spec_real = jnp.einsum("skb,bf->skf", moved[0], cos_two, precision=highest) + jnp.einsum(
        "skb,bf->skf", moved[1], sin_two, precision=highest
    )
    spec_imag = jnp.einsum("skb,bf->skf", moved[1], cos_two, precision=highest) - jnp.einsum(
        "skb,bf->skf", moved[0], sin_two, precision=highest
    )
    power_spec = jnp.maximum(
        jnp.mean(spec_real[:seg_count] ** 2 + spec_imag[:seg_count] ** 2, axis=0), 0.2 * length
    )
    whitened = jnp.stack(
        [spec_real[seg_count] / power_spec, spec_imag[seg_count] / power_spec]
    ).astype(jnp.bfloat16)
    own_rows = my_index * row_count + jnp.arange(row_count, dtype=jnp.int32)
    half_idx = jnp.arange(half_len, dtype=jnp.int32)
    freq_local = own_rows[:, None] + first_len * half_idx[None, :]
    chosen = jnp.take(bank, order, axis=1)
    cuts = jnp.take(cutoff, order)
    bank_real = chosen[0].astype(jnp.float32)
    bank_imag = chosen[1].astype(jnp.float32)
    in_band = freq_local[None] < cuts[:, None, None]
    local_norm = jnp.sum(
        jnp.where(in_band, (bank_real**2 + bank_imag**2) / power_spec, 0.0), axis=(1, 2)
    )
    norm_sq = lax.psum(local_norm, "tmpl")
    per_device = cuts.shape[0] // dev_count
    own_norm = lax.dynamic_slice_in_dim(norm_sq, my_index * per_device, per_device)
    stacked = filtered(whitened, chosen, cuts, freq_local)
    lifted = lax.all_to_all(
        inverse_rows(stacked, own_rows, second_len, length),
        "tmpl",
        split_axis=0,
        concat_axis=1,
        tiled=True,
    )
    field_real, field_imag = inverse_cols(lifted, first_len, second_len)
    magnitude = jnp.sqrt(field_real**2 + field_imag**2)
    return (magnitude / jnp.sqrt(own_norm)[:, None, None]).astype(jnp.bfloat16)


def local(strain, analysis, bank, cutoff, order):
    dev_count, segs, cols = lax.axis_size("tmpl"), strain.shape[0], strain.shape[2]
    rows = strain.shape[1] // dev_count // 2
    fits = rows == STEP and cols == 64 and segs % 2 == 0 and dev_count == len(EARLY + LATE)
    if fits and order.shape[0] == dev_count and lax.axis_size("grp") == 2:
        return tiled_local(strain, analysis, bank, cutoff, order)
    return plain_local(strain, analysis, bank, cutoff, order)


def solution(mesh):
    return jax.shard_map(
        local,
        mesh=mesh,
        in_specs=(P("grp", None, "tmpl"), P("grp", "tmpl"), P(None, None, "tmpl", None), P(), P()),
        out_specs=P(("grp", "tmpl"), None, None),
        check_vma=False,
    )
```

time: 92.4 us -> 68.9 us (0.75)
  waiting for transfers between devices: 43.4 us -> 30.5 us
  Pallas kernels: 29.4 us -> 20.3 us
    ppermute x1, waiting for transfers between devices: 12.8 us -> 0.01 us  [tiled_local(): other = lax.ppermute(own, 'grp', [(0, 1), (1, 0)])]
    pallas_call x5 -> x7, Pallas kernels: 29.4 us -> 20.3 us  [the longest x1 3.77 us: tiled_local(): inverse_tables(*in_hbm(*back))]
    ppermute x7 -> x8, waiting for transfers between devices: 12.3 us -> 9.44 us  [swap_with(): return lax.ppermute(array, 'tmpl', pairs)]
    all_to_all x1, waiting for transfers between devices: 18.4 us -> 21 us  [tiled_local(): lax.all_to_all(sent.reshape(dev_count, rows, lanes + 2 * half_len), 'tmpl...]
    ppermute x7 -> x8, starting transfers between devices: 9.18 us -> 8.46 us  [swap_with(): return lax.ppermute(array, 'tmpl', pairs)]
  transfers between devices with their start and end apart: 9 -> 10, of which waited for: 5 -> 5; matrix products, arithmetic and copies ran while one was open for 0% -> 0% of each run, Pallas kernels for 10% -> 15%
where the time goes in v1:
time: 68.9 us; the launch traced here: 68.6 us
  waiting for transfers between devices  30.5 us (44%)
  Pallas kernels  20.3 us (29%)
  starting transfers between devices  17.4 us (25%)
    all_to_all x1, waiting for transfers between devices, tiled_local(): lax.all_to_all(sent.reshape(dev_count, rows, lanes + 2 * half_len), 'tmpl...  21 us
    ppermute x8, waiting for transfers between devices, swap_with(): return lax.ppermute(array, 'tmpl', pairs)  9.44 us
    ppermute x8, starting transfers between devices, swap_with(): return lax.ppermute(array, 'tmpl', pairs)  8.46 us
    all_to_all x1, starting transfers between devices, tiled_local(): lax.all_to_all(sent.reshape(dev_count, rows, lanes + 2 * half_len), 'tmpl...  7.43 us
    pallas_call x1, Pallas kernels, tiled_local(): inverse_tables(*in_hbm(*back))  3.77 us
    pallas_call x1, Pallas kernels, tiled_local(): pl.pallas_call(stage_one_kernel, in_specs=[outside()] * 9, out_specs=whol...  3.72 us
    pallas_call x1, Pallas kernels, tiled_local(): pl.pallas_call(late_kernel, out_shape=[jax.ShapeDtypeStruct((1, first_len...  3.43 us
    pallas_call x1, Pallas kernels, tiled_local(): stage_two(moved, *in_vmem(near_c, near_s), *in_hbm(mid_c, mid_s, forward))  3.08 us
  transfers between devices with their start and end apart: 10, of which 5 were waited for; matrix products, arithmetic and copies ran while one was open for 0% of the time, Pallas kernels for 15%

profile of v1, /device:TPU:0, one launch (start us, length us, event | category | flops | bytes accessed | tf_op | source)
XLA Modules:
  0.0 68.6 jit_solution(9534783671265017124)
XLA Ops:
  0.0 3.7 %stage_one.1 = bf16[256,2176]{1,0:T(8,128)(2,1)} custom-call(s32[16]{0:T(128)} %order.1, f32[8,64,512]{2,1,0:T(8,128)} %bitcast.12, f32[64,512]{1,0:T(8,128)} %bitcast.17, f32[16,2,512]{2,1,0:T(2,128)} %constant.62.clone.spin_hbm, f32[64,512]{1,0:T(8,128)} %constant.63.clone.win_c_hbm, f32[64,512]{1,0:T(8,128)} %constant.64.clone.win_s_hbm, ...), custom_call_target="tpu_custom_call" | custom-call | tf_op jit(solution)/shard_map/stage_one/pallas_call | solution.py:490
  3.7 7.4 %all-to-all-start = ((bf16[16,16,2176]{2,1,0:T(8,128)(2,1)}), bf16[16,16,2176]{2,1,0:T(8,128)(2,1)S(1)}, u32[]{:S(2)}, u32[]{:S(2)}) async-start(bf16[16,16,2176]{2,1,0:T(8,128)(2,1)} %bitcast.2), calls=%async_computation | async-start | bytes 2228224 | tf_op jit(solution)/shard_map/all_to_all | solution.py:516
  11.2 2.9 %forward_tables.1 = (bf16[2,1024,512]{2,1,0:T(8,128)(2,1)}, f32[16,1024]{1,0:T(8,128)S(1)}, f32[16,1024]{1,0:T(8,128)S(1)}) custom-call(f32[16,512]{1,0:T(8,128)} %constant.67.clone.fore_c, f32[16,512]{1,0:T(8,128)} %constant.68.clone.fore_s, f32[1,512]{1,0:T(1,128)} %constant.69.clone.fore_rc, f32[1,512]{1,0:T(1,128)} %constant.70.clone.fore_rs, ...), custom_call_target="tpu_custom_call" | custom-call | flops 10000000 | bytes 20000000 | tf_op jit(solution)/shard_map/forward_tables/pallas_call | solution.py:541
  14.1 21.0 %all-to-all-done.moved = bf16[16,16,2176]{2,1,0:T(8,128)(2,1)S(1)} async-done(((bf16[16,16,2176]{2,1,0:T(8,128)(2,1)}), bf16[16,16,2176]{2,1,0:T(8,128)(2,1)S(1)}, u32[]{:S(2)}, u32[]{:S(2)}) %all-to-all-start) | async-done | bytes 1114144 | tf_op jit(solution)/shard_map/all_to_all | solution.py:516
  35.1 3.1 %stage_two.1 = bf16[32,1536]{1,0:T(8,128)(2,1)S(1)} custom-call(bf16[16,16,2176]{2,1,0:T(8,128)(2,1)S(1)} %all-to-all-done.moved, f32[16,1024]{1,0:T(8,128)S(1)} %get-tuple-element.18.near_c, f32[16,1024]{1,0:T(8,128)S(1)} %get-tuple-element.19.near_s, f32[1,1024]{1,0:T(1,128)} %constant.91.clone.mid_c_hbm, f32[1,1024]{1,0:T(1,128)} %constant.92.clone.mid_s_hbm, ...), custom_call_target="tpu_custom_call" | custom-call | flops 1000000000 | bytes 4000000 | tf_op jit(solution)/shard_map/stage_two/pallas_call | solution.py:604
  38.2 0.0 copy-start
  38.2 0.0 copy-start.1
  38.2 5.5 %collective-permute-start = (bf16[32,1536]{1,0:T(8,128)(2,1)S(1)}, bf16[32,1536]{1,0:T(8,128)(2,1)S(1)}, u32[]{:S(2)}, u32[]{:S(2)}) collective-permute-start(bf16[32,1536]{1,0:T(8,128)(2,1)S(1)} %stage_two.1), channel_id=1, source_target_pairs={{0,8},{1,9},{2,10},{3,11},{4,12},{5,13},{6,14},{7,15},{8,0},{9,1},... | collective-permute-start | bytes 294920 | tf_op jit(solution)/shard_map/ppermute | solution.py:468
  43.7 0.0 collective-permute-start.3
  43.7 1.4 %collective-permute-start.6 = (bf16[32,1536]{1,0:T(8,128)(2,1)S(1)}, bf16[32,1536]{1,0:T(8,128)(2,1)S(1)}, u32[]{:S(2)}, u32[]{:S(2)}) collective-permute-start(bf16[32,1536]{1,0:T(8,128)(2,1)S(1)} %stage_two.1), channel_id=1, source_target_pairs={{0,2},{1,3},{2,0},{3,1},{4,6},{5,7},{6,4},{7,5},{8,10},{9,11},{10,... | collective-permute-start | bytes 294920 | tf_op jit(solution)/shard_map/ppermute | solution.py:468
  45.2 0.1 slice.7.own
  45.2 1.6 %collective-permute-start.8 = (bf16[16,16,1024]{2,1,0:T(8,128)(2,1)S(1)}, bf16[16,16,1024]{2,1,0:T(8,128)(2,1)S(1)}, u32[]{:S(2)}, u32[]{:S(2)}) collective-permute-start(bf16[16,16,1024]{2,1,0:T(8,128)(2,1)S(1)} %slice.7.own), channel_id=1, source_target_pairs={{0,16},{16,0},{1,17},{17,1},{2,18},{18,2},{3,19},{19,3},{4,20},{20... | collective-permute-start | bytes 1572872 | tf_op jit(solution)/shard_map/ppermute | solution.py:520
  46.8 1.7 %collective-permute-done = bf16[32,1536]{1,0:T(8,128)(2,1)S(1)} collective-permute-done((bf16[32,1536]{1,0:T(8,128)(2,1)S(1)}, bf16[32,1536]{1,0:T(8,128)(2,1)S(1)}, u32[]{:S(2)}, u32[]{:S(2)}) %collective-permute-start) | collective-permute-done | bytes 98336 | tf_op jit(solution)/shard_map/ppermute | solution.py:468
  48.5 0.0 collective-permute-start.1
  48.5 0.5 collective-permute-done.3
  49.0 1.4 %collective-permute-start.4 = (bf16[2,32,1536]{2,1,0:T(8,128)(2,1)S(1)}, bf16[2,32,1536]{2,1,0:T(8,128)(2,1)S(1)}, u32[]{:S(2)}, u32[]{:S(2)}) collective-permute-start(bf16[2,32,1536]{2,1,0:T(8,128)(2,1)S(1)} %pad_maximum_fusion.2), channel_id=1, source_target_pairs={{0,2},{1,3},{2,0},{3,1},{4,6},{5,7},{6,4},{7,5},{8,10},{9,11},{10,... | collective-permute-start | bytes 589832 | tf_op jit(solution)/shard_map/ppermute | solution.py:468
  50.4 2.8 %collective-permute-done.1.far = bf16[32,1536]{1,0:T(8,128)(2,1)S(1)} collective-permute-done((bf16[32,1536]{1,0:T(8,128)(2,1)S(1)}, bf16[32,1536]{1,0:T(8,128)(2,1)S(1)}, u32[]{:S(2)}, u32[]{:S(2)}) %collective-permute-start.1) | collective-permute-done | bytes 98336 | tf_op jit(solution)/shard_map/ppermute | solution.py:468
  53.1 0.0 collective-permute-start.2
  53.1 0.0 collective-permute-done.6
  53.1 0.1 pad_maximum_fusion.1.near
  53.2 0.1 collective-permute-start.7
  53.3 4.5 %collective-permute-done.2.last = bf16[32,1536]{1,0:T(8,128)(2,1)S(1)} collective-permute-done((bf16[32,1536]{1,0:T(8,128)(2,1)S(1)}, bf16[32,1536]{1,0:T(8,128)(2,1)S(1)}, u32[]{:S(2)}, u32[]{:S(2)}) %collective-permute-start.2) | collective-permute-done | bytes 98336 | tf_op jit(solution)/shard_map/ppermute | solution.py:468
  57.8 0.0 collective-permute-done.4.both
  57.8 0.1 collective-permute-start.5
  57.9 3.8 %inverse_tables.1 = (bf16[512,1024]{1,0:T(8,128)(2,1)S(1)}, bf16[512,1024]{1,0:T(8,128)(2,1)S(1)}, f32[512,1024]{1,0:T(8,128)S(1)}, f32[512,1024]{1,0:T(8,128)S(...) custom-call(f32[16,512]{1,0:T(8,128)} %constant.75.clone.even_c, ...), custom_call_target="tpu_custom_call" | custom-call | flops 10000000 | bytes 20000000 | tf_op jit(solution)/shard_map/inverse_tables/pallas_call | solution.py:583
  61.7 0.0 collective-permute-done.8.other
  61.7 0.0 copy-done
  61.7 0.0 copy-done.1
  61.7 1.9 %choose.1.chosen = bf16[512,1024]{1,0:T(8,128)(2,1)S(1)} custom-call(s32[16]{0:T(128)S(1)} %copy-done, s32[16]{0:T(128)S(1)} %copy-done.1, bf16[16,16,1024]{2,1,0:T(8,128)(2,1)S(1)} %slice.7.own, bf16[16,16,1024]{2,1,0:T(8,128)(2,1)S(1)} %collective-permute-done.8.other, bf16[512,512]{1,0:T(8,128)(2,1)S(1)} %get-tuple-element.21.by_rows, ...), custom_call_target="tpu_custom_call" | custom-call | flops 1000000000 | bytes 4000000 | tf_op jit(solution)/shard_map/choose/pallas_call | solution.py:630
  63.6 0.0 collective-permute-done.7.theirs
  63.6 1.5 %early.1 = (bf16[1024,1024]{1,0:T(8,128)(2,1)S(1)}, f32[16,512]{1,0:T(8,128)S(1)}) custom-call(bf16[4,32,1536]{2,1,0:T(8,128)(2,1)S(1)} %pad_maximum_fusion.1.near, bf16[4,32,1536]{2,1,0:T(8,128)(2,1)S(1)} %collective-permute-done.7.theirs, bf16[2,32,1536]{2,1,0:T(8,128)(2,1)S(1)} %collective-permute-done.4.both, ...), custom_call_target="tpu_custom_call" | custom-call | flops 1000000000 | bytes 4000000 | tf_op jit(solution)/shard_map/early/pallas_call | solution.py:644
  65.1 0.0 collective-permute-done.5.theirs
  65.1 3.4 %late.1 = (bf16[1,512,1024]{2,1,0:T(8,128)(2,1)}, bf16[1024,1024]{1,0:T(8,128)(2,1)S(1)}) custom-call(bf16[32,1536]{1,0:T(8,128)(2,1)S(1)} %collective-permute-done.2.last, bf16[4,32,1536]{2,1,0:T(8,128)(2,1)S(1)} %collective-permute-done.5.theirs, bf16[1024,1024]{1,0:T(8,128)(2,1)S(1)} %get-tuple-element.27.early, ...), custom_call_target="tpu_custom_call", output_to_operand_aliasing={{1}: (2, {})} | custom-call | tf_op jit(solution)/shard_map/late/pallas_call | solution.py:645
  (2 shorter events, 0.1 us)
Async XLA Ops:
  3.7 31.4 %all-to-all-start = ((bf16[16,16,2176]{2,1,0:T(8,128)(2,1)}), bf16[16,16,2176]{2,1,0:T(8,128)(2,1)S(1)}, u32[]{:S(2)}, u32[]{:S(2)}) async-start(bf16[16,16,2176]{2,1,0:T(8,128)(2,1)} %bitcast.2), calls=%async_computation | async-start | bytes 2228224 | tf_op jit(solution)/shard_map/all_to_all | solution.py:516
  38.2 23.5 %copy-start = (s32[16]{0:T(128)S(1)}, s32[16]{0:T(128)}, u32[]{:S(2)}) copy-start(s32[16]{0:T(128)} %order.1) | copy-start | bytes 196
  38.2 23.5 %copy-start.1 = (s32[16]{0:T(128)S(1)}, s32[16]{0:T(128)}, u32[]{:S(2)}) copy-start(s32[16]{0:T(128)} %cuts.1) | copy-start | bytes 196
  38.2 10.3 %collective-permute-start = (bf16[32,1536]{1,0:T(8,128)(2,1)S(1)}, bf16[32,1536]{1,0:T(8,128)(2,1)S(1)}, u32[]{:S(2)}, u32[]{:S(2)}) collective-permute-start(bf16[32,1536]{1,0:T(8,128)(2,1)S(1)} %stage_two.1), channel_id=1, source_target_pairs={{0,8},{1,9},{2,10},{3,11},{4,12},{5,13},{6,14},{7,15},{8,0},{9,1},... | collective-permute-start | bytes 294920 | tf_op jit(solution)/shard_map/ppermute | solution.py:468
  43.7 5.3 %collective-permute-start.3 = (bf16[32,1536]{1,0:T(8,128)(2,1)S(1)}, bf16[32,1536]{1,0:T(8,128)(2,1)S(1)}, u32[]{:S(2)}, u32[]{:S(2)}) collective-permute-start(bf16[32,1536]{1,0:T(8,128)(2,1)S(1)} %stage_two.1), channel_id=1, source_target_pairs={{0,4},{1,5},{2,6},{3,7},{4,0},{5,1},{6,2},{7,3},{8,12},{9,13},{10,... | collective-permute-start | bytes 294920 | tf_op jit(solution)/shard_map/ppermute | solution.py:468
  43.7 9.4 %collective-permute-start.6 = (bf16[32,1536]{1,0:T(8,128)(2,1)S(1)}, bf16[32,1536]{1,0:T(8,128)(2,1)S(1)}, u32[]{:S(2)}, u32[]{:S(2)}) collective-permute-start(bf16[32,1536]{1,0:T(8,128)(2,1)S(1)} %stage_two.1), channel_id=1, source_target_pairs={{0,2},{1,3},{2,0},{3,1},{4,6},{5,7},{6,4},{7,5},{8,10},{9,11},{10,... | collective-permute-start | bytes 294920 | tf_op jit(solution)/shard_map/ppermute | solution.py:468
  45.2 16.4 %collective-permute-start.8 = (bf16[16,16,1024]{2,1,0:T(8,128)(2,1)S(1)}, bf16[16,16,1024]{2,1,0:T(8,128)(2,1)S(1)}, u32[]{:S(2)}, u32[]{:S(2)}) collective-permute-start(bf16[16,16,1024]{2,1,0:T(8,128)(2,1)S(1)} %slice.7.own), channel_id=1, source_target_pairs={{0,16},{16,0},{1,17},{17,1},{2,18},{18,2},{3,19},{19,3},{4,20},{20... | collective-permute-start | bytes 1572872 | tf_op jit(solution)/shard_map/ppermute | solution.py:520
  48.5 4.6 %collective-permute-start.1 = (bf16[32,1536]{1,0:T(8,128)(2,1)S(1)}, bf16[32,1536]{1,0:T(8,128)(2,1)S(1)}, u32[]{:S(2)}, u32[]{:S(2)}) collective-permute-start(bf16[32,1536]{1,0:T(8,128)(2,1)S(1)} %collective-permute-done), channel_id=1, source_target_pairs={{0,4},{1,5},{2,6},{3,7},{4,0},{5,1},{6,2},{7,3},{8,12},{9,13},{10,... | collective-permute-start | bytes 294920 | tf_op jit(solution)/shard_map/ppermute | solution.py:468
  49.0 8.7 %collective-permute-start.4 = (bf16[2,32,1536]{2,1,0:T(8,128)(2,1)S(1)}, bf16[2,32,1536]{2,1,0:T(8,128)(2,1)S(1)}, u32[]{:S(2)}, u32[]{:S(2)}) collective-permute-start(bf16[2,32,1536]{2,1,0:T(8,128)(2,1)S(1)} %pad_maximum_fusion.2), channel_id=1, source_target_pairs={{0,2},{1,3},{2,0},{3,1},{4,6},{5,7},{6,4},{7,5},{8,10},{9,11},{10,... | collective-permute-start | bytes 589832 | tf_op jit(solution)/shard_map/ppermute | solution.py:468
  53.1 4.6 %collective-permute-start.2 = (bf16[32,1536]{1,0:T(8,128)(2,1)S(1)}, bf16[32,1536]{1,0:T(8,128)(2,1)S(1)}, u32[]{:S(2)}, u32[]{:S(2)}) collective-permute-start(bf16[32,1536]{1,0:T(8,128)(2,1)S(1)} %collective-permute-done.1.far), channel_id=1, source_target_pairs={{0,2},{1,3},{2,0},{3,1},{4,6},{5,7},{6,4},{7,5},{8,10},{9,11},{10,... | collective-permute-start | bytes 294920 | tf_op jit(solution)/shard_map/ppermute | solution.py:468
  53.2 10.4 %collective-permute-start.7 = (bf16[4,32,1536]{2,1,0:T(8,128)(2,1)S(1)}, bf16[4,32,1536]{2,1,0:T(8,128)(2,1)S(1)}, u32[]{:S(2)}, u32[]{:S(2)}) collective-permute-start(bf16[4,32,1536]{2,1,0:T(8,128)(2,1)S(1)} %pad_maximum_fusion.1.near), channel_id=1, source_target_pairs={{0,1},{1,0},{2,3},{3,2},{4,5},{5,4},{6,7},{7,6},{8,9},{9,8},{10,11... | collective-permute-start | bytes 1179656 | tf_op jit(solution)/shard_map/ppermute | solution.py:468
  57.8 7.3 %collective-permute-start.5 = (bf16[4,32,1536]{2,1,0:T(8,128)(2,1)S(1)}, bf16[4,32,1536]{2,1,0:T(8,128)(2,1)S(1)}, u32[]{:S(2)}, u32[]{:S(2)}) collective-permute-start(bf16[4,32,1536]{2,1,0:T(8,128)(2,1)S(1)} %pad_maximum_fusion), channel_id=1, source_target_pairs={{0,1},{1,0},{2,3},{3,2},{4,5},{5,4},{6,7},{7,6},{8,9},{9,8},{10,11... | collective-permute-start | bytes 1179656 | tf_op jit(solution)/shard_map/ppermute | solution.py:468

commit v2 on v1

--- a/solution.py
+++ b/solution.py
@@ -14,7 +14,8 @@
 STEP = 16
 PIECE = 128
 EARLY = (0, 2, 4, 8, 1, 3, 5, 9, 6, 10, 12)
-LATE = (14, 7, 11, 13, 15)
+MIDDLE = (7, 11, 13)
+LATE = (14, 15)
 
 
 def turns(product, period):
@@ -67,6 +68,10 @@
     return pltpu.CompilerParams(vmem_limit_bytes=mib << 20)
 
 
+def turn(cos, sin, by_cos, by_sin):
+    return cos * by_cos - sin * by_sin, sin * by_cos + cos * by_sin
+
+
 def halves(count):
     return np.concatenate([np.arange(0, count, 2), np.arange(1, count, 2)])
 
@@ -76,27 +81,27 @@
 
 
 def stage_one_kernel(
-    order_hbm, strain_hbm, analysis_hbm, spin_hbm, win_c_hbm, win_s_hbm, cos_hbm, sin_hbm, bank, out,
-    order, strain, analysis, spin, win_c, win_s, cos, sin, packed, sems, bank_sems,
+    turns_of_eight, order_hbm, strain_hbm, analysis_hbm, spin_hbm, win_hbm, wave_hbm, bank, out,
+    order, strain, analysis, spin, win, wave, packed, sems, bank_sems,
 ):
-    segs, cols, _ = strain.shape
+    segs, cols, first_len = strain.shape
     tail = segs * cols
     templates, half_len = bank.shape[1], bank.shape[3]
     rows = out.shape[0] // templates
+    half = first_len // 2
     place, group = position()
     sources = [
+        (order_hbm, order),
         (spin_hbm.at[place], spin),
-        (win_c_hbm, win_c),
-        (win_s_hbm, win_s),
+        (win_hbm, win),
         *[(strain_hbm.at[seg], strain.at[seg]) for seg in range(segs)],
         (analysis_hbm, analysis),
-        (cos_hbm, cos),
-        (sin_hbm, sin),
-        (order_hbm, order),
+        (wave_hbm, wave),
     ]
     copies = start_copies(sources, sems)
-    copies.pop().wait()
     lane = 2 * (tail + cols)
+    for copy in copies[:3]:
+        copy.wait()
     bank_pairs = []
     for row in range(templates):
         for part in range(2):
@@ -110,28 +115,38 @@
                 )
             )
     bank_copies = start_copies(bank_pairs, bank_sems)
-    for copy in copies[:3]:
-        copy.wait()
     scale = 0.5 * math.sqrt(8.0 / 3.0)
-    window = scale - scale * (win_c[...] * spin[0:1, :] - win_s[...] * spin[1:2, :])
+    win_c, win_s = turn(win[0], win[1], spin[0:1, :], spin[1:2, :])
+    window = jnp.concatenate(
+        [scale - (win_c * (scale * by_cos) - win_s * (scale * by_sin)) for by_cos, by_sin in turns_of_eight], 0
+    )
+
+    def pack(at, values):
+        packed[0, at : at + cols, :] = (values[:, :half] + values[:, half:]).astype(BF16)
+        packed[1, at : at + cols, :] = (values[:, :half] - values[:, half:]).astype(BF16)
+
     for seg in range(segs):
         copies[3 + seg].wait()
-        packed[seg * cols : (seg + 1) * cols, :] = (strain[seg] * window).astype(BF16)
-    for copy in copies[3 + segs :]:
-        copy.wait()
-    packed[tail:, :] = analysis[...].astype(BF16)
-    real = matmul_nt(cos[...], packed[...])
-    imag = -matmul_nt(sin[...], packed[...])
+        pack(seg * cols, strain[seg] * window)
+    copies[3 + segs].wait()
+    pack(tail, analysis[...])
+    copies[4 + segs].wait()
+    both = [matmul_nt(wave[odd], packed[odd]) for odd in range(2)]
+    count = out.shape[0] // 2
+
+    def woven(part):
+        halves_of = [
+            table[part * count : (part + 1) * count].reshape(templates, rows // 2, tail + cols) for table in both
+        ]
+        return jnp.concatenate(halves_of, 1).reshape(2 * count, tail + cols)
+
+    real, imag = woven(0), woven(1)
     out[:, 0:tail] = real[:, :tail].astype(BF16)
     out[:, tail : 2 * tail] = imag[:, :tail].astype(BF16)
     joined = jnp.concatenate([real[:, tail:], imag[:, tail:]], 1)
     out[:, 2 * tail : lane] = joined.astype(BF16)
     for copy in bank_copies:
         copy.wait()
-
-
-def turn(cos, sin, by_cos, by_sin):
-    return cos * by_cos - sin * by_sin, sin * by_cos + cos * by_sin
 
 
 def forward_kernel(
@@ -225,7 +240,8 @@
     mid_c, mid_s, forward, stacked, middle, product, sems,
 ):
     place, _ = position()
-    _, second_len, half_len = forward.shape
+    _, half_len, _ = forward.shape
+    second_len = 2 * half_len
     quarter = half_len // 2
     pieces = [(forward_hbm.at[odd], forward.at[odd]) for odd in range(2)]
     pieces += [(mid_c_hbm, mid_c), (mid_s_hbm, mid_s)]
@@ -246,23 +262,31 @@
         )
 
     middle[...] = jnp.zeros_like(middle)
-    for tile in range(sources // 2):
+    tiles = sources // 2
+    for tile in range(tiles // 2):
         lane = slice(tile * width, (tile + 1) * width)
-        cos, sin = near_c[:, lane], near_s[:, lane]
+        lanes = (lane, slice(half_len + tile * width, half_len + (tile + 1) * width))
 
         def piece(lo, tile=tile):
             hi = lo + width
-            return pair(
-                moved[2 * tile, :, lo:hi].astype(F32), moved[2 * tile + 1, :, lo:hi].astype(F32)
-            )
-
-        def put(seg, real, imag, lane=lane, cos=cos, sin=sin):
-            middle[seg : seg + 1, lane] = imag[0:1, :]
-            imag = jnp.where(drop, 0.0, imag)
-            at = seg * rows
-            stacked[at : at + rows, lane] = (real * cos + imag * sin).astype(BF16)
-            at += all_rows
-            stacked[at : at + rows, lane] = (imag * cos - real * sin).astype(BF16)
+            found = []
+            for source in (2 * tile, 2 * tile + tiles):
+                found.append(
+                    pair(moved[source, :, lo:hi].astype(F32), moved[source + 1, :, lo:hi].astype(F32))
+                )
+            return [(found[0][at], found[1][at]) for at in range(2)]
+
+        def put(seg, real, imag, lane=lane, lanes=lanes):
+            turned_real, turned_imag = [], []
+            for half in range(2):
+                middle[seg : seg + 1, lanes[half]] = imag[half][0:1, :]
+                kept = jnp.where(drop, 0.0, imag[half])
+                cos, sin = near_c[:, lanes[half]], near_s[:, lanes[half]]
+                turned_real.append(real[half] * cos + kept * sin)
+                turned_imag.append(kept * cos - real[half] * sin)
+            for at, (low_half, high_half) in ((seg * rows, turned_real), (all_rows + seg * rows, turned_imag)):
+                stacked[0, at : at + rows, lane] = (low_half + high_half).astype(BF16)
+                stacked[1, at : at + rows, lane] = (low_half - high_half).astype(BF16)
 
         for twin in range(segs // 2):
             real_one, real_two = piece(twin * width)
@@ -273,8 +297,10 @@
         put(segs, real, imag)
     for copy in copies[2:]:
         copy.wait()
-    stacked[2 * all_rows : 2 * all_rows + rows, :] = (middle[...] * mid_c[...]).astype(BF16)
-    stacked[2 * all_rows + rows :, :] = (middle[...] * -mid_s[...]).astype(BF16)
+    for part, turned in enumerate((middle[...] * mid_c[...], middle[...] * -mid_s[...])):
+        at = slice(2 * all_rows + part * rows, 2 * all_rows + (part + 1) * rows)
+        stacked[0, at, :] = (turned[:, :half_len] + turned[:, half_len:]).astype(BF16)
+        stacked[1, at, :] = (turned[:, :half_len] - turned[:, half_len:]).astype(BF16)
 
     first_lane = lax.broadcasted_iota(jnp.int32, (rows, quarter), 1) == 0
     swap = jnp.logical_and(lax.broadcasted_iota(jnp.int32, (rows, quarter), 0) == 0, own_first)
@@ -284,7 +310,7 @@
         cos_at = slice(odd * half_len, odd * half_len + quarter)
         sin_at = slice(odd * half_len + quarter, (odd + 1) * half_len)
         copies[odd].wait()
-        product[:, odd * half_len : (odd + 1) * half_len] = matmul(stacked[...], forward[odd])
+        product[:, odd * half_len : (odd + 1) * half_len] = matmul(stacked[odd], forward[odd])
 
         def parts(at, lower_at, cos_at=cos_at, sin_at=sin_at):
             return (
@@ -444,10 +470,15 @@
     norm[...] = filter_blocks(EARLY, blocks, chosen, tables, zero, filtered, lifted)
 
 
+def middle_kernel(theirs, early, early_norm, chosen, *refs):
+    tables, (lifted, norm, filtered) = refs[:4], refs[4:]
+    blocks = [theirs.at[at] for at in range(3)]
+    norm[...] = filter_blocks(MIDDLE, blocks, chosen, tables, early_norm[...], filtered, lifted)
+
+
 def late_kernel(last, theirs, early, early_norm, chosen, *refs):
     tables, (cols_table, out, lifted, filtered) = refs[:4], refs[4:]
-    blocks = [last, *[theirs.at[at] for at in range(4)]]
-    norm = filter_blocks(LATE, blocks, chosen, tables, early_norm[...], filtered, lifted)
+    norm = filter_blocks(LATE, [last, theirs], chosen, tables, early_norm[...], filtered, lifted)
     scale = lax.rsqrt(jnp.sum(norm, keepdims=True))
     first_len = chosen.shape[0]
     per = first_len // 2
@@ -481,27 +512,30 @@
     first, second, half = np.arange(first_len), np.arange(second_len), np.arange(half_len)
     devices, step = np.arange(dev_count), np.arange(STEP)
     near = halves(rows)
-    packed = (devices[:, None] * rows + near[None, :]).reshape(-1, 1)
-    cos_one, sin_one = turns(packed * first[None, :], first_len)
-    sin_one[0] = 2 * (first % 2) - 1.0
-    win_c, win_s = turns(np.arange(cols)[:, None] + second_len * first[None, :], length)
+    packed = (devices[:, None] * rows + near[None, :]).reshape(dev_count, 2, rows // 2)
+    waves = []
+    for odd in range(2):
+        cos, sin = turns(packed[:, odd].reshape(-1, 1) * first[None, : first_len // 2], first_len)
+        if not odd:
+            sin[0] = 2 * (first[: first_len // 2] % 2) - 1.0
+        waves.append(np.concatenate([cos, -sin]))
+    win = np.stack(turns(np.arange(8)[:, None] + second_len * first[None, :], length))
     spin = np.stack(turns(cols * devices, length), 1)[:, :, None] * np.ones((1, 1, first_len), np.float32)
+    turns_of_eight = [tuple(float(at) for at in turns(8 * block, length)) for block in range(cols // 8)]
 
     sent = pl.pallas_call(
-        stage_one_kernel,
-        in_specs=[outside()] * 9,
+        functools.partial(stage_one_kernel, turns_of_eight),
+        in_specs=[outside()] * 7,
         out_specs=whole(),
         scratch_shapes=[
             pltpu.SMEM((templates,), jnp.int32),
             vmem((segs, cols, first_len), F32),
             vmem((cols, first_len), F32),
             vmem((2, first_len), F32),
-            vmem((cols, first_len), F32),
-            vmem((cols, first_len), F32),
-            vmem((dev_count * rows, first_len)),
-            vmem((dev_count * rows, first_len)),
-            vmem(((segs + 1) * cols, first_len)),
-            pltpu.SemaphoreType.DMA((segs + 7,)),
+            vmem((2, 8, first_len), F32),
+            vmem((2, dev_count * rows, first_len // 2)),
+            vmem((2, (segs + 1) * cols, first_len // 2)),
+            pltpu.SemaphoreType.DMA((segs + 5,)),
             pltpu.SemaphoreType.DMA((2 * templates,)),
         ],
         out_shape=pltpu.VMEM((dev_count * rows, lanes + 2 * half_len), BF16),
@@ -509,8 +543,8 @@
         name="stage_one",
     )(
         *in_hbm(
-            order, jnp.swapaxes(strain, 1, 2), jnp.swapaxes(analysis, 0, 1), spin, win_c, win_s,
-            cos_one.astype(BF16), sin_one.astype(BF16), bank,
+            order, jnp.swapaxes(strain, 1, 2), jnp.swapaxes(analysis, 0, 1), spin, win,
+            np.stack(waves).astype(BF16), bank,
         ),
     )
     moved = lax.all_to_all(
@@ -541,12 +575,12 @@
     forward, near_c, near_s = pl.pallas_call(
         forward_kernel,
         out_shape=[
-            pltpu.HBM((2, second_len, half_len), BF16),
+            pltpu.HBM((2, half_len, half_len), BF16),
             *[pltpu.VMEM((rows, second_len), F32)] * 2,
         ],
         in_specs=[whole()] * len(fore),
         out_specs=[outside()] + [whole()] * 2,
-        scratch_shapes=[vmem((2, second_len, half_len)), pltpu.SemaphoreType.DMA],
+        scratch_shapes=[vmem((2, half_len, half_len)), pltpu.SemaphoreType.DMA],
         compiler_params=params(16),
         cost_estimate=pl.CostEstimate(flops=10**7, bytes_accessed=2 * 10**7, transcendentals=0),
         name="forward_tables",
@@ -592,7 +626,7 @@
         scratch_shapes=[
             *[vmem((1, second_len), F32)] * 2,
             vmem(forward.shape),
-            vmem((all_rows, second_len)),
+            vmem((2, all_rows, half_len)),
             vmem((rows, second_len), F32),
             vmem((all_rows, second_len), F32),
             pltpu.SemaphoreType.DMA((4,)),
@@ -611,7 +645,8 @@
     near = jnp.stack([block, beside, one, two])
     theirs = swap_with(near, 1)
     last = swap_with(far, 2)
-    late = swap_with(jnp.stack([both[0], both[1], far, last]), 1)
+    more = swap_with(jnp.stack([both[0], both[1], far]), 1)
+    late = swap_with(last, 1)
 
     choose = pl.pallas_call(
         choose_kernel,
@@ -642,6 +677,18 @@
         name="early",
     )
     lifted, norm = early(near, theirs, both, far, chosen, *tables)
+    middle = pl.pallas_call(
+        middle_kernel,
+        out_shape=[pltpu.VMEM(*spread), pltpu.VMEM((rows, half_len), F32)],
+        in_specs=[whole()] * 8,
+        out_specs=[whole()] * 2,
+        scratch_shapes=[vmem((len(MIDDLE) * 2 * rows, 2 * half_len))],
+        input_output_aliases={1: 0},
+        compiler_params=params(16),
+        cost_estimate=pl.CostEstimate(flops=10**9, bytes_accessed=4 * 10**6, transcendentals=0),
+        name="middle",
+    )
+    lifted, norm = middle(more, *in_vmem(lifted, norm), chosen, *tables)
     result, _ = pl.pallas_call(
         late_kernel,
         out_shape=[jax.ShapeDtypeStruct((1, first_len, second_len), BF16), pltpu.VMEM(*spread)],
@@ -781,7 +828,7 @@
 def local(strain, analysis, bank, cutoff, order):
     dev_count, segs, cols = lax.axis_size("tmpl"), strain.shape[0], strain.shape[2]
     rows = strain.shape[1] // dev_count // 2
-    fits = rows == STEP and cols == 64 and segs % 2 == 0 and dev_count == len(EARLY + LATE)
+    fits = rows == STEP and cols == 64 and segs % 2 == 0 and dev_count == len(EARLY + MIDDLE + LATE)
     if fits and order.shape[0] == dev_count and lax.axis_size("grp") == 2:
         return tiled_local(strain, analysis, bank, cutoff, order)
     return plain_local(strain, analysis, bank, cutoff, order)

time: 68.9 us -> 68.6 us (level)
  starting transfers between devices: 17.4 us -> 19.1 us
  Pallas kernels: 20.3 us -> 18.8 us
    ppermute x8 -> x9, starting transfers between devices: 8.46 us -> 10.1 us  [swap_with(): return lax.ppermute(array, 'tmpl', pairs)]
    ppermute x8 -> x9, waiting for transfers between devices: 9.44 us -> 8.37 us  [swap_with(): return lax.ppermute(array, 'tmpl', pairs)]
    pallas_call x1, Pallas kernels: 3.08 us -> 2.1 us  [tiled_local(): stage_two(moved, *in_vmem(near_c, near_s), *in_hbm(mid_c, mid_s, forward))]
    pallas_call x2 -> x3, Pallas kernels: 6.65 us -> 6.28 us  [the longest x1 3.38 us: tiled_local(): pl.pallas_call(functools.partial(stage_one_kernel, turns_of_eight), in_sp...]
  transfers between devices with their start and end apart: 10 -> 11, of which waited for: 5 -> 5; matrix products, arithmetic and copies ran while one was open for 0% -> 0% of each run, Pallas kernels for 15% -> 15%
where the time goes in v2:
time: 68.6 us; the launch traced here: 68.3 us
  waiting for transfers between devices  30 us (44%)
  starting transfers between devices  19.1 us (28%)
  Pallas kernels  18.8 us (27%)
    all_to_all x1, waiting for transfers between devices, tiled_local(): lax.all_to_all(sent.reshape(dev_count, rows, lanes + 2 * half_len), 'tmpl...  21.7 us
    ppermute x9, starting transfers between devices, swap_with(): return lax.ppermute(array, 'tmpl', pairs)  10.1 us
    ppermute x9, waiting for transfers between devices, swap_with(): return lax.ppermute(array, 'tmpl', pairs)  8.37 us
    all_to_all x1, starting transfers between devices, tiled_local(): lax.all_to_all(sent.reshape(dev_count, rows, lanes + 2 * half_len), 'tmpl...  7.43 us
    pallas_call x1, Pallas kernels, tiled_local(): inverse_tables(*in_hbm(*back))  3.75 us
    pallas_call x1, Pallas kernels, tiled_local(): pl.pallas_call(functools.partial(stage_one_kernel, turns_of_eight), in_sp...  3.38 us
    pallas_call x1, Pallas kernels, tiled_local(): pl.pallas_call(late_kernel, out_shape=[jax.ShapeDtypeStruct((1, first_len...  3.28 us
    pallas_call x1, Pallas kernels, tiled_local(): pl.pallas_call(forward_kernel, out_shape=[pltpu.HBM((2, half_len, half_le...  2.28 us
  transfers between devices with their start and end apart: 11, of which 5 were waited for; matrix products, arithmetic and copies ran while one was open for 0% of the time, Pallas kernels for 15%

profile of v2, /device:TPU:0, one launch (start us, length us, event | category | flops | bytes accessed | tf_op | source)
XLA Modules:
  0.0 68.3 jit_solution(7209833975819542492)
XLA Ops:
  0.0 3.4 %stage_one.1 = bf16[256,2176]{1,0:T(8,128)(2,1)} custom-call(s32[16]{0:T(128)} %order.1, f32[8,64,512]{2,1,0:T(8,128)} %bitcast.10, f32[64,512]{1,0:T(8,128)} %bitcast.15, f32[16,2,512]{2,1,0:T(2,128)} %constant.58.clone.spin_hbm, f32[2,8,512]{2,1,0:T(8,128)} %constant.59.clone.win_hbm, bf16[2,256,256]{2,1,0:T(8,128)(2,1)} %constant.60.clone.wave_hbm, ...), custom_call_target="tpu_custom_call" | custom-call | tf_op jit(solution)/shard_map/stage_one/pallas_call | solution.py:526
  3.4 7.4 %all-to-all-start = ((bf16[16,16,2176]{2,1,0:T(8,128)(2,1)}), bf16[16,16,2176]{2,1,0:T(8,128)(2,1)S(1)}, u32[]{:S(2)}, u32[]{:S(2)}) async-start(bf16[16,16,2176]{2,1,0:T(8,128)(2,1)} %bitcast.2), calls=%async_computation | async-start | bytes 2228224 | tf_op jit(solution)/shard_map/all_to_all | solution.py:550
  10.8 2.3 %forward_tables.1 = (bf16[2,512,512]{2,1,0:T(8,128)(2,1)}, f32[16,1024]{1,0:T(8,128)S(1)}, f32[16,1024]{1,0:T(8,128)S(1)}) custom-call(f32[16,512]{1,0:T(8,128)} %constant.61.clone.fore_c, f32[16,512]{1,0:T(8,128)} %constant.62.clone.fore_s, f32[1,512]{1,0:T(1,128)} %constant.63.clone.fore_rc, f32[1,512]{1,0:T(1,128)} %constant.64.clone.fore_rs, ...), custom_call_target="tpu_custom_call" | custom-call | flops 10000000 | bytes 20000000 | tf_op jit(solution)/shard_map/forward_tables/pallas_call | solution.py:575
  13.1 21.7 %all-to-all-done.moved = bf16[16,16,2176]{2,1,0:T(8,128)(2,1)S(1)} async-done(((bf16[16,16,2176]{2,1,0:T(8,128)(2,1)}), bf16[16,16,2176]{2,1,0:T(8,128)(2,1)S(1)}, u32[]{:S(2)}, u32[]{:S(2)}) %all-to-all-start) | async-done | bytes 1114144 | tf_op jit(solution)/shard_map/all_to_all | solution.py:550
  34.8 2.1 %stage_two.1 = bf16[32,1536]{1,0:T(8,128)(2,1)S(1)} custom-call(bf16[16,16,2176]{2,1,0:T(8,128)(2,1)S(1)} %all-to-all-done.moved, f32[16,1024]{1,0:T(8,128)S(1)} %get-tuple-element.20.near_c, f32[16,1024]{1,0:T(8,128)S(1)} %get-tuple-element.21.near_s, f32[1,1024]{1,0:T(1,128)} %constant.85.clone.mid_c_hbm, f32[1,1024]{1,0:T(1,128)} %constant.86.clone.mid_s_hbm, ...), custom_call_target="tpu_custom_call" | custom-call | flops 1000000000 | bytes 4000000 | tf_op jit(solution)/shard_map/stage_two/pallas_call | solution.py:638
  36.9 0.0 copy-start
  36.9 0.0 copy-start.1
  36.9 3.4 %collective-permute-start.4 = (bf16[32,1536]{1,0:T(8,128)(2,1)S(1)}, bf16[32,1536]{1,0:T(8,128)(2,1)S(1)}, u32[]{:S(2)}, u32[]{:S(2)}) collective-permute-start(bf16[32,1536]{1,0:T(8,128)(2,1)S(1)} %stage_two.1), channel_id=1, source_target_pairs={{0,4},{1,5},{2,6},{3,7},{4,0},{5,1},{6,2},{7,3},{8,12},{9,13},{10,... | collective-permute-start | bytes 294920 | tf_op jit(solution)/shard_map/ppermute | solution.py:499
  40.3 2.1 %collective-permute-start = (bf16[32,1536]{1,0:T(8,128)(2,1)S(1)}, bf16[32,1536]{1,0:T(8,128)(2,1)S(1)}, u32[]{:S(2)}, u32[]{:S(2)}) collective-permute-start(bf16[32,1536]{1,0:T(8,128)(2,1)S(1)} %stage_two.1), channel_id=1, source_target_pairs={{0,8},{1,9},{2,10},{3,11},{4,12},{5,13},{6,14},{7,15},{8,0},{9,1},... | collective-permute-start | bytes 294920 | tf_op jit(solution)/shard_map/ppermute | solution.py:499
  42.5 1.4 %collective-permute-start.7 = (bf16[32,1536]{1,0:T(8,128)(2,1)S(1)}, bf16[32,1536]{1,0:T(8,128)(2,1)S(1)}, u32[]{:S(2)}, u32[]{:S(2)}) collective-permute-start(bf16[32,1536]{1,0:T(8,128)(2,1)S(1)} %stage_two.1), channel_id=1, source_target_pairs={{0,2},{1,3},{2,0},{3,1},{4,6},{5,7},{6,4},{7,5},{8,10},{9,11},{10,... | collective-permute-start | bytes 294920 | tf_op jit(solution)/shard_map/ppermute | solution.py:499
  43.8 0.1 slice.7.own
  43.9 1.6 %collective-permute-start.9 = (bf16[16,16,1024]{2,1,0:T(8,128)(2,1)S(1)}, bf16[16,16,1024]{2,1,0:T(8,128)(2,1)S(1)}, u32[]{:S(2)}, u32[]{:S(2)}) collective-permute-start(bf16[16,16,1024]{2,1,0:T(8,128)(2,1)S(1)} %slice.7.own), channel_id=1, source_target_pairs={{0,16},{16,0},{1,17},{17,1},{2,18},{18,2},{3,19},{19,3},{4,20},{20... | collective-permute-start | bytes 1572872 | tf_op jit(solution)/shard_map/ppermute | solution.py:554
  45.5 0.0 collective-permute-done.4
  45.5 3.3 %collective-permute-done = bf16[32,1536]{1,0:T(8,128)(2,1)S(1)} collective-permute-done((bf16[32,1536]{1,0:T(8,128)(2,1)S(1)}, bf16[32,1536]{1,0:T(8,128)(2,1)S(1)}, u32[]{:S(2)}, u32[]{:S(2)}) %collective-permute-start) | collective-permute-done | bytes 98336 | tf_op jit(solution)/shard_map/ppermute | solution.py:499
  48.8 1.6 %collective-permute-start.5 = (bf16[2,32,1536]{2,1,0:T(8,128)(2,1)S(1)}, bf16[2,32,1536]{2,1,0:T(8,128)(2,1)S(1)}, u32[]{:S(2)}, u32[]{:S(2)}) collective-permute-start(bf16[2,32,1536]{2,1,0:T(8,128)(2,1)S(1)} %pad_maximum_fusion.2), channel_id=1, source_target_pairs={{0,2},{1,3},{2,0},{3,1},{4,6},{5,7},{6,4},{7,5},{8,10},{9,11},{10,... | collective-permute-start | bytes 589832 | tf_op jit(solution)/shard_map/ppermute | solution.py:499
  50.3 0.0 collective-permute-start.1
  50.3 0.0 collective-permute-done.7
  50.3 0.1 pad_maximum_fusion.near
  50.4 0.1 collective-permute-start.8
  50.5 4.5 %collective-permute-done.1.far = bf16[32,1536]{1,0:T(8,128)(2,1)S(1)} collective-permute-done((bf16[32,1536]{1,0:T(8,128)(2,1)S(1)}, bf16[32,1536]{1,0:T(8,128)(2,1)S(1)}, u32[]{:S(2)}, u32[]{:S(2)}) %collective-permute-start.1) | collective-permute-done | bytes 98336 | tf_op jit(solution)/shard_map/ppermute | solution.py:499
  54.9 0.5 collective-permute-done.5.both
  55.5 0.1 collective-permute-start.6
  55.6 1.4 %collective-permute-start.2 = (bf16[32,1536]{1,0:T(8,128)(2,1)S(1)}, bf16[32,1536]{1,0:T(8,128)(2,1)S(1)}, u32[]{:S(2)}, u32[]{:S(2)}) collective-permute-start(bf16[32,1536]{1,0:T(8,128)(2,1)S(1)} %collective-permute-done.1.far), channel_id=1, source_target_pairs={{0,2},{1,3},{2,0},{3,1},{4,6},{5,7},{6,4},{7,5},{8,10},{9,11},{10,... | collective-permute-start | bytes 294920 | tf_op jit(solution)/shard_map/ppermute | solution.py:499
  56.9 3.8 %inverse_tables.1 = (bf16[512,1024]{1,0:T(8,128)(2,1)S(1)}, bf16[512,1024]{1,0:T(8,128)(2,1)S(1)}, f32[512,1024]{1,0:T(8,128)S(1)}, f32[512,1024]{1,0:T(8,128)S(...) custom-call(f32[16,512]{1,0:T(8,128)} %constant.69.clone.even_c, ...), custom_call_target="tpu_custom_call" | custom-call | flops 10000000 | bytes 20000000 | tf_op jit(solution)/shard_map/inverse_tables/pallas_call | solution.py:617
  60.7 0.1 collective-permute-done.2.last
  60.8 0.1 collective-permute-start.3
  60.9 0.0 collective-permute-done.9.other
  60.9 0.0 copy-done
  60.9 0.0 copy-done.1
  60.9 1.9 %choose.1.chosen = bf16[512,1024]{1,0:T(8,128)(2,1)S(1)} custom-call(s32[16]{0:T(128)S(1)} %copy-done, s32[16]{0:T(128)S(1)} %copy-done.1, bf16[16,16,1024]{2,1,0:T(8,128)(2,1)S(1)} %slice.7.own, bf16[16,16,1024]{2,1,0:T(8,128)(2,1)S(1)} %collective-permute-done.9.other, bf16[512,512]{1,0:T(8,128)(2,1)S(1)} %get-tuple-element.23.by_rows, ...), custom_call_target="tpu_custom_call" | custom-call | flops 1000000000 | bytes 4000000 | tf_op jit(solution)/shard_map/choose/pallas_call | solution.py:665
  62.8 0.0 collective-permute-done.8.theirs
  62.9 1.5 %early.1 = (bf16[1024,1024]{1,0:T(8,128)(2,1)S(1)}, f32[16,512]{1,0:T(8,128)S(1)}) custom-call(bf16[4,32,1536]{2,1,0:T(8,128)(2,1)S(1)} %pad_maximum_fusion.near, bf16[4,32,1536]{2,1,0:T(8,128)(2,1)S(1)} %collective-permute-done.8.theirs, bf16[2,32,1536]{2,1,0:T(8,128)(2,1)S(1)} %collective-permute-done.5.both, ...), custom_call_target="tpu_custom_call" | custom-call | flops 1000000000 | bytes 4000000 | tf_op jit(solution)/shard_map/early/pallas_call | solution.py:679
  64.3 0.0 collective-permute-done.6.theirs
  64.3 0.6 middle.1
  65.0 0.0 collective-permute-done.3.theirs
  65.0 3.3 %late.1 = (bf16[1,512,1024]{2,1,0:T(8,128)(2,1)}, bf16[1024,1024]{1,0:T(8,128)(2,1)S(1)}) custom-call(bf16[32,1536]{1,0:T(8,128)(2,1)S(1)} %collective-permute-done.2.last, bf16[32,1536]{1,0:T(8,128)(2,1)S(1)} %collective-permute-done.3.theirs, bf16[1024,1024]{1,0:T(8,128)(2,1)S(1)} %get-tuple-element.31.early, ...), custom_call_target="tpu_custom_call", output_to_operand_aliasing={{1}: (2, {})} | custom-call | tf_op jit(solution)/shard_map/late/pallas_call | solution.py:692
  (2 shorter events, 0.0 us)
Async XLA Ops:
  3.4 31.4 %all-to-all-start = ((bf16[16,16,2176]{2,1,0:T(8,128)(2,1)}), bf16[16,16,2176]{2,1,0:T(8,128)(2,1)S(1)}, u32[]{:S(2)}, u32[]{:S(2)}) async-start(bf16[16,16,2176]{2,1,0:T(8,128)(2,1)} %bitcast.2), calls=%async_computation | async-start | bytes 2228224 | tf_op jit(solution)/shard_map/all_to_all | solution.py:550
  36.9 24.0 %copy-start = (s32[16]{0:T(128)S(1)}, s32[16]{0:T(128)}, u32[]{:S(2)}) copy-start(s32[16]{0:T(128)} %order.1) | copy-start | bytes 196
  36.9 24.0 %copy-start.1 = (s32[16]{0:T(128)S(1)}, s32[16]{0:T(128)}, u32[]{:S(2)}) copy-start(s32[16]{0:T(128)} %cuts.1) | copy-start | bytes 196
  36.9 8.6 %collective-permute-start.4 = (bf16[32,1536]{1,0:T(8,128)(2,1)S(1)}, bf16[32,1536]{1,0:T(8,128)(2,1)S(1)}, u32[]{:S(2)}, u32[]{:S(2)}) collective-permute-start(bf16[32,1536]{1,0:T(8,128)(2,1)S(1)} %stage_two.1), channel_id=1, source_target_pairs={{0,4},{1,5},{2,6},{3,7},{4,0},{5,1},{6,2},{7,3},{8,12},{9,13},{10,... | collective-permute-start | bytes 294920 | tf_op jit(solution)/shard_map/ppermute | solution.py:499
  40.3 8.4 %collective-permute-start = (bf16[32,1536]{1,0:T(8,128)(2,1)S(1)}, bf16[32,1536]{1,0:T(8,128)(2,1)S(1)}, u32[]{:S(2)}, u32[]{:S(2)}) collective-permute-start(bf16[32,1536]{1,0:T(8,128)(2,1)S(1)} %stage_two.1), channel_id=1, source_target_pairs={{0,8},{1,9},{2,10},{3,11},{4,12},{5,13},{6,14},{7,15},{8,0},{9,1},... | collective-permute-start | bytes 294920 | tf_op jit(solution)/shard_map/ppermute | solution.py:499
  42.5 7.8 %collective-permute-start.7 = (bf16[32,1536]{1,0:T(8,128)(2,1)S(1)}, bf16[32,1536]{1,0:T(8,128)(2,1)S(1)}, u32[]{:S(2)}, u32[]{:S(2)}) collective-permute-start(bf16[32,1536]{1,0:T(8,128)(2,1)S(1)} %stage_two.1), channel_id=1, source_target_pairs={{0,2},{1,3},{2,0},{3,1},{4,6},{5,7},{6,4},{7,5},{8,10},{9,11},{10,... | collective-permute-start | bytes 294920 | tf_op jit(solution)/shard_map/ppermute | solution.py:499
  43.9 17.0 %collective-permute-start.9 = (bf16[16,16,1024]{2,1,0:T(8,128)(2,1)S(1)}, bf16[16,16,1024]{2,1,0:T(8,128)(2,1)S(1)}, u32[]{:S(2)}, u32[]{:S(2)}) collective-permute-start(bf16[16,16,1024]{2,1,0:T(8,128)(2,1)S(1)} %slice.7.own), channel_id=1, source_target_pairs={{0,16},{16,0},{1,17},{17,1},{2,18},{18,2},{3,19},{19,3},{4,20},{20... | collective-permute-start | bytes 1572872 | tf_op jit(solution)/shard_map/ppermute | solution.py:554
  48.8 6.7 %collective-permute-start.5 = (bf16[2,32,1536]{2,1,0:T(8,128)(2,1)S(1)}, bf16[2,32,1536]{2,1,0:T(8,128)(2,1)S(1)}, u32[]{:S(2)}, u32[]{:S(2)}) collective-permute-start(bf16[2,32,1536]{2,1,0:T(8,128)(2,1)S(1)} %pad_maximum_fusion.2), channel_id=1, source_target_pairs={{0,2},{1,3},{2,0},{3,1},{4,6},{5,7},{6,4},{7,5},{8,10},{9,11},{10,... | collective-permute-start | bytes 589832 | tf_op jit(solution)/shard_map/ppermute | solution.py:499
  50.3 4.6 %collective-permute-start.1 = (bf16[32,1536]{1,0:T(8,128)(2,1)S(1)}, bf16[32,1536]{1,0:T(8,128)(2,1)S(1)}, u32[]{:S(2)}, u32[]{:S(2)}) collective-permute-start(bf16[32,1536]{1,0:T(8,128)(2,1)S(1)} %collective-permute-done), channel_id=1, source_target_pairs={{0,4},{1,5},{2,6},{3,7},{4,0},{5,1},{6,2},{7,3},{8,12},{9,13},{10,... | collective-permute-start | bytes 294920 | tf_op jit(solution)/shard_map/ppermute | solution.py:499
  50.4 12.5 %collective-permute-start.8 = (bf16[4,32,1536]{2,1,0:T(8,128)(2,1)S(1)}, bf16[4,32,1536]{2,1,0:T(8,128)(2,1)S(1)}, u32[]{:S(2)}, u32[]{:S(2)}) collective-permute-start(bf16[4,32,1536]{2,1,0:T(8,128)(2,1)S(1)} %pad_maximum_fusion.near), channel_id=1, source_target_pairs={{0,1},{1,0},{2,3},{3,2},{4,5},{5,4},{6,7},{7,6},{8,9},{9,8},{10,11... | collective-permute-start | bytes 1179656 | tf_op jit(solution)/shard_map/ppermute | solution.py:499
  55.5 8.8 %collective-permute-start.6 = (bf16[3,32,1536]{2,1,0:T(8,128)(2,1)S(1)}, bf16[3,32,1536]{2,1,0:T(8,128)(2,1)S(1)}, u32[]{:S(2)}, u32[]{:S(2)}) collective-permute-start(bf16[3,32,1536]{2,1,0:T(8,128)(2,1)S(1)} %pad_maximum_fusion.1), channel_id=1, source_target_pairs={{0,1},{1,0},{2,3},{3,2},{4,5},{5,4},{6,7},{7,6},{8,9},{9,8},{10,11... | collective-permute-start | bytes 884744 | tf_op jit(solution)/shard_map/ppermute | solution.py:499
  55.6 5.2 %collective-permute-start.2 = (bf16[32,1536]{1,0:T(8,128)(2,1)S(1)}, bf16[32,1536]{1,0:T(8,128)(2,1)S(1)}, u32[]{:S(2)}, u32[]{:S(2)}) collective-permute-start(bf16[32,1536]{1,0:T(8,128)(2,1)S(1)} %collective-permute-done.1.far), channel_id=1, source_target_pairs={{0,2},{1,3},{2,0},{3,1},{4,6},{5,7},{6,4},{7,5},{8,10},{9,11},{10,... | collective-permute-start | bytes 294920 | tf_op jit(solution)/shard_map/ppermute | solution.py:499
  60.8 4.2 %collective-permute-start.3 = (bf16[32,1536]{1,0:T(8,128)(2,1)S(1)}, bf16[32,1536]{1,0:T(8,128)(2,1)S(1)}, u32[]{:S(2)}, u32[]{:S(2)}) collective-permute-start(bf16[32,1536]{1,0:T(8,128)(2,1)S(1)} %collective-permute-done.2.last), channel_id=1, source_target_pairs={{0,1},{1,0},{2,3},{3,2},{4,5},{5,4},{6,7},{7,6},{8,9},{9,8},{10,11... | collective-permute-start | bytes 294920 | tf_op jit(solution)/shard_map/ppermute | solution.py:499

commit v3 on v2

--- a/solution.py
+++ b/solution.py
@@ -151,7 +151,7 @@
 
 def forward_kernel(
     fore_c, fore_s, fore_rc, fore_rs, near_c, near_s, base_c, base_s,
-    forward_hbm, near_out_c, near_out_s, forward, sem,
+    forward, near_out_c, near_out_s,
 ):
     half_len = fore_c.shape[1]
     quarter = half_len // 2
@@ -169,10 +169,7 @@
         return turn(cos, sin, fore_rc[...], fore_rs[...])
 
     lax.fori_loop(0, forward.shape[1] // STEP, fore, (fore_c[...], fore_s[...]))
-    copy = pltpu.make_async_copy(forward, forward_hbm, sem)
-    copy.start()
     near_out_c[...], near_out_s[...] = turn(near_c[...], near_s[...], base_c[place], base_s[place])
-    copy.wait()
 
 
 def inverse_tables_kernel(
@@ -236,16 +233,14 @@
 
 
 def stage_two_kernel(
-    segs, cols, moved, near_c, near_s, mid_c_hbm, mid_s_hbm, forward_hbm, out,
-    mid_c, mid_s, forward, stacked, middle, product, sems,
+    segs, cols, moved, near_c, near_s, mid_c_hbm, mid_s_hbm, forward, out,
+    mid_c, mid_s, stacked, middle, product, sems,
 ):
     place, _ = position()
     _, half_len, _ = forward.shape
     second_len = 2 * half_len
     quarter = half_len // 2
-    pieces = [(forward_hbm.at[odd], forward.at[odd]) for odd in range(2)]
-    pieces += [(mid_c_hbm, mid_c), (mid_s_hbm, mid_s)]
-    copies = start_copies(pieces, sems)
+    copies = start_copies([(mid_c_hbm, mid_c), (mid_s_hbm, mid_s)], sems)
     sources, rows, _ = moved.shape
     tail = segs * cols
     all_rows = (segs + 1) * rows
@@ -295,7 +290,7 @@
             put(2 * twin + 1, real_two, imag_two)
         real, imag = piece(2 * tail)
         put(segs, real, imag)
-    for copy in copies[2:]:
+    for copy in copies:
         copy.wait()
     for part, turned in enumerate((middle[...] * mid_c[...], middle[...] * -mid_s[...])):
         at = slice(2 * all_rows + part * rows, 2 * all_rows + (part + 1) * rows)
@@ -309,7 +304,6 @@
     for odd in range(2):
         cos_at = slice(odd * half_len, odd * half_len + quarter)
         sin_at = slice(odd * half_len + quarter, (odd + 1) * half_len)
-        copies[odd].wait()
         product[:, odd * half_len : (odd + 1) * half_len] = matmul(stacked[odd], forward[odd])
 
         def parts(at, lower_at, cos_at=cos_at, sin_at=sin_at):
@@ -363,61 +357,66 @@
 
 
 def sort_tables(rows, rows_out, bins_out):
-    first_len, half_len = rows_out.shape[0], bins_out.shape[0]
-    per = first_len // 2
+    _, per, _ = rows_out.shape
     _, group = position()
-    deep = 128
 
     def one_hot(mask):
         return jnp.where(mask, 1.0, 0.0).astype(BF16)
 
-    def body(step, carry):
-        at = aligned(step * deep, deep)
-        row = packed_row_of(step * deep + lax.broadcasted_iota(jnp.int32, (deep, first_len), 0), first_len, rows)
+    at = lax.broadcasted_iota(jnp.int32, (per, per), 0)
+    lane = lax.broadcasted_iota(jnp.int32, (per, per), 1)
+    for turned in range(2):
+        row = packed_row_of(at, turned, 2 * per, rows)
         share = (row // rows) % 2
-        column = (row // (2 * rows)) * rows + row % rows + jnp.where(share == group, 0, per)
-        rows_out[at, :] = one_hot(column == lax.broadcasted_iota(jnp.int32, (deep, first_len), 1))
-        return carry
-
-    lax.fori_loop(0, first_len // deep, body, 0)
-
-    def bins(step, carry):
-        row = step * deep + lax.broadcasted_iota(jnp.int32, (deep, half_len), 0)
-        lane = lax.broadcasted_iota(jnp.int32, (deep, half_len), 1)
-        bins_out[aligned(step * deep, deep), :] = one_hot(row == bin_of(lane, half_len))
-        return carry
-
-    lax.fori_loop(0, half_len // deep, bins, 0)
-
-
-def bin_of(lane, half_len):
-    return jnp.where(lane < half_len // 2, 2 * lane, 2 * lane - half_len + 1)
-
-
-def packed_row_of(at, first_len, rows):
-    per = first_len // 2
-    packed = (at % per) // rows * rows + 2 * (at % (rows // 2)) + at // per
-    turned = jnp.where(packed == 0, first_len // 2, first_len - packed)
-    return jnp.where(at % rows >= rows // 2, turned, packed)
+        source = row // (2 * rows) - turned * (per // (2 * rows))
+        column = source * rows + row % rows + jnp.where(share == group, 0, per // 2)
+        rows_out[turned] = one_hot(column == lane)
+    wide = bins_out.shape[0]
+    at = lax.broadcasted_iota(jnp.int32, (wide, wide), 0)
+    lane = lax.broadcasted_iota(jnp.int32, (wide, wide), 1)
+    bins_out[...] = one_hot(at == jnp.where(lane < wide // 2, 2 * lane, 2 * lane - wide + 1))
+
+
+def packed_row_of(at, turned, first_len, rows):
+    half = first_len // 4
+    packed = at % half // (rows // 2) * rows + 2 * (at % (rows // 2)) + at // half
+    if not turned:
+        return packed
+    return jnp.where(packed == 0, first_len // 2, first_len - packed)
 
 
 def choose_kernel(order, cuts, own, other, by_rows, by_bins, out, held):
     place, _ = position()
-    rows, sources = own.shape[1], own.shape[0]
+    sources, rows, _ = own.shape
     per = sources * rows
-    first_len, half_len = 2 * per, own.shape[2] // 2
+    half_len = own.shape[2] // 2
     for source in range(sources):
-        held[source * rows : (source + 1) * rows, :] = own[source]
-        held[per + source * rows : per + (source + 1) * rows, :] = other[source]
-    picked = matmul(by_rows[...], held[...]).astype(BF16)
-    at = lax.broadcasted_iota(jnp.int32, (first_len, 128), 0)
-    room = cuts[order[place]] - packed_row_of(at, first_len, rows)
+        turned, at = source // (sources // 2), source % (sources // 2) * rows
+        held[turned, at : at + rows, :] = own[source]
+        held[turned, per // 2 + at : per // 2 + at + rows, :] = other[source]
+    cut = cuts[order[place]]
+    moved, room = [], []
+    for turned in range(2):
+        moved.append(matmul(by_rows[turned], held[turned]).reshape(per // (rows // 2), rows // 2, 2 * half_len))
+        at = lax.broadcasted_iota(jnp.int32, (per, 128), 0)
+        room.append((cut - packed_row_of(at, turned, 2 * per, rows)).reshape(per // (rows // 2), rows // 2, 128))
+    picked = jnp.concatenate(moved, 1).reshape(2 * per, 2 * half_len).astype(BF16)
+    room = jnp.concatenate(room, 1).reshape(2 * per, 128)
+    wide = by_bins.shape[0]
     for part in range(2):
-        moved = matmul(picked[:, part * half_len : (part + 1) * half_len], by_bins[...])
-        for lane in range(0, half_len, 128):
-            bins = bin_of(lane + lax.broadcasted_iota(jnp.int32, (1, 128), 1), half_len)
-            kept = jnp.where(first_len * bins < room, moved[:, lane : lane + 128], 0.0)
-            out[:, part * half_len + lane : part * half_len + lane + 128] = kept.astype(BF16)
+        for block in range(half_len // wide):
+            lane = part * half_len + block * wide
+            sorted_bins = matmul(picked[:, lane : lane + wide], by_bins[...])
+            for odd in range(2):
+                for at in range(0, wide // 2, 128):
+                    first = block * (wide // 2) + at
+                    bins = 2 * (first + lax.broadcasted_iota(jnp.int32, (1, 128), 1)) + odd
+                    from_lane = odd * (wide // 2) + at
+                    kept = jnp.where(
+                        2 * per * bins < room, sorted_bins[:, from_lane : from_lane + 128], 0.0
+                    )
+                    to = part * half_len + odd * (half_len // 2) + first
+                    out[:, to : to + 128] = kept.astype(BF16)
 
 
 def filter_blocks(offsets, blocks, chosen, tables, norm, filtered, lifted):
@@ -477,21 +476,35 @@
 
 
 def late_kernel(last, theirs, early, early_norm, chosen, *refs):
-    tables, (cols_table, out, lifted, filtered) = refs[:4], refs[4:]
+    tables, (cols_table, out, lifted, filtered, result, sems) = refs[:4], refs[4:]
     norm = filter_blocks(LATE, [last, theirs], chosen, tables, early_norm[...], filtered, lifted)
     scale = lax.rsqrt(jnp.sum(norm, keepdims=True))
     first_len = chosen.shape[0]
     per = first_len // 2
     wide = 256
-    for lane in range(0, lifted.shape[1], wide):
-        at = slice(lane, lane + wide)
-        even = matmul(cols_table[:, :first_len], lifted[:first_len, at])
-        odd = matmul(cols_table[:, first_len:], lifted[first_len:, at])
+    lanes = [slice(lane, lane + wide) for lane in range(0, lifted.shape[1], wide)]
+
+    def products(at):
+        return (
+            matmul(cols_table[:, :first_len], lifted[:first_len, at]),
+            matmul(cols_table[:, first_len:], lifted[first_len:, at]),
+        )
+
+    copies = []
+    following = products(lanes[0])
+    for block, at in enumerate(lanes):
+        even, odd = following
+        if block + 1 < len(lanes):
+            following = products(lanes[block + 1])
         for upper in range(2):
             total = even - odd if upper else even + odd
             power = total[:per] * total[:per] + total[per:] * total[per:]
             size = power * lax.rsqrt(jnp.maximum(power, 1e-37))
-            out[0, upper * per : (upper + 1) * per, at] = (size * scale).astype(BF16)
+            result[upper * per : (upper + 1) * per, at] = (size * scale).astype(BF16)
+        copies.append(pltpu.make_async_copy(result.at[:, at], out.at[0, :, at], sems.at[block]))
+        copies[-1].start()
+    for copy in copies:
+        copy.wait()
 
 
 def swap_with(array, flip):
@@ -575,12 +588,11 @@
     forward, near_c, near_s = pl.pallas_call(
         forward_kernel,
         out_shape=[
-            pltpu.HBM((2, half_len, half_len), BF16),
+            pltpu.VMEM((2, half_len, half_len), BF16),
             *[pltpu.VMEM((rows, second_len), F32)] * 2,
         ],
         in_specs=[whole()] * len(fore),
-        out_specs=[outside()] + [whole()] * 2,
-        scratch_shapes=[vmem((2, half_len, half_len)), pltpu.SemaphoreType.DMA],
+        out_specs=[whole()] * 3,
         compiler_params=params(16),
         cost_estimate=pl.CostEstimate(flops=10**7, bytes_accessed=2 * 10**7, transcendentals=0),
         name="forward_tables",
@@ -602,8 +614,8 @@
         ((first_len, second_len), F32),
         ((first_len, second_len), F32),
         ((first_len, 2 * first_len), BF16),
-        ((first_len, first_len), BF16),
-        ((half_len, half_len), BF16),
+        ((2, first_len // 2, first_len // 2), BF16),
+        ((256, 256), BF16),
     ]
     inverse_tables = pl.pallas_call(
         inverse_tables_kernel,
@@ -621,21 +633,20 @@
     stage_two = pl.pallas_call(
         functools.partial(stage_two_kernel, segs, cols),
         out_shape=jax.ShapeDtypeStruct((2 * rows, 3 * half_len), BF16),
-        in_specs=[whole()] * 3 + [outside()] * 3,
+        in_specs=[whole()] * 3 + [outside()] * 2 + [whole()],
         out_specs=whole(),
         scratch_shapes=[
             *[vmem((1, second_len), F32)] * 2,
-            vmem(forward.shape),
             vmem((2, all_rows, half_len)),
             vmem((rows, second_len), F32),
             vmem((all_rows, second_len), F32),
-            pltpu.SemaphoreType.DMA((4,)),
+            pltpu.SemaphoreType.DMA((2,)),
         ],
         compiler_params=params(24),
         cost_estimate=pl.CostEstimate(flops=10**9, bytes_accessed=4 * 10**6, transcendentals=0),
         name="stage_two",
     )
-    block = stage_two(moved, *in_vmem(near_c, near_s), *in_hbm(mid_c, mid_s, forward))
+    block = stage_two(moved, *in_vmem(near_c, near_s), *in_hbm(mid_c, mid_s), *in_vmem(forward))
 
     two = swap_with(block, 8)
     one = swap_with(block, 4)
@@ -655,7 +666,7 @@
             grid=(),
             in_specs=[whole()] * 4,
             out_specs=whole(),
-            scratch_shapes=[vmem((first_len, 2 * half_len))],
+            scratch_shapes=[vmem((2, first_len // 2, 2 * half_len))],
         ),
         out_shape=jax.ShapeDtypeStruct((first_len, 2 * half_len), BF16),
         compiler_params=params(16),
@@ -691,10 +702,14 @@
     lifted, norm = middle(more, *in_vmem(lifted, norm), chosen, *tables)
     result, _ = pl.pallas_call(
         late_kernel,
-        out_shape=[jax.ShapeDtypeStruct((1, first_len, second_len), BF16), pltpu.VMEM(*spread)],
+        out_shape=[pltpu.HBM((1, first_len, second_len), BF16), pltpu.VMEM(*spread)],
         in_specs=[whole()] * 10,
-        out_specs=[whole()] * 2,
-        scratch_shapes=[vmem((len(LATE) * 2 * rows, 2 * half_len))],
+        out_specs=[outside(), whole()],
+        scratch_shapes=[
+            vmem((len(LATE) * 2 * rows, 2 * half_len)),
+            vmem((first_len, second_len)),
+            pltpu.SemaphoreType.DMA((second_len // 256,)),
+        ],
         input_output_aliases={2: 1},
         compiler_params=params(16),
         name="late",

time: 68.6 us -> 66.9 us (0.975)
  Pallas kernels: 18.8 us -> 15.6 us
  waiting for transfers between devices: 30 us -> 31.7 us
    pallas_call x3, Pallas kernels: 7.66 us -> 5.67 us  [the longest x1 2.97 us: tiled_local(): pl.pallas_call(late_kernel, out_shape=[pltpu.HBM((1, first_len, second_le...]
    all_to_all x1, waiting for transfers between devices: 21.7 us -> 22.6 us  [tiled_local(): lax.all_to_all(sent.reshape(dev_count, rows, lanes + 2 * half_len), 'tmpl...]
  transfers between devices with their start and end apart: 11 -> 11, of which waited for: 5 -> 5; matrix products, arithmetic and copies ran while one was open for 0% -> 0% of each run, Pallas kernels for 15% -> 12%
where the time goes in v3:
time: 66.9 us; the launch traced here: 66.6 us
  waiting for transfers between devices  31.7 us (47%)
  starting transfers between devices  19 us (28%)
  Pallas kernels  15.6 us (23%)
    all_to_all x1, waiting for transfers between devices, tiled_local(): lax.all_to_all(sent.reshape(dev_count, rows, lanes + 2 * half_len), 'tmpl...  22.6 us
    ppermute x9, starting transfers between devices, swap_with(): return lax.ppermute(array, 'tmpl', pairs)  10 us
    ppermute x9, waiting for transfers between devices, swap_with(): return lax.ppermute(array, 'tmpl', pairs)  9.06 us
    all_to_all x1, starting transfers between devices, tiled_local(): lax.all_to_all(sent.reshape(dev_count, rows, lanes + 2 * half_len), 'tmpl...  7.43 us
    pallas_call x1, Pallas kernels, tiled_local(): pl.pallas_call(functools.partial(stage_one_kernel, turns_of_eight), in_sp...  3.38 us
    pallas_call x1, Pallas kernels, tiled_local(): inverse_tables(*in_hbm(*back))  3.07 us
    pallas_call x1, Pallas kernels, tiled_local(): pl.pallas_call(late_kernel, out_shape=[pltpu.HBM((1, first_len, second_le...  2.97 us
    ppermute x1, starting transfers between devices, tiled_local(): other = lax.ppermute(own, 'grp', [(0, 1), (1, 0)])  1.56 us
  transfers between devices with their start and end apart: 11, of which 5 were waited for; matrix products, arithmetic and copies ran while one was open for 0% of the time, Pallas kernels for 12%

profile of v3, /device:TPU:0, one launch (start us, length us, event | category | flops | bytes accessed | tf_op | source)
XLA Modules:
  0.0 66.6 jit_solution(5650519864159761503)
XLA Ops:
  0.0 3.4 %stage_one.1 = bf16[256,2176]{1,0:T(8,128)(2,1)} custom-call(s32[16]{0:T(128)} %order.1, f32[8,64,512]{2,1,0:T(8,128)} %bitcast.10, f32[64,512]{1,0:T(8,128)} %bitcast.15, f32[16,2,512]{2,1,0:T(2,128)} %constant.58.clone.spin_hbm, f32[2,8,512]{2,1,0:T(8,128)} %constant.59.clone.win_hbm, bf16[2,256,256]{2,1,0:T(8,128)(2,1)} %constant.60.clone.wave_hbm, ...), custom_call_target="tpu_custom_call" | custom-call | tf_op jit(solution)/shard_map/stage_one/pallas_call | solution.py:539
  3.4 7.4 %all-to-all-start = ((bf16[16,16,2176]{2,1,0:T(8,128)(2,1)}), bf16[16,16,2176]{2,1,0:T(8,128)(2,1)S(1)}, u32[]{:S(2)}, u32[]{:S(2)}) async-start(bf16[16,16,2176]{2,1,0:T(8,128)(2,1)} %bitcast.2), calls=%async_computation | async-start | bytes 2228224 | tf_op jit(solution)/shard_map/all_to_all | solution.py:563
  10.8 1.3 %forward_tables.1 = (bf16[2,512,512]{2,1,0:T(8,128)(2,1)S(1)}, f32[16,1024]{1,0:T(8,128)S(1)}, f32[16,1024]{1,0:T(8,128)S(1)}) custom-call(f32[16,512]{1,0:T(8,128)} %constant.61.clone.fore_c, f32[16,512]{1,0:T(8,128)} %constant.62.clone.fore_s, f32[1,512]{1,0:T(1,128)} %constant.63.clone.fore_rc, f32[1,512]{1,0:T(1,128)} %constant.64.clone.fore_rs, ...), custom_call_target="tpu_custom_call" | custom-call | flops 10000000 | bytes 20000000 | tf_op jit(solution)/shard_map/forward_tables/pallas_call | solution.py:588
  12.1 22.6 %all-to-all-done.moved = bf16[16,16,2176]{2,1,0:T(8,128)(2,1)S(1)} async-done(((bf16[16,16,2176]{2,1,0:T(8,128)(2,1)}), bf16[16,16,2176]{2,1,0:T(8,128)(2,1)S(1)}, u32[]{:S(2)}, u32[]{:S(2)}) %all-to-all-start) | async-done | bytes 1114144 | tf_op jit(solution)/shard_map/all_to_all | solution.py:563
  34.8 1.4 %stage_two.1 = bf16[32,1536]{1,0:T(8,128)(2,1)S(1)} custom-call(bf16[16,16,2176]{2,1,0:T(8,128)(2,1)S(1)} %all-to-all-done.moved, f32[16,1024]{1,0:T(8,128)S(1)} %get-tuple-element.20.near_c, f32[16,1024]{1,0:T(8,128)S(1)} %get-tuple-element.21.near_s, f32[1,1024]{1,0:T(1,128)} %constant.85.clone.mid_c_hbm, f32[1,1024]{1,0:T(1,128)} %constant.86.clone.mid_s_hbm, ...), custom_call_target="tpu_custom_call" | custom-call | flops 1000000000 | bytes 4000000 | tf_op jit(solution)/shard_map/stage_two/pallas_call | solution.py:649
  36.2 0.0 copy-start
  36.2 0.0 copy-start.1
  36.2 3.4 %collective-permute-start.4 = (bf16[32,1536]{1,0:T(8,128)(2,1)S(1)}, bf16[32,1536]{1,0:T(8,128)(2,1)S(1)}, u32[]{:S(2)}, u32[]{:S(2)}) collective-permute-start(bf16[32,1536]{1,0:T(8,128)(2,1)S(1)} %stage_two.1), channel_id=1, source_target_pairs={{0,4},{1,5},{2,6},{3,7},{4,0},{5,1},{6,2},{7,3},{8,12},{9,13},{10,... | collective-permute-start | bytes 294920 | tf_op jit(solution)/shard_map/ppermute | solution.py:512
  39.6 2.1 %collective-permute-start = (bf16[32,1536]{1,0:T(8,128)(2,1)S(1)}, bf16[32,1536]{1,0:T(8,128)(2,1)S(1)}, u32[]{:S(2)}, u32[]{:S(2)}) collective-permute-start(bf16[32,1536]{1,0:T(8,128)(2,1)S(1)} %stage_two.1), channel_id=1, source_target_pairs={{0,8},{1,9},{2,10},{3,11},{4,12},{5,13},{6,14},{7,15},{8,0},{9,1},... | collective-permute-start | bytes 294920 | tf_op jit(solution)/shard_map/ppermute | solution.py:512
  41.8 1.4 %collective-permute-start.7 = (bf16[32,1536]{1,0:T(8,128)(2,1)S(1)}, bf16[32,1536]{1,0:T(8,128)(2,1)S(1)}, u32[]{:S(2)}, u32[]{:S(2)}) collective-permute-start(bf16[32,1536]{1,0:T(8,128)(2,1)S(1)} %stage_two.1), channel_id=1, source_target_pairs={{0,2},{1,3},{2,0},{3,1},{4,6},{5,7},{6,4},{7,5},{8,10},{9,11},{10,... | collective-permute-start | bytes 294920 | tf_op jit(solution)/shard_map/ppermute | solution.py:512
  43.1 0.1 slice.7.own
  43.2 1.6 %collective-permute-start.9 = (bf16[16,16,1024]{2,1,0:T(8,128)(2,1)S(1)}, bf16[16,16,1024]{2,1,0:T(8,128)(2,1)S(1)}, u32[]{:S(2)}, u32[]{:S(2)}) collective-permute-start(bf16[16,16,1024]{2,1,0:T(8,128)(2,1)S(1)} %slice.7.own), channel_id=1, source_target_pairs={{0,16},{16,0},{1,17},{17,1},{2,18},{18,2},{3,19},{19,3},{4,20},{20... | collective-permute-start | bytes 1572872 | tf_op jit(solution)/shard_map/ppermute | solution.py:567
  44.7 0.0 collective-permute-done.4
  44.7 3.3 %collective-permute-done = bf16[32,1536]{1,0:T(8,128)(2,1)S(1)} collective-permute-done((bf16[32,1536]{1,0:T(8,128)(2,1)S(1)}, bf16[32,1536]{1,0:T(8,128)(2,1)S(1)}, u32[]{:S(2)}, u32[]{:S(2)}) %collective-permute-start) | collective-permute-done | bytes 98336 | tf_op jit(solution)/shard_map/ppermute | solution.py:512
  48.0 1.6 %collective-permute-start.5 = (bf16[2,32,1536]{2,1,0:T(8,128)(2,1)S(1)}, bf16[2,32,1536]{2,1,0:T(8,128)(2,1)S(1)}, u32[]{:S(2)}, u32[]{:S(2)}) collective-permute-start(bf16[2,32,1536]{2,1,0:T(8,128)(2,1)S(1)} %pad_maximum_fusion.2), channel_id=1, source_target_pairs={{0,2},{1,3},{2,0},{3,1},{4,6},{5,7},{6,4},{7,5},{8,10},{9,11},{10,... | collective-permute-start | bytes 589832 | tf_op jit(solution)/shard_map/ppermute | solution.py:512
  49.6 0.0 collective-permute-start.1
  49.6 0.0 collective-permute-done.7
  49.6 0.1 pad_maximum_fusion.near
  49.7 0.1 collective-permute-start.8
  49.7 4.5 %collective-permute-done.1.far = bf16[32,1536]{1,0:T(8,128)(2,1)S(1)} collective-permute-done((bf16[32,1536]{1,0:T(8,128)(2,1)S(1)}, bf16[32,1536]{1,0:T(8,128)(2,1)S(1)}, u32[]{:S(2)}, u32[]{:S(2)}) %collective-permute-start.1) | collective-permute-done | bytes 98336 | tf_op jit(solution)/shard_map/ppermute | solution.py:512
  54.2 0.5 collective-permute-done.5.both
  54.8 0.1 collective-permute-start.6
  54.9 1.4 %collective-permute-start.2 = (bf16[32,1536]{1,0:T(8,128)(2,1)S(1)}, bf16[32,1536]{1,0:T(8,128)(2,1)S(1)}, u32[]{:S(2)}, u32[]{:S(2)}) collective-permute-start(bf16[32,1536]{1,0:T(8,128)(2,1)S(1)} %collective-permute-done.1.far), channel_id=1, source_target_pairs={{0,2},{1,3},{2,0},{3,1},{4,6},{5,7},{6,4},{7,5},{8,10},{9,11},{10,... | collective-permute-start | bytes 294920 | tf_op jit(solution)/shard_map/ppermute | solution.py:512
  56.2 3.1 %inverse_tables.1 = (bf16[512,1024]{1,0:T(8,128)(2,1)S(1)}, bf16[512,1024]{1,0:T(8,128)(2,1)S(1)}, f32[512,1024]{1,0:T(8,128)S(1)}, f32[512,1024]{1,0:T(8,128)S(...) custom-call(f32[16,512]{1,0:T(8,128)} %constant.69.clone.even_c, ...), custom_call_target="tpu_custom_call" | custom-call | flops 10000000 | bytes 20000000 | tf_op jit(solution)/shard_map/inverse_tables/pallas_call | solution.py:629
  59.3 0.8 %collective-permute-done.2.last = bf16[32,1536]{1,0:T(8,128)(2,1)S(1)} collective-permute-done((bf16[32,1536]{1,0:T(8,128)(2,1)S(1)}, bf16[32,1536]{1,0:T(8,128)(2,1)S(1)}, u32[]{:S(2)}, u32[]{:S(2)}) %collective-permute-start.2) | collective-permute-done | bytes 98336 | tf_op jit(solution)/shard_map/ppermute | solution.py:512
  60.0 0.0 collective-permute-start.3
  60.1 0.0 collective-permute-done.9.other
  60.1 0.0 copy-done
  60.1 0.0 copy-done.1
  60.1 1.4 %choose.1.chosen = bf16[512,1024]{1,0:T(8,128)(2,1)S(1)} custom-call(s32[16]{0:T(128)S(1)} %copy-done, s32[16]{0:T(128)S(1)} %copy-done.1, bf16[16,16,1024]{2,1,0:T(8,128)(2,1)S(1)} %slice.7.own, bf16[16,16,1024]{2,1,0:T(8,128)(2,1)S(1)} %collective-permute-done.9.other, bf16[2,256,256]{2,1,0:T(8,128)(2,1)S(1)} %get-tuple-element.23.by_rows, ...), custom_call_target="tpu_custom_call" | custom-call | flops 1000000000 | bytes 4000000 | tf_op jit(solution)/shard_map/choose/pallas_call | solution.py:676
  61.4 0.0 collective-permute-done.8.theirs
  61.4 1.5 %early.1 = (bf16[1024,1024]{1,0:T(8,128)(2,1)S(1)}, f32[16,512]{1,0:T(8,128)S(1)}) custom-call(bf16[4,32,1536]{2,1,0:T(8,128)(2,1)S(1)} %pad_maximum_fusion.near, bf16[4,32,1536]{2,1,0:T(8,128)(2,1)S(1)} %collective-permute-done.8.theirs, bf16[2,32,1536]{2,1,0:T(8,128)(2,1)S(1)} %collective-permute-done.5.both, ...), custom_call_target="tpu_custom_call" | custom-call | flops 1000000000 | bytes 4000000 | tf_op jit(solution)/shard_map/early/pallas_call | solution.py:690
  62.9 0.0 collective-permute-done.6.theirs
  62.9 0.6 middle.1
  63.6 0.0 collective-permute-done.3.theirs
  63.6 3.0 %late.1 = (bf16[1,512,1024]{2,1,0:T(8,128)(2,1)}, bf16[1024,1024]{1,0:T(8,128)(2,1)S(1)}) custom-call(bf16[32,1536]{1,0:T(8,128)(2,1)S(1)} %collective-permute-done.2.last, bf16[32,1536]{1,0:T(8,128)(2,1)S(1)} %collective-permute-done.3.theirs, bf16[1024,1024]{1,0:T(8,128)(2,1)S(1)} %get-tuple-element.31.early, ...), custom_call_target="tpu_custom_call", output_to_operand_aliasing={{1}: (2, {})} | custom-call | tf_op jit(solution)/shard_map/late/pallas_call | solution.py:703
  (2 shorter events, 0.0 us)
Async XLA Ops:
  3.4 31.4 %all-to-all-start = ((bf16[16,16,2176]{2,1,0:T(8,128)(2,1)}), bf16[16,16,2176]{2,1,0:T(8,128)(2,1)S(1)}, u32[]{:S(2)}, u32[]{:S(2)}) async-start(bf16[16,16,2176]{2,1,0:T(8,128)(2,1)} %bitcast.2), calls=%async_computation | async-start | bytes 2228224 | tf_op jit(solution)/shard_map/all_to_all | solution.py:563
  36.2 23.9 %copy-start = (s32[16]{0:T(128)S(1)}, s32[16]{0:T(128)}, u32[]{:S(2)}) copy-start(s32[16]{0:T(128)} %order.1) | copy-start | bytes 196
  36.2 23.9 %copy-start.1 = (s32[16]{0:T(128)S(1)}, s32[16]{0:T(128)}, u32[]{:S(2)}) copy-start(s32[16]{0:T(128)} %cuts.1) | copy-start | bytes 196
  36.2 8.6 %collective-permute-start.4 = (bf16[32,1536]{1,0:T(8,128)(2,1)S(1)}, bf16[32,1536]{1,0:T(8,128)(2,1)S(1)}, u32[]{:S(2)}, u32[]{:S(2)}) collective-permute-start(bf16[32,1536]{1,0:T(8,128)(2,1)S(1)} %stage_two.1), channel_id=1, source_target_pairs={{0,4},{1,5},{2,6},{3,7},{4,0},{5,1},{6,2},{7,3},{8,12},{9,13},{10,... | collective-permute-start | bytes 294920 | tf_op jit(solution)/shard_map/ppermute | solution.py:512
  39.6 8.4 %collective-permute-start = (bf16[32,1536]{1,0:T(8,128)(2,1)S(1)}, bf16[32,1536]{1,0:T(8,128)(2,1)S(1)}, u32[]{:S(2)}, u32[]{:S(2)}) collective-permute-start(bf16[32,1536]{1,0:T(8,128)(2,1)S(1)} %stage_two.1), channel_id=1, source_target_pairs={{0,8},{1,9},{2,10},{3,11},{4,12},{5,13},{6,14},{7,15},{8,0},{9,1},... | collective-permute-start | bytes 294920 | tf_op jit(solution)/shard_map/ppermute | solution.py:512
  41.8 7.8 %collective-permute-start.7 = (bf16[32,1536]{1,0:T(8,128)(2,1)S(1)}, bf16[32,1536]{1,0:T(8,128)(2,1)S(1)}, u32[]{:S(2)}, u32[]{:S(2)}) collective-permute-start(bf16[32,1536]{1,0:T(8,128)(2,1)S(1)} %stage_two.1), channel_id=1, source_target_pairs={{0,2},{1,3},{2,0},{3,1},{4,6},{5,7},{6,4},{7,5},{8,10},{9,11},{10,... | collective-permute-start | bytes 294920 | tf_op jit(solution)/shard_map/ppermute | solution.py:512
  43.2 16.9 %collective-permute-start.9 = (bf16[16,16,1024]{2,1,0:T(8,128)(2,1)S(1)}, bf16[16,16,1024]{2,1,0:T(8,128)(2,1)S(1)}, u32[]{:S(2)}, u32[]{:S(2)}) collective-permute-start(bf16[16,16,1024]{2,1,0:T(8,128)(2,1)S(1)} %slice.7.own), channel_id=1, source_target_pairs={{0,16},{16,0},{1,17},{17,1},{2,18},{18,2},{3,19},{19,3},{4,20},{20... | collective-permute-start | bytes 1572872 | tf_op jit(solution)/shard_map/ppermute | solution.py:567
  48.0 6.7 %collective-permute-start.5 = (bf16[2,32,1536]{2,1,0:T(8,128)(2,1)S(1)}, bf16[2,32,1536]{2,1,0:T(8,128)(2,1)S(1)}, u32[]{:S(2)}, u32[]{:S(2)}) collective-permute-start(bf16[2,32,1536]{2,1,0:T(8,128)(2,1)S(1)} %pad_maximum_fusion.2), channel_id=1, source_target_pairs={{0,2},{1,3},{2,0},{3,1},{4,6},{5,7},{6,4},{7,5},{8,10},{9,11},{10,... | collective-permute-start | bytes 589832 | tf_op jit(solution)/shard_map/ppermute | solution.py:512
  49.6 4.6 %collective-permute-start.1 = (bf16[32,1536]{1,0:T(8,128)(2,1)S(1)}, bf16[32,1536]{1,0:T(8,128)(2,1)S(1)}, u32[]{:S(2)}, u32[]{:S(2)}) collective-permute-start(bf16[32,1536]{1,0:T(8,128)(2,1)S(1)} %collective-permute-done), channel_id=1, source_target_pairs={{0,4},{1,5},{2,6},{3,7},{4,0},{5,1},{6,2},{7,3},{8,12},{9,13},{10,... | collective-permute-start | bytes 294920 | tf_op jit(solution)/shard_map/ppermute | solution.py:512
  49.7 11.8 %collective-permute-start.8 = (bf16[4,32,1536]{2,1,0:T(8,128)(2,1)S(1)}, bf16[4,32,1536]{2,1,0:T(8,128)(2,1)S(1)}, u32[]{:S(2)}, u32[]{:S(2)}) collective-permute-start(bf16[4,32,1536]{2,1,0:T(8,128)(2,1)S(1)} %pad_maximum_fusion.near), channel_id=1, source_target_pairs={{0,1},{1,0},{2,3},{3,2},{4,5},{5,4},{6,7},{7,6},{8,9},{9,8},{10,11... | collective-permute-start | bytes 1179656 | tf_op jit(solution)/shard_map/ppermute | solution.py:512
  54.8 8.2 %collective-permute-start.6 = (bf16[3,32,1536]{2,1,0:T(8,128)(2,1)S(1)}, bf16[3,32,1536]{2,1,0:T(8,128)(2,1)S(1)}, u32[]{:S(2)}, u32[]{:S(2)}) collective-permute-start(bf16[3,32,1536]{2,1,0:T(8,128)(2,1)S(1)} %pad_maximum_fusion.1), channel_id=1, source_target_pairs={{0,1},{1,0},{2,3},{3,2},{4,5},{5,4},{6,7},{7,6},{8,9},{9,8},{10,11... | collective-permute-start | bytes 884744 | tf_op jit(solution)/shard_map/ppermute | solution.py:512
  54.9 5.2 %collective-permute-start.2 = (bf16[32,1536]{1,0:T(8,128)(2,1)S(1)}, bf16[32,1536]{1,0:T(8,128)(2,1)S(1)}, u32[]{:S(2)}, u32[]{:S(2)}) collective-permute-start(bf16[32,1536]{1,0:T(8,128)(2,1)S(1)} %collective-permute-done.1.far), channel_id=1, source_target_pairs={{0,2},{1,3},{2,0},{3,1},{4,6},{5,7},{6,4},{7,5},{8,10},{9,11},{10,... | collective-permute-start | bytes 294920 | tf_op jit(solution)/shard_map/ppermute | solution.py:512
  60.0 3.5 %collective-permute-start.3 = (bf16[32,1536]{1,0:T(8,128)(2,1)S(1)}, bf16[32,1536]{1,0:T(8,128)(2,1)S(1)}, u32[]{:S(2)}, u32[]{:S(2)}) collective-permute-start(bf16[32,1536]{1,0:T(8,128)(2,1)S(1)} %collective-permute-done.2.last), channel_id=1, source_target_pairs={{0,1},{1,0},{2,3},{3,2},{4,5},{5,4},{6,7},{7,6},{8,9},{9,8},{10,11... | collective-permute-start | bytes 294920 | tf_op jit(solution)/shard_map/ppermute | solution.py:512

commit v4 on v3

--- a/solution.py
+++ b/solution.py
@@ -13,8 +13,8 @@
 F32 = jnp.float32
 STEP = 16
 PIECE = 128
-EARLY = (0, 2, 4, 8, 1, 3, 5, 9, 6, 10, 12)
-MIDDLE = (7, 11, 13)
+EARLY = (0, 2, 4, 8, 1, 3, 5, 9)
+MIDDLE = (6, 10, 12, 7, 11, 13)
 LATE = (14, 15)
 
 
@@ -82,7 +82,7 @@
 
 def stage_one_kernel(
     turns_of_eight, order_hbm, strain_hbm, analysis_hbm, spin_hbm, win_hbm, wave_hbm, bank, out,
-    order, strain, analysis, spin, win, wave, packed, sems, bank_sems,
+    order, strain, analysis, spin, win, wave, packed, sems, bank_sem,
 ):
     segs, cols, first_len = strain.shape
     tail = segs * cols
@@ -114,7 +114,8 @@
                     ],
                 )
             )
-    bank_copies = start_copies(bank_pairs, bank_sems)
+    for source, target in bank_pairs:
+        pltpu.make_async_copy(source, target, bank_sem).start()
     scale = 0.5 * math.sqrt(8.0 / 3.0)
     win_c, win_s = turn(win[0], win[1], spin[0:1, :], spin[1:2, :])
     window = jnp.concatenate(
@@ -145,8 +146,8 @@
     out[:, tail : 2 * tail] = imag[:, :tail].astype(BF16)
     joined = jnp.concatenate([real[:, tail:], imag[:, tail:]], 1)
     out[:, 2 * tail : lane] = joined.astype(BF16)
-    for copy in bank_copies:
-        copy.wait()
+    whole_bank = out.at[:, lane:]
+    pltpu.make_async_copy(whole_bank, whole_bank, bank_sem).wait()
 
 
 def forward_kernel(
@@ -174,13 +175,11 @@
 
 def inverse_tables_kernel(
     even_c, even_s, odd_c, odd_s, rows_rc, rows_rs, lift_c, lift_s, lift_rc, lift_rs, mid_c, mid_s,
-    cols_c, cols_s, cols_rc, cols_rs,
-    even_out, odd_out, lift_out_c, lift_out_s, cols_out, rows_out, bins_out,
+    even_out, odd_out, lift_out_c, lift_out_s,
 ):
     half_len = even_c.shape[1]
     quarter = half_len // 2
-    first_len = cols_c.shape[1]
-    per = first_len // 2
+    per = lift_out_c.shape[0] // 2
 
     def spread(out, cos, sin):
         def body(step, carry):
@@ -214,6 +213,11 @@
     lift_out_c[0:STEP, :] = mid_c[...]
     lift_out_s[0:STEP, :] = mid_s[...]
 
+
+def column_tables_kernel(rows, cols_c, cols_s, cols_rc, cols_rs, cols_out, rows_out, bins_out):
+    first_len = cols_c.shape[1]
+    per = first_len // 2
+
     def columns(step, carry):
         cos, sin = carry
         upper = aligned(step * STEP, STEP)
@@ -229,7 +233,7 @@
         return turn(cos, sin, cols_rc[...], cols_rs[...])
 
     lax.fori_loop(0, per // STEP, columns, (cols_c[...], cols_s[...]))
-    sort_tables(lift_c.shape[1], rows_out, bins_out)
+    sort_tables(rows, rows_out, bins_out)
 
 
 def stage_two_kernel(
@@ -462,16 +466,16 @@
     return norm
 
 
-def early_kernel(near, theirs, both, far, chosen, *refs):
+def early_kernel(near, theirs, chosen, *refs):
     tables, (lifted, norm, filtered) = refs[:4], refs[4:]
-    blocks = [*[near.at[at] for at in range(4)], *[theirs.at[at] for at in range(4)], both.at[0], both.at[1], far]
+    blocks = [*[near.at[at] for at in range(4)], *[theirs.at[at] for at in range(4)]]
     zero = jnp.zeros(norm.shape, F32)
     norm[...] = filter_blocks(EARLY, blocks, chosen, tables, zero, filtered, lifted)
 
 
-def middle_kernel(theirs, early, early_norm, chosen, *refs):
+def middle_kernel(both, far, theirs, early, early_norm, chosen, *refs):
     tables, (lifted, norm, filtered) = refs[:4], refs[4:]
-    blocks = [theirs.at[at] for at in range(3)]
+    blocks = [both.at[0], both.at[1], far, *[theirs.at[at] for at in range(3)]]
     norm[...] = filter_blocks(MIDDLE, blocks, chosen, tables, early_norm[...], filtered, lifted)
 
 
@@ -549,7 +553,7 @@
             vmem((2, dev_count * rows, first_len // 2)),
             vmem((2, (segs + 1) * cols, first_len // 2)),
             pltpu.SemaphoreType.DMA((segs + 5,)),
-            pltpu.SemaphoreType.DMA((2 * templates,)),
+            pltpu.SemaphoreType.DMA,
         ],
         out_shape=pltpu.VMEM((dev_count * rows, lanes + 2 * half_len), BF16),
         compiler_params=params(16),
@@ -605,6 +609,8 @@
         np.stack([lift_init[0][1], lift_init[1][1]]),
         *turns(step_sign[:, None] * second[None, :], length),
         *turns(mid_rows[:, None] * second[None, :], length),
+    ]
+    columns = [
         *turns(step[:, None] * cols_rows[None, :], first_len),
         *turns(STEP * cols_rows[None, :], first_len),
     ]
@@ -613,6 +619,8 @@
         ((half_len, second_len), BF16),
         ((first_len, second_len), F32),
         ((first_len, second_len), F32),
+    ]
+    column_shapes = [
         ((first_len, 2 * first_len), BF16),
         ((2, first_len // 2, first_len // 2), BF16),
         ((256, 256), BF16),
@@ -626,7 +634,17 @@
         cost_estimate=pl.CostEstimate(flops=10**7, bytes_accessed=2 * 10**7, transcendentals=0),
         name="inverse_tables",
     )
-    even_table, odd_table, lift_c, lift_s, cols_table, by_rows, by_bins = inverse_tables(*in_hbm(*back))
+    even_table, odd_table, lift_c, lift_s = inverse_tables(*in_hbm(*back))
+    column_tables = pl.pallas_call(
+        functools.partial(column_tables_kernel, rows),
+        out_shape=[pltpu.VMEM(*shape) for shape in column_shapes],
+        in_specs=[whole()] * len(columns),
+        out_specs=[whole()] * len(column_shapes),
+        compiler_params=params(8),
+        cost_estimate=pl.CostEstimate(flops=10**7, bytes_accessed=10**7, transcendentals=0),
+        name="column_tables",
+    )
+    cols_table, by_rows, by_bins = column_tables(*in_hbm(*columns))
 
     mid_c, mid_s = turns(first_len // 2 * second[None, :], length)
     all_rows = 2 * (segs + 2) * rows
@@ -680,26 +698,26 @@
     early = pl.pallas_call(
         early_kernel,
         out_shape=[pltpu.VMEM(*spread), pltpu.VMEM((rows, half_len), F32)],
-        in_specs=[whole()] * 9,
+        in_specs=[whole()] * 7,
         out_specs=[whole()] * 2,
         scratch_shapes=[vmem((len(EARLY) * 2 * rows, 2 * half_len))],
         compiler_params=params(16),
         cost_estimate=pl.CostEstimate(flops=10**9, bytes_accessed=4 * 10**6, transcendentals=0),
         name="early",
     )
-    lifted, norm = early(near, theirs, both, far, chosen, *tables)
+    lifted, norm = early(near, theirs, chosen, *tables)
     middle = pl.pallas_call(
         middle_kernel,
         out_shape=[pltpu.VMEM(*spread), pltpu.VMEM((rows, half_len), F32)],
-        in_specs=[whole()] * 8,
+        in_specs=[whole()] * 10,
         out_specs=[whole()] * 2,
         scratch_shapes=[vmem((len(MIDDLE) * 2 * rows, 2 * half_len))],
-        input_output_aliases={1: 0},
+        input_output_aliases={3: 0},
         compiler_params=params(16),
         cost_estimate=pl.CostEstimate(flops=10**9, bytes_accessed=4 * 10**6, transcendentals=0),
         name="middle",
     )
-    lifted, norm = middle(more, *in_vmem(lifted, norm), chosen, *tables)
+    lifted, norm = middle(both, far, more, *in_vmem(lifted, norm), chosen, *tables)
     result, _ = pl.pallas_call(
         late_kernel,
         out_shape=[pltpu.HBM((1, first_len, second_len), BF16), pltpu.VMEM(*spread)],

time: 66.9 us -> 66.6 us (level)
  waiting for transfers between devices: 31.7 us -> 30.9 us
    ppermute x9, waiting for transfers between devices: 9.06 us -> 8.29 us  [swap_with(): return lax.ppermute(array, 'tmpl', pairs)]
    pallas_call x3 -> x4, Pallas kernels: 5.17 us -> 5.68 us  [the longest x1 2.33 us: tiled_local(): even_table, odd_table, lift_c, lift_s = inverse_tables(*in_hbm(*back))]
  transfers between devices with their start and end apart: 11 -> 11, of which waited for: 5 -> 4; matrix products, arithmetic and copies ran while one was open for 0% -> 0% of each run, Pallas kernels for 12% -> 13%
where the time goes in v4:
time: 66.6 us; the launch traced here: 66.1 us
  waiting for transfers between devices  30.9 us (46%)
  starting transfers between devices  19.2 us (29%)
  Pallas kernels  15.7 us (24%)
    all_to_all x1, waiting for transfers between devices, tiled_local(): lax.all_to_all(sent.reshape(dev_count, rows, lanes + 2 * half_len), 'tmpl...  22.6 us
    ppermute x9, starting transfers between devices, swap_with(): return lax.ppermute(array, 'tmpl', pairs)  10.2 us
    ppermute x9, waiting for transfers between devices, swap_with(): return lax.ppermute(array, 'tmpl', pairs)  8.29 us
    all_to_all x1, starting transfers between devices, tiled_local(): lax.all_to_all(sent.reshape(dev_count, rows, lanes + 2 * half_len), 'tmpl...  7.43 us
    pallas_call x1, Pallas kernels, tiled_local(): pl.pallas_call(functools.partial(stage_one_kernel, turns_of_eight), in_sp...  3.05 us
    pallas_call x1, Pallas kernels, tiled_local(): pl.pallas_call(late_kernel, out_shape=[pltpu.HBM((1, first_len, second_le...  2.93 us
    pallas_call x1, Pallas kernels, tiled_local(): even_table, odd_table, lift_c, lift_s = inverse_tables(*in_hbm(*back))  2.33 us
    ppermute x1, starting transfers between devices, tiled_local(): other = lax.ppermute(own, 'grp', [(0, 1), (1, 0)])  1.56 us
  transfers between devices with their start and end apart: 11, of which 4 were waited for; matrix products, arithmetic and copies ran while one was open for 0% of the time, Pallas kernels for 13%

profile of v4, /device:TPU:0, one launch (start us, length us, event | category | flops | bytes accessed | tf_op | source)
XLA Modules:
  0.0 66.1 jit_solution(14070262342734211582)
XLA Ops:
  0.0 3.0 %stage_one.1 = bf16[256,2176]{1,0:T(8,128)(2,1)} custom-call(s32[16]{0:T(128)} %order.1, f32[8,64,512]{2,1,0:T(8,128)} %bitcast.10, f32[64,512]{1,0:T(8,128)} %bitcast.15, f32[16,2,512]{2,1,0:T(2,128)} %constant.58.clone.spin_hbm, f32[2,8,512]{2,1,0:T(8,128)} %constant.59.clone.win_hbm, bf16[2,256,256]{2,1,0:T(8,128)(2,1)} %constant.60.clone.wave_hbm, ...), custom_call_target="tpu_custom_call" | custom-call | tf_op jit(solution)/shard_map/stage_one/pallas_call | solution.py:543
  3.1 7.4 %all-to-all-start = ((bf16[16,16,2176]{2,1,0:T(8,128)(2,1)}), bf16[16,16,2176]{2,1,0:T(8,128)(2,1)S(1)}, u32[]{:S(2)}, u32[]{:S(2)}) async-start(bf16[16,16,2176]{2,1,0:T(8,128)(2,1)} %bitcast.2), calls=%async_computation | async-start | bytes 2228224 | tf_op jit(solution)/shard_map/all_to_all | solution.py:567
  10.5 1.3 %forward_tables.1 = (bf16[2,512,512]{2,1,0:T(8,128)(2,1)S(1)}, f32[16,1024]{1,0:T(8,128)S(1)}, f32[16,1024]{1,0:T(8,128)S(1)}) custom-call(f32[16,512]{1,0:T(8,128)} %constant.61.clone.fore_c, f32[16,512]{1,0:T(8,128)} %constant.62.clone.fore_s, f32[1,512]{1,0:T(1,128)} %constant.63.clone.fore_rc, f32[1,512]{1,0:T(1,128)} %constant.64.clone.fore_rs, ...), custom_call_target="tpu_custom_call" | custom-call | flops 10000000 | bytes 20000000 | tf_op jit(solution)/shard_map/forward_tables/pallas_call | solution.py:592
  11.8 22.6 %all-to-all-done.moved = bf16[16,16,2176]{2,1,0:T(8,128)(2,1)S(1)} async-done(((bf16[16,16,2176]{2,1,0:T(8,128)(2,1)}), bf16[16,16,2176]{2,1,0:T(8,128)(2,1)S(1)}, u32[]{:S(2)}, u32[]{:S(2)}) %all-to-all-start) | async-done | bytes 1114144 | tf_op jit(solution)/shard_map/all_to_all | solution.py:567
  34.4 1.4 %stage_two.1 = bf16[32,1536]{1,0:T(8,128)(2,1)S(1)} custom-call(bf16[16,16,2176]{2,1,0:T(8,128)(2,1)S(1)} %all-to-all-done.moved, f32[16,1024]{1,0:T(8,128)S(1)} %get-tuple-element.20.near_c, f32[16,1024]{1,0:T(8,128)S(1)} %get-tuple-element.21.near_s, f32[1,1024]{1,0:T(1,128)} %constant.85.clone.mid_c_hbm, f32[1,1024]{1,0:T(1,128)} %constant.86.clone.mid_s_hbm, ...), custom_call_target="tpu_custom_call" | custom-call | flops 1000000000 | bytes 4000000 | tf_op jit(solution)/shard_map/stage_two/pallas_call | solution.py:667
  35.8 0.0 copy-start
  35.8 0.0 copy-start.1
  35.9 3.4 %collective-permute-start.4 = (bf16[32,1536]{1,0:T(8,128)(2,1)S(1)}, bf16[32,1536]{1,0:T(8,128)(2,1)S(1)}, u32[]{:S(2)}, u32[]{:S(2)}) collective-permute-start(bf16[32,1536]{1,0:T(8,128)(2,1)S(1)} %stage_two.1), channel_id=1, source_target_pairs={{0,4},{1,5},{2,6},{3,7},{4,0},{5,1},{6,2},{7,3},{8,12},{9,13},{10,... | collective-permute-start | bytes 294920 | tf_op jit(solution)/shard_map/ppermute | solution.py:516
  39.3 2.1 %collective-permute-start = (bf16[32,1536]{1,0:T(8,128)(2,1)S(1)}, bf16[32,1536]{1,0:T(8,128)(2,1)S(1)}, u32[]{:S(2)}, u32[]{:S(2)}) collective-permute-start(bf16[32,1536]{1,0:T(8,128)(2,1)S(1)} %stage_two.1), channel_id=1, source_target_pairs={{0,8},{1,9},{2,10},{3,11},{4,12},{5,13},{6,14},{7,15},{8,0},{9,1},... | collective-permute-start | bytes 294920 | tf_op jit(solution)/shard_map/ppermute | solution.py:516
  41.4 1.4 %collective-permute-start.7 = (bf16[32,1536]{1,0:T(8,128)(2,1)S(1)}, bf16[32,1536]{1,0:T(8,128)(2,1)S(1)}, u32[]{:S(2)}, u32[]{:S(2)}) collective-permute-start(bf16[32,1536]{1,0:T(8,128)(2,1)S(1)} %stage_two.1), channel_id=1, source_target_pairs={{0,2},{1,3},{2,0},{3,1},{4,6},{5,7},{6,4},{7,5},{8,10},{9,11},{10,... | collective-permute-start | bytes 294920 | tf_op jit(solution)/shard_map/ppermute | solution.py:516
  42.8 0.1 slice.7.own
  42.9 1.6 %collective-permute-start.9 = (bf16[16,16,1024]{2,1,0:T(8,128)(2,1)S(1)}, bf16[16,16,1024]{2,1,0:T(8,128)(2,1)S(1)}, u32[]{:S(2)}, u32[]{:S(2)}) collective-permute-start(bf16[16,16,1024]{2,1,0:T(8,128)(2,1)S(1)} %slice.7.own), channel_id=1, source_target_pairs={{0,16},{16,0},{1,17},{17,1},{2,18},{18,2},{3,19},{19,3},{4,20},{20... | collective-permute-start | bytes 1572872 | tf_op jit(solution)/shard_map/ppermute | solution.py:571
  44.4 0.0 collective-permute-done.4
  44.4 3.3 %collective-permute-done = bf16[32,1536]{1,0:T(8,128)(2,1)S(1)} collective-permute-done((bf16[32,1536]{1,0:T(8,128)(2,1)S(1)}, bf16[32,1536]{1,0:T(8,128)(2,1)S(1)}, u32[]{:S(2)}, u32[]{:S(2)}) %collective-permute-start) | collective-permute-done | bytes 98336 | tf_op jit(solution)/shard_map/ppermute | solution.py:516
  47.7 1.6 %collective-permute-start.5 = (bf16[2,32,1536]{2,1,0:T(8,128)(2,1)S(1)}, bf16[2,32,1536]{2,1,0:T(8,128)(2,1)S(1)}, u32[]{:S(2)}, u32[]{:S(2)}) collective-permute-start(bf16[2,32,1536]{2,1,0:T(8,128)(2,1)S(1)} %pad_maximum_fusion.2), channel_id=1, source_target_pairs={{0,2},{1,3},{2,0},{3,1},{4,6},{5,7},{6,4},{7,5},{8,10},{9,11},{10,... | collective-permute-start | bytes 589832 | tf_op jit(solution)/shard_map/ppermute | solution.py:516
  49.3 0.0 collective-permute-start.1
  49.3 0.0 collective-permute-done.7
  49.3 0.1 pad_maximum_fusion.near
  49.3 0.1 collective-permute-start.8
  49.4 4.5 %collective-permute-done.1.far = bf16[32,1536]{1,0:T(8,128)(2,1)S(1)} collective-permute-done((bf16[32,1536]{1,0:T(8,128)(2,1)S(1)}, bf16[32,1536]{1,0:T(8,128)(2,1)S(1)}, u32[]{:S(2)}, u32[]{:S(2)}) %collective-permute-start.1) | collective-permute-done | bytes 98336 | tf_op jit(solution)/shard_map/ppermute | solution.py:516
  53.9 0.5 collective-permute-done.5.both
  54.4 0.1 collective-permute-start.6
  54.5 1.4 %collective-permute-start.2 = (bf16[32,1536]{1,0:T(8,128)(2,1)S(1)}, bf16[32,1536]{1,0:T(8,128)(2,1)S(1)}, u32[]{:S(2)}, u32[]{:S(2)}) collective-permute-start(bf16[32,1536]{1,0:T(8,128)(2,1)S(1)} %collective-permute-done.1.far), channel_id=1, source_target_pairs={{0,2},{1,3},{2,0},{3,1},{4,6},{5,7},{6,4},{7,5},{8,10},{9,11},{10,... | collective-permute-start | bytes 294920 | tf_op jit(solution)/shard_map/ppermute | solution.py:516
  55.9 1.5 %column_tables.1 = (bf16[512,1024]{1,0:T(8,128)(2,1)S(1)}, bf16[2,256,256]{2,1,0:T(8,128)(2,1)S(1)}, bf16[256,256]{1,0:T(8,128)(2,1)S(1)}) custom-call(f32[16,512]{1,0:T(8,128)} %constant.81.clone.cols_c, f32[16,512]{1,0:T(8,128)} %constant.82.clone.cols_s, f32[1,512]{1,0:T(1,128)} %constant.83.clone.cols_rc, f32[1,512]{1,0:T(1,128)} %constant.84.clone.cols_rs), custom_call_target="tpu_custom_call" | custom-call | flops 10000000 | bytes 10000000 | tf_op jit(solution)/shard_map/column_tables/pallas_call | solution.py:647
  57.4 2.3 %inverse_tables.1 = (bf16[512,1024]{1,0:T(8,128)(2,1)S(1)}, bf16[512,1024]{1,0:T(8,128)(2,1)S(1)}, f32[512,1024]{1,0:T(8,128)S(1)}, f32[512,1024]{1,0:T(8,128)S(1)}) custom-call(f32[16,512]{1,0:T(8,128)} %constant.69.clone.even_c, f32[16,512]{1,0:T(8,128)} %constant.70.clone.even_s, f32[16,512]{1,0:T(8,128)} %constant.71.clone.odd_c, ...), custom_call_target="tpu_custom_call" | custom-call | flops 10000000 | bytes 20000000 | tf_op jit(solution)/shard_map/inverse_tables/pallas_call | solution.py:637
  59.7 0.0 collective-permute-done.2.last
  59.7 0.2 collective-permute-start.3
  59.9 0.0 collective-permute-done.9.other
  59.9 0.0 copy-done
  59.9 0.0 copy-done.1
  60.0 1.3 %choose.1.chosen = bf16[512,1024]{1,0:T(8,128)(2,1)S(1)} custom-call(s32[16]{0:T(128)S(1)} %copy-done, s32[16]{0:T(128)S(1)} %copy-done.1, bf16[16,16,1024]{2,1,0:T(8,128)(2,1)S(1)} %slice.7.own, bf16[16,16,1024]{2,1,0:T(8,128)(2,1)S(1)} %collective-permute-done.9.other, bf16[2,256,256]{2,1,0:T(8,128)(2,1)S(1)} %get-tuple-element.23.by_rows, ...), custom_call_target="tpu_custom_call" | custom-call | flops 1000000000 | bytes 4000000 | tf_op jit(solution)/shard_map/choose/pallas_call | solution.py:694
  61.3 0.0 collective-permute-done.8.theirs
  61.3 1.0 %early.1 = (bf16[1024,1024]{1,0:T(8,128)(2,1)S(1)}, f32[16,512]{1,0:T(8,128)S(1)}) custom-call(bf16[4,32,1536]{2,1,0:T(8,128)(2,1)S(1)} %pad_maximum_fusion.near, bf16[4,32,1536]{2,1,0:T(8,128)(2,1)S(1)} %collective-permute-done.8.theirs, bf16[512,1024]{1,0:T(8,128)(2,1)S(1)} %choose.1.chosen, bf16[512,1024]{1,0:T(8,128)(2,1)S(1)} %get-tuple-element.25.refs_0_, ...), custom_call_target="tpu_custom_call" | custom-call | flops 1000000000 | bytes 4000000 | tf_op jit(solution)/shard_map/early/pallas_call | solution.py:708
  62.4 0.0 collective-permute-done.6.theirs
  62.4 0.8 %middle.1 = (bf16[1024,1024]{1,0:T(8,128)(2,1)S(1)}, f32[16,512]{1,0:T(8,128)S(1)}) custom-call(bf16[2,32,1536]{2,1,0:T(8,128)(2,1)S(1)} %collective-permute-done.5.both, bf16[32,1536]{1,0:T(8,128)(2,1)S(1)} %collective-permute-done.1.far, bf16[3,32,1536]{2,1,0:T(8,128)(2,1)S(1)} %collective-permute-done.6.theirs, ...), custom_call_target="tpu_custom_call", output_to_operand_aliasing={{0}: (3, {})} | custom-call | flops 1000000000 | bytes 4000000 | tf_op jit(solution)/shard_map/middle/pallas_call | solution.py:720
  63.2 0.0 collective-permute-done.3.theirs
  63.2 2.9 %late.1 = (bf16[1,512,1024]{2,1,0:T(8,128)(2,1)}, bf16[1024,1024]{1,0:T(8,128)(2,1)S(1)}) custom-call(bf16[32,1536]{1,0:T(8,128)(2,1)S(1)} %collective-permute-done.2.last, bf16[32,1536]{1,0:T(8,128)(2,1)S(1)} %collective-permute-done.3.theirs, bf16[1024,1024]{1,0:T(8,128)(2,1)S(1)} %get-tuple-element.31.early, ...), custom_call_target="tpu_custom_call", output_to_operand_aliasing={{1}: (2, {})} | custom-call | tf_op jit(solution)/shard_map/late/pallas_call | solution.py:721
  (2 shorter events, 0.0 us)
Async XLA Ops:
  3.1 31.4 %all-to-all-start = ((bf16[16,16,2176]{2,1,0:T(8,128)(2,1)}), bf16[16,16,2176]{2,1,0:T(8,128)(2,1)S(1)}, u32[]{:S(2)}, u32[]{:S(2)}) async-start(bf16[16,16,2176]{2,1,0:T(8,128)(2,1)} %bitcast.2), calls=%async_computation | async-start | bytes 2228224 | tf_op jit(solution)/shard_map/all_to_all | solution.py:567
  35.8 24.1 %copy-start = (s32[16]{0:T(128)S(1)}, s32[16]{0:T(128)}, u32[]{:S(2)}) copy-start(s32[16]{0:T(128)} %order.1) | copy-start | bytes 196
  35.8 24.1 %copy-start.1 = (s32[16]{0:T(128)S(1)}, s32[16]{0:T(128)}, u32[]{:S(2)}) copy-start(s32[16]{0:T(128)} %cuts.1) | copy-start | bytes 196
  35.9 8.6 %collective-permute-start.4 = (bf16[32,1536]{1,0:T(8,128)(2,1)S(1)}, bf16[32,1536]{1,0:T(8,128)(2,1)S(1)}, u32[]{:S(2)}, u32[]{:S(2)}) collective-permute-start(bf16[32,1536]{1,0:T(8,128)(2,1)S(1)} %stage_two.1), channel_id=1, source_target_pairs={{0,4},{1,5},{2,6},{3,7},{4,0},{5,1},{6,2},{7,3},{8,12},{9,13},{10,... | collective-permute-start | bytes 294920 | tf_op jit(solution)/shard_map/ppermute | solution.py:516
  39.3 8.4 %collective-permute-start = (bf16[32,1536]{1,0:T(8,128)(2,1)S(1)}, bf16[32,1536]{1,0:T(8,128)(2,1)S(1)}, u32[]{:S(2)}, u32[]{:S(2)}) collective-permute-start(bf16[32,1536]{1,0:T(8,128)(2,1)S(1)} %stage_two.1), channel_id=1, source_target_pairs={{0,8},{1,9},{2,10},{3,11},{4,12},{5,13},{6,14},{7,15},{8,0},{9,1},... | collective-permute-start | bytes 294920 | tf_op jit(solution)/shard_map/ppermute | solution.py:516
  41.4 7.8 %collective-permute-start.7 = (bf16[32,1536]{1,0:T(8,128)(2,1)S(1)}, bf16[32,1536]{1,0:T(8,128)(2,1)S(1)}, u32[]{:S(2)}, u32[]{:S(2)}) collective-permute-start(bf16[32,1536]{1,0:T(8,128)(2,1)S(1)} %stage_two.1), channel_id=1, source_target_pairs={{0,2},{1,3},{2,0},{3,1},{4,6},{5,7},{6,4},{7,5},{8,10},{9,11},{10,... | collective-permute-start | bytes 294920 | tf_op jit(solution)/shard_map/ppermute | solution.py:516
  42.9 17.1 %collective-permute-start.9 = (bf16[16,16,1024]{2,1,0:T(8,128)(2,1)S(1)}, bf16[16,16,1024]{2,1,0:T(8,128)(2,1)S(1)}, u32[]{:S(2)}, u32[]{:S(2)}) collective-permute-start(bf16[16,16,1024]{2,1,0:T(8,128)(2,1)S(1)} %slice.7.own), channel_id=1, source_target_pairs={{0,16},{16,0},{1,17},{17,1},{2,18},{18,2},{3,19},{19,3},{4,20},{20... | collective-permute-start | bytes 1572872 | tf_op jit(solution)/shard_map/ppermute | solution.py:571
  47.7 6.7 %collective-permute-start.5 = (bf16[2,32,1536]{2,1,0:T(8,128)(2,1)S(1)}, bf16[2,32,1536]{2,1,0:T(8,128)(2,1)S(1)}, u32[]{:S(2)}, u32[]{:S(2)}) collective-permute-start(bf16[2,32,1536]{2,1,0:T(8,128)(2,1)S(1)} %pad_maximum_fusion.2), channel_id=1, source_target_pairs={{0,2},{1,3},{2,0},{3,1},{4,6},{5,7},{6,4},{7,5},{8,10},{9,11},{10,... | collective-permute-start | bytes 589832 | tf_op jit(solution)/shard_map/ppermute | solution.py:516
  49.3 4.6 %collective-permute-start.1 = (bf16[32,1536]{1,0:T(8,128)(2,1)S(1)}, bf16[32,1536]{1,0:T(8,128)(2,1)S(1)}, u32[]{:S(2)}, u32[]{:S(2)}) collective-permute-start(bf16[32,1536]{1,0:T(8,128)(2,1)S(1)} %collective-permute-done), channel_id=1, source_target_pairs={{0,4},{1,5},{2,6},{3,7},{4,0},{5,1},{6,2},{7,3},{8,12},{9,13},{10,... | collective-permute-start | bytes 294920 | tf_op jit(solution)/shard_map/ppermute | solution.py:516
  49.3 12.0 %collective-permute-start.8 = (bf16[4,32,1536]{2,1,0:T(8,128)(2,1)S(1)}, bf16[4,32,1536]{2,1,0:T(8,128)(2,1)S(1)}, u32[]{:S(2)}, u32[]{:S(2)}) collective-permute-start(bf16[4,32,1536]{2,1,0:T(8,128)(2,1)S(1)} %pad_maximum_fusion.near), channel_id=1, source_target_pairs={{0,1},{1,0},{2,3},{3,2},{4,5},{5,4},{6,7},{7,6},{8,9},{9,8},{10,11... | collective-permute-start | bytes 1179656 | tf_op jit(solution)/shard_map/ppermute | solution.py:516
  54.4 7.9 %collective-permute-start.6 = (bf16[3,32,1536]{2,1,0:T(8,128)(2,1)S(1)}, bf16[3,32,1536]{2,1,0:T(8,128)(2,1)S(1)}, u32[]{:S(2)}, u32[]{:S(2)}) collective-permute-start(bf16[3,32,1536]{2,1,0:T(8,128)(2,1)S(1)} %pad_maximum_fusion.1), channel_id=1, source_target_pairs={{0,1},{1,0},{2,3},{3,2},{4,5},{5,4},{6,7},{7,6},{8,9},{9,8},{10,11... | collective-permute-start | bytes 884744 | tf_op jit(solution)/shard_map/ppermute | solution.py:516
  54.5 5.2 %collective-permute-start.2 = (bf16[32,1536]{1,0:T(8,128)(2,1)S(1)}, bf16[32,1536]{1,0:T(8,128)(2,1)S(1)}, u32[]{:S(2)}, u32[]{:S(2)}) collective-permute-start(bf16[32,1536]{1,0:T(8,128)(2,1)S(1)} %collective-permute-done.1.far), channel_id=1, source_target_pairs={{0,2},{1,3},{2,0},{3,1},{4,6},{5,7},{6,4},{7,5},{8,10},{9,11},{10,... | collective-permute-start | bytes 294920 | tf_op jit(solution)/shard_map/ppermute | solution.py:516
  59.7 3.5 %collective-permute-start.3 = (bf16[32,1536]{1,0:T(8,128)(2,1)S(1)}, bf16[32,1536]{1,0:T(8,128)(2,1)S(1)}, u32[]{:S(2)}, u32[]{:S(2)}) collective-permute-start(bf16[32,1536]{1,0:T(8,128)(2,1)S(1)} %collective-permute-done.2.last), channel_id=1, source_target_pairs={{0,1},{1,0},{2,3},{3,2},{4,5},{5,4},{6,7},{7,6},{8,9},{9,8},{10,11... | collective-permute-start | bytes 294920 | tf_op jit(solution)/shard_map/ppermute | solution.py:516

commit v5 on v4

--- a/solution.py
+++ b/solution.py
@@ -473,9 +473,9 @@
     norm[...] = filter_blocks(EARLY, blocks, chosen, tables, zero, filtered, lifted)
 
 
-def middle_kernel(both, far, theirs, early, early_norm, chosen, *refs):
+def middle_kernel(six, ten, far, theirs, early, early_norm, chosen, *refs):
     tables, (lifted, norm, filtered) = refs[:4], refs[4:]
-    blocks = [both.at[0], both.at[1], far, *[theirs.at[at] for at in range(3)]]
+    blocks = [six, ten, far, *[theirs.at[at] for at in range(3)]]
     norm[...] = filter_blocks(MIDDLE, blocks, chosen, tables, early_norm[...], filtered, lifted)
 
 
@@ -669,12 +669,15 @@
     two = swap_with(block, 8)
     one = swap_with(block, 4)
     beside = swap_with(block, 2)
-    both = swap_with(jnp.stack([one, two]), 2)
     far = swap_with(two, 4)
+    ten = swap_with(two, 2)
+    six = swap_with(one, 2)
     near = jnp.stack([block, beside, one, two])
     theirs = swap_with(near, 1)
-    last = swap_with(far, 2)
-    more = swap_with(jnp.stack([both[0], both[1], far]), 1)
+    last_upper = swap_with(far[:rows], 2)
+    last_lower = swap_with(ten[rows:], 4)
+    last = jnp.concatenate([last_upper, last_lower], 0)
+    more = swap_with(jnp.stack([six, ten, far]), 1)
     late = swap_with(last, 1)
 
     choose = pl.pallas_call(
@@ -709,15 +712,15 @@
     middle = pl.pallas_call(
         middle_kernel,
         out_shape=[pltpu.VMEM(*spread), pltpu.VMEM((rows, half_len), F32)],
-        in_specs=[whole()] * 10,
+        in_specs=[whole()] * 11,
         out_specs=[whole()] * 2,
         scratch_shapes=[vmem((len(MIDDLE) * 2 * rows, 2 * half_len))],
-        input_output_aliases={3: 0},
+        input_output_aliases={4: 0},
         compiler_params=params(16),
         cost_estimate=pl.CostEstimate(flops=10**9, bytes_accessed=4 * 10**6, transcendentals=0),
         name="middle",
     )
-    lifted, norm = middle(both, far, more, *in_vmem(lifted, norm), chosen, *tables)
+    lifted, norm = middle(six, ten, far, more, *in_vmem(lifted, norm), chosen, *tables)
     result, _ = pl.pallas_call(
         late_kernel,
         out_shape=[pltpu.HBM((1, first_len, second_len), BF16), pltpu.VMEM(*spread)],

time: 66.6 us -> 66.7 us (level)
  starting transfers between devices: 19.2 us -> 21.1 us
  waiting for transfers between devices: 30.9 us -> 29.2 us
    ppermute x9 -> x11, waiting for transfers between devices: 8.29 us -> 4.66 us  [swap_with(): return lax.ppermute(array, 'tmpl', pairs)]
    ppermute x9 -> x11, starting transfers between devices: 10.2 us -> 12.1 us  [swap_with(): return lax.ppermute(array, 'tmpl', pairs)]
    ppermute x1, waiting for transfers between devices: 0.01 us -> 1.89 us  [tiled_local(): other = lax.ppermute(own, 'grp', [(0, 1), (1, 0)])]
  transfers between devices with their start and end apart: 11 -> 13, of which waited for: 4 -> 4; matrix products, arithmetic and copies ran while one was open for 0% -> 0% of each run, Pallas kernels for 13% -> 13%
where the time goes in v5:
time: 66.7 us; the launch traced here: 66.3 us
  waiting for transfers between devices  29.2 us (44%)
  starting transfers between devices  21.1 us (32%)
  Pallas kernels  15.7 us (24%)
    all_to_all x1, waiting for transfers between devices, tiled_local(): lax.all_to_all(sent.reshape(dev_count, rows, lanes + 2 * half_len), 'tmpl...  22.6 us
    ppermute x11, starting transfers between devices, swap_with(): return lax.ppermute(array, 'tmpl', pairs)  12.1 us
    all_to_all x1, starting transfers between devices, tiled_local(): lax.all_to_all(sent.reshape(dev_count, rows, lanes + 2 * half_len), 'tmpl...  7.43 us
    ppermute x11, waiting for transfers between devices, swap_with(): return lax.ppermute(array, 'tmpl', pairs)  4.66 us
    pallas_call x1, Pallas kernels, tiled_local(): pl.pallas_call(functools.partial(stage_one_kernel, turns_of_eight), in_sp...  3.06 us
    pallas_call x1, Pallas kernels, tiled_local(): pl.pallas_call(late_kernel, out_shape=[pltpu.HBM((1, first_len, second_le...  2.92 us
    pallas_call x1, Pallas kernels, tiled_local(): even_table, odd_table, lift_c, lift_s = inverse_tables(*in_hbm(*back))  2.33 us
    ppermute x1, waiting for transfers between devices, tiled_local(): other = lax.ppermute(own, 'grp', [(0, 1), (1, 0)])  1.89 us
  transfers between devices with their start and end apart: 13, of which 4 were waited for; matrix products, arithmetic and copies ran while one was open for 0% of the time, Pallas kernels for 13%

profile of v5, /device:TPU:0, one launch (start us, length us, event | category | flops | bytes accessed | tf_op | source)
XLA Modules:
  0.0 66.3 jit_solution(4296040016868997033)
XLA Ops:
  0.0 3.1 %stage_one.1 = bf16[256,2176]{1,0:T(8,128)(2,1)} custom-call(s32[16]{0:T(128)} %order.1, f32[8,64,512]{2,1,0:T(8,128)} %bitcast.14, f32[64,512]{1,0:T(8,128)} %bitcast.15, f32[16,2,512]{2,1,0:T(2,128)} %constant.58.clone.spin_hbm, f32[2,8,512]{2,1,0:T(8,128)} %constant.59.clone.win_hbm, bf16[2,256,256]{2,1,0:T(8,128)(2,1)} %constant.60.clone.wave_hbm, ...), custom_call_target="tpu_custom_call" | custom-call | tf_op jit(solution)/shard_map/stage_one/pallas_call | solution.py:543
  3.1 7.4 %all-to-all-start = ((bf16[16,16,2176]{2,1,0:T(8,128)(2,1)}), bf16[16,16,2176]{2,1,0:T(8,128)(2,1)S(1)}, u32[]{:S(2)}, u32[]{:S(2)}) async-start(bf16[16,16,2176]{2,1,0:T(8,128)(2,1)} %bitcast.2), calls=%async_computation | async-start | bytes 2228224 | tf_op jit(solution)/shard_map/all_to_all | solution.py:567
  10.5 1.3 %forward_tables.1 = (bf16[2,512,512]{2,1,0:T(8,128)(2,1)S(1)}, f32[16,1024]{1,0:T(8,128)S(1)}, f32[16,1024]{1,0:T(8,128)S(1)}) custom-call(f32[16,512]{1,0:T(8,128)} %constant.61.clone.fore_c, f32[16,512]{1,0:T(8,128)} %constant.62.clone.fore_s, f32[1,512]{1,0:T(1,128)} %constant.63.clone.fore_rc, f32[1,512]{1,0:T(1,128)} %constant.64.clone.fore_rs, ...), custom_call_target="tpu_custom_call" | custom-call | flops 10000000 | bytes 20000000 | tf_op jit(solution)/shard_map/forward_tables/pallas_call | solution.py:592
  11.8 22.6 %all-to-all-done.moved = bf16[16,16,2176]{2,1,0:T(8,128)(2,1)S(1)} async-done(((bf16[16,16,2176]{2,1,0:T(8,128)(2,1)}), bf16[16,16,2176]{2,1,0:T(8,128)(2,1)S(1)}, u32[]{:S(2)}, u32[]{:S(2)}) %all-to-all-start) | async-done | bytes 1114144 | tf_op jit(solution)/shard_map/all_to_all | solution.py:567
  34.5 1.4 %stage_two.1 = bf16[32,1536]{1,0:T(8,128)(2,1)S(1)} custom-call(bf16[16,16,2176]{2,1,0:T(8,128)(2,1)S(1)} %all-to-all-done.moved, f32[16,1024]{1,0:T(8,128)S(1)} %get-tuple-element.20.near_c, f32[16,1024]{1,0:T(8,128)S(1)} %get-tuple-element.21.near_s, f32[1,1024]{1,0:T(1,128)} %constant.85.clone.mid_c_hbm, f32[1,1024]{1,0:T(1,128)} %constant.86.clone.mid_s_hbm, ...), custom_call_target="tpu_custom_call" | custom-call | flops 1000000000 | bytes 4000000 | tf_op jit(solution)/shard_map/stage_two/pallas_call | solution.py:667
  35.8 0.0 copy-start
  35.8 0.0 copy-start.1
  35.9 5.5 %collective-permute-start = (bf16[32,1536]{1,0:T(8,128)(2,1)S(1)}, bf16[32,1536]{1,0:T(8,128)(2,1)S(1)}, u32[]{:S(2)}, u32[]{:S(2)}) collective-permute-start(bf16[32,1536]{1,0:T(8,128)(2,1)S(1)} %stage_two.1), channel_id=1, source_target_pairs={{0,8},{1,9},{2,10},{3,11},{4,12},{5,13},{6,14},{7,15},{8,0},{9,1},... | collective-permute-start | bytes 294920 | tf_op jit(solution)/shard_map/ppermute | solution.py:516
  41.4 0.0 collective-permute-start.6
  41.4 1.4 %collective-permute-start.9 = (bf16[32,1536]{1,0:T(8,128)(2,1)S(1)}, bf16[32,1536]{1,0:T(8,128)(2,1)S(1)}, u32[]{:S(2)}, u32[]{:S(2)}) collective-permute-start(bf16[32,1536]{1,0:T(8,128)(2,1)S(1)} %stage_two.1), channel_id=1, source_target_pairs={{0,2},{1,3},{2,0},{3,1},{4,6},{5,7},{6,4},{7,5},{8,10},{9,11},{10,... | collective-permute-start | bytes 294920 | tf_op jit(solution)/shard_map/ppermute | solution.py:516
  42.8 1.5 %column_tables.1 = (bf16[512,1024]{1,0:T(8,128)(2,1)S(1)}, bf16[2,256,256]{2,1,0:T(8,128)(2,1)S(1)}, bf16[256,256]{1,0:T(8,128)(2,1)S(1)}) custom-call(f32[16,512]{1,0:T(8,128)} %constant.81.clone.cols_c, f32[16,512]{1,0:T(8,128)} %constant.82.clone.cols_s, f32[1,512]{1,0:T(1,128)} %constant.83.clone.cols_rc, f32[1,512]{1,0:T(1,128)} %constant.84.clone.cols_rs), custom_call_target="tpu_custom_call" | custom-call | flops 10000000 | bytes 10000000 | tf_op jit(solution)/shard_map/column_tables/pallas_call | solution.py:647
  44.3 2.3 %inverse_tables.1 = (bf16[512,1024]{1,0:T(8,128)(2,1)S(1)}, bf16[512,1024]{1,0:T(8,128)(2,1)S(1)}, f32[512,1024]{1,0:T(8,128)S(1)}, f32[512,1024]{1,0:T(8,128)S(1)}) custom-call(f32[16,512]{1,0:T(8,128)} %constant.69.clone.even_c, f32[16,512]{1,0:T(8,128)} %constant.70.clone.even_s, f32[16,512]{1,0:T(8,128)} %constant.71.clone.odd_c, ...), custom_call_target="tpu_custom_call" | custom-call | flops 10000000 | bytes 20000000 | tf_op jit(solution)/shard_map/inverse_tables/pallas_call | solution.py:637
  46.6 0.1 slice.14.own
  46.7 1.6 %collective-permute-start.11 = (bf16[16,16,1024]{2,1,0:T(8,128)(2,1)S(1)}, bf16[16,16,1024]{2,1,0:T(8,128)(2,1)S(1)}, u32[]{:S(2)}, u32[]{:S(2)}) collective-permute-start(bf16[16,16,1024]{2,1,0:T(8,128)(2,1)S(1)} %slice.14.own), channel_id=1, source_target_pairs={{0,16},{16,0},{1,17},{17,1},{2,18},{18,2},{3,19},{19,3},{4,20},{20... | collective-permute-start | bytes 1572872 | tf_op jit(solution)/shard_map/ppermute | solution.py:571
  48.3 0.0 collective-permute-done
  48.3 0.6 collective-permute-start.3
  48.8 2.0 %collective-permute-start.1 = (bf16[32,1536]{1,0:T(8,128)(2,1)S(1)}, bf16[32,1536]{1,0:T(8,128)(2,1)S(1)}, u32[]{:S(2)}, u32[]{:S(2)}) collective-permute-start(bf16[32,1536]{1,0:T(8,128)(2,1)S(1)} %collective-permute-done), channel_id=1, source_target_pairs={{0,4},{1,5},{2,6},{3,7},{4,0},{5,1},{6,2},{7,3},{8,12},{9,13},{10,... | collective-permute-start | bytes 294920 | tf_op jit(solution)/shard_map/ppermute | solution.py:516
  50.9 0.0 collective-permute-done.6
  50.9 0.0 collective-permute-start.7
  50.9 0.0 collective-permute-done.9
  50.9 0.1 pad_maximum_fusion.near
  50.9 0.1 collective-permute-start.10
  51.0 2.4 %collective-permute-done.3.ten = bf16[32,1536]{1,0:T(8,128)(2,1)S(1)} collective-permute-done((bf16[32,1536]{1,0:T(8,128)(2,1)S(1)}, bf16[32,1536]{1,0:T(8,128)(2,1)S(1)}, u32[]{:S(2)}, u32[]{:S(2)}) %collective-permute-start.3) | collective-permute-done | bytes 98336 | tf_op jit(solution)/shard_map/ppermute | solution.py:516
  53.4 0.6 collective-permute-start.4
  54.0 0.0 collective-permute-done.1.far
  54.0 1.8 %collective-permute-start.2 = (bf16[16,1536]{1,0:T(8,128)(2,1)S(1)}, bf16[16,1536]{1,0:T(8,128)(2,1)S(1)}, u32[]{:S(2)}, u32[]{:S(2)}) collective-permute-start(bf16[16,1536]{1,0:T(8,128)(2,1)S(1)} %slice.12), channel_id=1, source_target_pairs={{0,2},{1,3},{2,0},{3,1},{4,6},{5,7},{6,4},{7,5},{8,10},{9,11},{10,... | collective-permute-start | bytes 147464 | tf_op jit(solution)/shard_map/ppermute | solution.py:516
  55.8 0.0 collective-permute-done.7.six
  55.8 0.1 collective-permute-start.8
  55.9 2.2 %collective-permute-done.2 = bf16[16,1536]{1,0:T(8,128)(2,1)S(1)} collective-permute-done((bf16[16,1536]{1,0:T(8,128)(2,1)S(1)}, bf16[16,1536]{1,0:T(8,128)(2,1)S(1)}, u32[]{:S(2)}, u32[]{:S(2)}) %collective-permute-start.2) | collective-permute-done | bytes 49184 | tf_op jit(solution)/shard_map/ppermute | solution.py:516
  58.2 0.0 collective-permute-done.4
  58.2 0.1 collective-permute-start.5
  58.3 1.9 %collective-permute-done.11.other = bf16[16,16,1024]{2,1,0:T(8,128)(2,1)S(1)} collective-permute-done((bf16[16,16,1024]{2,1,0:T(8,128)(2,1)S(1)}, bf16[16,16,1024]{2,1,0:T(8,128)(2,1)S(1)}, u32[]{:S(2)}, u32[]{:S(2)}) %collective-permute-start.11) | collective-permute-done | bytes 524320 | tf_op jit(solution)/shard_map/ppermute | solution.py:571
  60.1 0.0 copy-done
  60.2 0.0 copy-done.1
  60.2 1.3 %choose.1.chosen = bf16[512,1024]{1,0:T(8,128)(2,1)S(1)} custom-call(s32[16]{0:T(128)S(1)} %copy-done, s32[16]{0:T(128)S(1)} %copy-done.1, bf16[16,16,1024]{2,1,0:T(8,128)(2,1)S(1)} %slice.14.own, bf16[16,16,1024]{2,1,0:T(8,128)(2,1)S(1)} %collective-permute-done.11.other, bf16[2,256,256]{2,1,0:T(8,128)(2,1)S(1)} %get-tuple-element.23.by_rows, ...), custom_call_target="tpu_custom_call" | custom-call | flops 1000000000 | bytes 4000000 | tf_op jit(solution)/shard_map/choose/pallas_call | solution.py:697
  61.5 0.0 collective-permute-done.10.theirs
  61.5 1.0 %early.1 = (bf16[1024,1024]{1,0:T(8,128)(2,1)S(1)}, f32[16,512]{1,0:T(8,128)S(1)}) custom-call(bf16[4,32,1536]{2,1,0:T(8,128)(2,1)S(1)} %pad_maximum_fusion.near, bf16[4,32,1536]{2,1,0:T(8,128)(2,1)S(1)} %collective-permute-done.10.theirs, bf16[512,1024]{1,0:T(8,128)(2,1)S(1)} %choose.1.chosen, bf16[512,1024]{1,0:T(8,128)(2,1)S(1)} %get-tuple-element.25.refs_0_, ...), custom_call_target="tpu_custom_call" | custom-call | flops 1000000000 | bytes 4000000 | tf_op jit(solution)/shard_map/early/pallas_call | solution.py:711
  62.5 0.0 collective-permute-done.8.theirs
  62.6 0.8 %middle.1 = (bf16[1024,1024]{1,0:T(8,128)(2,1)S(1)}, f32[16,512]{1,0:T(8,128)S(1)}) custom-call(bf16[32,1536]{1,0:T(8,128)(2,1)S(1)} %collective-permute-done.7.six, bf16[32,1536]{1,0:T(8,128)(2,1)S(1)} %collective-permute-done.3.ten, bf16[32,1536]{1,0:T(8,128)(2,1)S(1)} %collective-permute-done.1.far, ...), custom_call_target="tpu_custom_call", output_to_operand_aliasing={{0}: (4, {})} | custom-call | flops 1000000000 | bytes 4000000 | tf_op jit(solution)/shard_map/middle/pallas_call | solution.py:723
  63.4 0.0 collective-permute-done.5.theirs
  63.4 2.9 %late.1 = (bf16[1,512,1024]{2,1,0:T(8,128)(2,1)}, bf16[1024,1024]{1,0:T(8,128)(2,1)S(1)}) custom-call(bf16[32,1536]{1,0:T(8,128)(2,1)S(1)} %constant_dynamic-update-slice_fusion.last, bf16[32,1536]{1,0:T(8,128)(2,1)S(1)} %collective-permute-done.5.theirs, bf16[1024,1024]{1,0:T(8,128)(2,1)S(1)} %get-tuple-element.31.early, ...), custom_call_target="tpu_custom_call", output_to_operand_aliasing={{1}: (2, {})} | custom-call | tf_op jit(solution)/shard_map/late/pallas_call | solution.py:724
  (5 shorter events, 0.1 us)
Async XLA Ops:
  3.1 31.4 %all-to-all-start = ((bf16[16,16,2176]{2,1,0:T(8,128)(2,1)}), bf16[16,16,2176]{2,1,0:T(8,128)(2,1)S(1)}, u32[]{:S(2)}, u32[]{:S(2)}) async-start(bf16[16,16,2176]{2,1,0:T(8,128)(2,1)} %bitcast.2), calls=%async_computation | async-start | bytes 2228224 | tf_op jit(solution)/shard_map/all_to_all | solution.py:567
  35.8 24.3 %copy-start = (s32[16]{0:T(128)S(1)}, s32[16]{0:T(128)}, u32[]{:S(2)}) copy-start(s32[16]{0:T(128)} %order.1) | copy-start | bytes 196
  35.8 24.3 %copy-start.1 = (s32[16]{0:T(128)S(1)}, s32[16]{0:T(128)}, u32[]{:S(2)}) copy-start(s32[16]{0:T(128)} %cuts.1) | copy-start | bytes 196
  35.9 12.4 %collective-permute-start = (bf16[32,1536]{1,0:T(8,128)(2,1)S(1)}, bf16[32,1536]{1,0:T(8,128)(2,1)S(1)}, u32[]{:S(2)}, u32[]{:S(2)}) collective-permute-start(bf16[32,1536]{1,0:T(8,128)(2,1)S(1)} %stage_two.1), channel_id=1, source_target_pairs={{0,8},{1,9},{2,10},{3,11},{4,12},{5,13},{6,14},{7,15},{8,0},{9,1},... | collective-permute-start | bytes 294920 | tf_op jit(solution)/shard_map/ppermute | solution.py:516
  41.4 9.5 %collective-permute-start.6 = (bf16[32,1536]{1,0:T(8,128)(2,1)S(1)}, bf16[32,1536]{1,0:T(8,128)(2,1)S(1)}, u32[]{:S(2)}, u32[]{:S(2)}) collective-permute-start(bf16[32,1536]{1,0:T(8,128)(2,1)S(1)} %stage_two.1), channel_id=1, source_target_pairs={{0,4},{1,5},{2,6},{3,7},{4,0},{5,1},{6,2},{7,3},{8,12},{9,13},{10,... | collective-permute-start | bytes 294920 | tf_op jit(solution)/shard_map/ppermute | solution.py:516
  41.4 9.5 %collective-permute-start.9 = (bf16[32,1536]{1,0:T(8,128)(2,1)S(1)}, bf16[32,1536]{1,0:T(8,128)(2,1)S(1)}, u32[]{:S(2)}, u32[]{:S(2)}) collective-permute-start(bf16[32,1536]{1,0:T(8,128)(2,1)S(1)} %stage_two.1), channel_id=1, source_target_pairs={{0,2},{1,3},{2,0},{3,1},{4,6},{5,7},{6,4},{7,5},{8,10},{9,11},{10,... | collective-permute-start | bytes 294920 | tf_op jit(solution)/shard_map/ppermute | solution.py:516
  46.7 13.4 %collective-permute-start.11 = (bf16[16,16,1024]{2,1,0:T(8,128)(2,1)S(1)}, bf16[16,16,1024]{2,1,0:T(8,128)(2,1)S(1)}, u32[]{:S(2)}, u32[]{:S(2)}) collective-permute-start(bf16[16,16,1024]{2,1,0:T(8,128)(2,1)S(1)} %slice.14.own), channel_id=1, source_target_pairs={{0,16},{16,0},{1,17},{17,1},{2,18},{18,2},{3,19},{19,3},{4,20},{20... | collective-permute-start | bytes 1572872 | tf_op jit(solution)/shard_map/ppermute | solution.py:571
  48.3 5.2 %collective-permute-start.3 = (bf16[32,1536]{1,0:T(8,128)(2,1)S(1)}, bf16[32,1536]{1,0:T(8,128)(2,1)S(1)}, u32[]{:S(2)}, u32[]{:S(2)}) collective-permute-start(bf16[32,1536]{1,0:T(8,128)(2,1)S(1)} %collective-permute-done), channel_id=1, source_target_pairs={{0,2},{1,3},{2,0},{3,1},{4,6},{5,7},{6,4},{7,5},{8,10},{9,11},{10,... | collective-permute-start | bytes 294920 | tf_op jit(solution)/shard_map/ppermute | solution.py:516
  48.8 5.2 %collective-permute-start.1 = (bf16[32,1536]{1,0:T(8,128)(2,1)S(1)}, bf16[32,1536]{1,0:T(8,128)(2,1)S(1)}, u32[]{:S(2)}, u32[]{:S(2)}) collective-permute-start(bf16[32,1536]{1,0:T(8,128)(2,1)S(1)} %collective-permute-done), channel_id=1, source_target_pairs={{0,4},{1,5},{2,6},{3,7},{4,0},{5,1},{6,2},{7,3},{8,12},{9,13},{10,... | collective-permute-start | bytes 294920 | tf_op jit(solution)/shard_map/ppermute | solution.py:516
  50.9 4.9 %collective-permute-start.7 = (bf16[32,1536]{1,0:T(8,128)(2,1)S(1)}, bf16[32,1536]{1,0:T(8,128)(2,1)S(1)}, u32[]{:S(2)}, u32[]{:S(2)}) collective-permute-start(bf16[32,1536]{1,0:T(8,128)(2,1)S(1)} %collective-permute-done.6), channel_id=1, source_target_pairs={{0,2},{1,3},{2,0},{3,1},{4,6},{5,7},{6,4},{7,5},{8,10},{9,11},{10,... | collective-permute-start | bytes 294920 | tf_op jit(solution)/shard_map/ppermute | solution.py:516
  50.9 10.6 %collective-permute-start.10 = (bf16[4,32,1536]{2,1,0:T(8,128)(2,1)S(1)}, bf16[4,32,1536]{2,1,0:T(8,128)(2,1)S(1)}, u32[]{:S(2)}, u32[]{:S(2)}) collective-permute-start(bf16[4,32,1536]{2,1,0:T(8,128)(2,1)S(1)} %pad_maximum_fusion.near), channel_id=1, source_target_pairs={{0,1},{1,0},{2,3},{3,2},{4,5},{5,4},{6,7},{7,6},{8,9},{9,8},{10,11... | collective-permute-start | bytes 1179656 | tf_op jit(solution)/shard_map/ppermute | solution.py:516
  53.4 4.7 %collective-permute-start.4 = (bf16[16,1536]{1,0:T(8,128)(2,1)S(1)}, bf16[16,1536]{1,0:T(8,128)(2,1)S(1)}, u32[]{:S(2)}, u32[]{:S(2)}) collective-permute-start(bf16[16,1536]{1,0:T(8,128)(2,1)S(1)} %slice.13), channel_id=1, source_target_pairs={{0,4},{1,5},{2,6},{3,7},{4,0},{5,1},{6,2},{7,3},{8,12},{9,13},{10,... | collective-permute-start | bytes 147464 | tf_op jit(solution)/shard_map/ppermute | solution.py:516
  54.0 4.2 %collective-permute-start.2 = (bf16[16,1536]{1,0:T(8,128)(2,1)S(1)}, bf16[16,1536]{1,0:T(8,128)(2,1)S(1)}, u32[]{:S(2)}, u32[]{:S(2)}) collective-permute-start(bf16[16,1536]{1,0:T(8,128)(2,1)S(1)} %slice.12), channel_id=1, source_target_pairs={{0,2},{1,3},{2,0},{3,1},{4,6},{5,7},{6,4},{7,5},{8,10},{9,11},{10,... | collective-permute-start | bytes 147464 | tf_op jit(solution)/shard_map/ppermute | solution.py:516
  55.8 6.7 %collective-permute-start.8 = (bf16[3,32,1536]{2,1,0:T(8,128)(2,1)S(1)}, bf16[3,32,1536]{2,1,0:T(8,128)(2,1)S(1)}, u32[]{:S(2)}, u32[]{:S(2)}) collective-permute-start(bf16[3,32,1536]{2,1,0:T(8,128)(2,1)S(1)} %pad_maximum_fusion.1), channel_id=1, source_target_pairs={{0,1},{1,0},{2,3},{3,2},{4,5},{5,4},{6,7},{7,6},{8,9},{9,8},{10,11... | collective-permute-start | bytes 884744 | tf_op jit(solution)/shard_map/ppermute | solution.py:516
  58.2 5.2 %collective-permute-start.5 = (bf16[32,1536]{1,0:T(8,128)(2,1)S(1)}, bf16[32,1536]{1,0:T(8,128)(2,1)S(1)}, u32[]{:S(2)}, u32[]{:S(2)}) collective-permute-start(bf16[32,1536]{1,0:T(8,128)(2,1)S(1)} %constant_dynamic-update-slice_fusion.last), channel_id=1, source_target_pairs={{0,1},{1,0},{2,3},{3,2},{4,5},{5,4},{6,7},{7,6},{8,9},{9,8},{10,11... | collective-permute-start | bytes 294920 | tf_op jit(solution)/shard_map/ppermute | solution.py:516

commit v6 on v5

--- a/solution.py
+++ b/solution.py
@@ -100,8 +100,7 @@
     ]
     copies = start_copies(sources, sems)
     lane = 2 * (tail + cols)
-    for copy in copies[:3]:
-        copy.wait()
+    copies[0].wait()
     bank_pairs = []
     for row in range(templates):
         for part in range(2):
@@ -116,6 +115,8 @@
             )
     for source, target in bank_pairs:
         pltpu.make_async_copy(source, target, bank_sem).start()
+    for copy in copies[1:3]:
+        copy.wait()
     scale = 0.5 * math.sqrt(8.0 / 3.0)
     win_c, win_s = turn(win[0], win[1], spin[0:1, :], spin[1:2, :])
     window = jnp.concatenate(
@@ -174,12 +175,10 @@
 
 
 def inverse_tables_kernel(
-    even_c, even_s, odd_c, odd_s, rows_rc, rows_rs, lift_c, lift_s, lift_rc, lift_rs, mid_c, mid_s,
-    even_out, odd_out, lift_out_c, lift_out_s,
+    even_c, even_s, odd_c, odd_s, rows_rc, rows_rs, even_out, odd_out
 ):
     half_len = even_c.shape[1]
     quarter = half_len // 2
-    per = lift_out_c.shape[0] // 2
 
     def spread(out, cos, sin):
         def body(step, carry):
@@ -200,6 +199,11 @@
     spread(even_out, even_c[...], even_s[...])
     spread(odd_out, odd_c[...], odd_s[...])
 
+
+def lift_tables_kernel(
+    lift_c, lift_s, lift_rc, lift_rs, mid_c, mid_s, lift_out_c, lift_out_s
+):
+    per = lift_out_c.shape[0] // 2
     for parity in range(2):
 
         def lifts(step, carry, parity=parity):
@@ -605,6 +609,8 @@
         *turns(2 * step[:, None] * half[None, :], second_len),
         *turns((2 * step[:, None] + 1) * half[None, :], second_len),
         *turns(2 * STEP * half[None, :], second_len),
+    ]
+    lifts = [
         np.stack([lift_init[0][0], lift_init[1][0]]),
         np.stack([lift_init[0][1], lift_init[1][1]]),
         *turns(step_sign[:, None] * second[None, :], length),
@@ -614,12 +620,8 @@
         *turns(step[:, None] * cols_rows[None, :], first_len),
         *turns(STEP * cols_rows[None, :], first_len),
     ]
-    shapes = [
-        ((half_len, second_len), BF16),
-        ((half_len, second_len), BF16),
-        ((first_len, second_len), F32),
-        ((first_len, second_len), F32),
-    ]
+    shapes = [((half_len, second_len), BF16)] * 2
+    lift_shapes = [((first_len, second_len), F32)] * 2
     column_shapes = [
         ((first_len, 2 * first_len), BF16),
         ((2, first_len // 2, first_len // 2), BF16),
@@ -634,7 +636,17 @@
         cost_estimate=pl.CostEstimate(flops=10**7, bytes_accessed=2 * 10**7, transcendentals=0),
         name="inverse_tables",
     )
-    even_table, odd_table, lift_c, lift_s = inverse_tables(*in_hbm(*back))
+    even_table, odd_table = inverse_tables(*in_hbm(*back))
+    lift_tables = pl.pallas_call(
+        lift_tables_kernel,
+        out_shape=[pltpu.VMEM(*shape) for shape in lift_shapes],
+        in_specs=[whole()] * len(lifts),
+        out_specs=[whole()] * len(lift_shapes),
+        compiler_params=params(8),
+        cost_estimate=pl.CostEstimate(flops=10**7, bytes_accessed=10**7, transcendentals=0),
+        name="lift_tables",
+    )
+    lift_c, lift_s = lift_tables(*in_hbm(*lifts))
     column_tables = pl.pallas_call(
         functools.partial(column_tables_kernel, rows),
         out_shape=[pltpu.VMEM(*shape) for shape in column_shapes],

time: 66.7 us -> 67.5 us (1.012)
  Pallas kernels: 15.7 us -> 16.4 us
    pallas_call x1 -> x2, Pallas kernels: 2.33 us -> 3.01 us  [the longest x1 1.82 us: tiled_local(): lift_c, lift_s = lift_tables(*in_hbm(*lifts))]
where the time goes in v6:
time: 67.5 us; the launch traced here: 67 us
  waiting for transfers between devices  29.2 us (43%)
  starting transfers between devices  21.1 us (31%)
  Pallas kernels  16.4 us (24%)
    all_to_all x1, waiting for transfers between devices, tiled_local(): lax.all_to_all(sent.reshape(dev_count, rows, lanes + 2 * half_len), 'tmpl...  22.6 us
    ppermute x11, starting transfers between devices, swap_with(): return lax.ppermute(array, 'tmpl', pairs)  12.1 us
    all_to_all x1, starting transfers between devices, tiled_local(): lax.all_to_all(sent.reshape(dev_count, rows, lanes + 2 * half_len), 'tmpl...  7.43 us
    ppermute x11, waiting for transfers between devices, swap_with(): return lax.ppermute(array, 'tmpl', pairs)  4.66 us
    pallas_call x1, Pallas kernels, tiled_local(): pl.pallas_call(functools.partial(stage_one_kernel, turns_of_eight), in_sp...  3.07 us
    pallas_call x1, Pallas kernels, tiled_local(): pl.pallas_call(late_kernel, out_shape=[pltpu.HBM((1, first_len, second_le...  2.93 us
    ppermute x1, waiting for transfers between devices, tiled_local(): other = lax.ppermute(own, 'grp', [(0, 1), (1, 0)])  1.89 us
    pallas_call x1, Pallas kernels, tiled_local(): lift_c, lift_s = lift_tables(*in_hbm(*lifts))  1.82 us
  transfers between devices with their start and end apart: 13, of which 4 were waited for; matrix products, arithmetic and copies ran while one was open for 0% of the time, Pallas kernels for 13%

profile of v6, /device:TPU:0, one launch (start us, length us, event | category | flops | bytes accessed | tf_op | source)
XLA Modules:
  0.0 67.0 jit_solution(1773264133779669123)
XLA Ops:
  0.0 3.1 %stage_one.1 = bf16[256,2176]{1,0:T(8,128)(2,1)} custom-call(s32[16]{0:T(128)} %order.1, f32[8,64,512]{2,1,0:T(8,128)} %bitcast.14, f32[64,512]{1,0:T(8,128)} %bitcast.15, f32[16,2,512]{2,1,0:T(2,128)} %constant.58.clone.spin_hbm, f32[2,8,512]{2,1,0:T(8,128)} %constant.59.clone.win_hbm, bf16[2,256,256]{2,1,0:T(8,128)(2,1)} %constant.60.clone.wave_hbm, ...), custom_call_target="tpu_custom_call" | custom-call | tf_op jit(solution)/shard_map/stage_one/pallas_call | solution.py:547
  3.1 7.4 %all-to-all-start = ((bf16[16,16,2176]{2,1,0:T(8,128)(2,1)}), bf16[16,16,2176]{2,1,0:T(8,128)(2,1)S(1)}, u32[]{:S(2)}, u32[]{:S(2)}) async-start(bf16[16,16,2176]{2,1,0:T(8,128)(2,1)} %bitcast.2), calls=%async_computation | async-start | bytes 2228224 | tf_op jit(solution)/shard_map/all_to_all | solution.py:571
  10.5 1.3 %forward_tables.1 = (bf16[2,512,512]{2,1,0:T(8,128)(2,1)S(1)}, f32[16,1024]{1,0:T(8,128)S(1)}, f32[16,1024]{1,0:T(8,128)S(1)}) custom-call(f32[16,512]{1,0:T(8,128)} %constant.61.clone.fore_c, f32[16,512]{1,0:T(8,128)} %constant.62.clone.fore_s, f32[1,512]{1,0:T(1,128)} %constant.63.clone.fore_rc, f32[1,512]{1,0:T(1,128)} %constant.64.clone.fore_rs, ...), custom_call_target="tpu_custom_call" | custom-call | flops 10000000 | bytes 20000000 | tf_op jit(solution)/shard_map/forward_tables/pallas_call | solution.py:596
  11.8 22.6 %all-to-all-done.moved = bf16[16,16,2176]{2,1,0:T(8,128)(2,1)S(1)} async-done(((bf16[16,16,2176]{2,1,0:T(8,128)(2,1)}), bf16[16,16,2176]{2,1,0:T(8,128)(2,1)S(1)}, u32[]{:S(2)}, u32[]{:S(2)}) %all-to-all-start) | async-done | bytes 1114144 | tf_op jit(solution)/shard_map/all_to_all | solution.py:571
  34.5 1.4 %stage_two.1 = bf16[32,1536]{1,0:T(8,128)(2,1)S(1)} custom-call(bf16[16,16,2176]{2,1,0:T(8,128)(2,1)S(1)} %all-to-all-done.moved, f32[16,1024]{1,0:T(8,128)S(1)} %get-tuple-element.20.near_c, f32[16,1024]{1,0:T(8,128)S(1)} %get-tuple-element.21.near_s, f32[1,1024]{1,0:T(1,128)} %constant.85.clone.mid_c_hbm, f32[1,1024]{1,0:T(1,128)} %constant.86.clone.mid_s_hbm, ...), custom_call_target="tpu_custom_call" | custom-call | flops 1000000000 | bytes 4000000 | tf_op jit(solution)/shard_map/stage_two/pallas_call | solution.py:679
  35.9 0.0 copy-start
  35.9 0.0 copy-start.1
  35.9 5.5 %collective-permute-start = (bf16[32,1536]{1,0:T(8,128)(2,1)S(1)}, bf16[32,1536]{1,0:T(8,128)(2,1)S(1)}, u32[]{:S(2)}, u32[]{:S(2)}) collective-permute-start(bf16[32,1536]{1,0:T(8,128)(2,1)S(1)} %stage_two.1), channel_id=1, source_target_pairs={{0,8},{1,9},{2,10},{3,11},{4,12},{5,13},{6,14},{7,15},{8,0},{9,1},... | collective-permute-start | bytes 294920 | tf_op jit(solution)/shard_map/ppermute | solution.py:520
  41.4 0.0 collective-permute-start.6
  41.4 1.4 %collective-permute-start.9 = (bf16[32,1536]{1,0:T(8,128)(2,1)S(1)}, bf16[32,1536]{1,0:T(8,128)(2,1)S(1)}, u32[]{:S(2)}, u32[]{:S(2)}) collective-permute-start(bf16[32,1536]{1,0:T(8,128)(2,1)S(1)} %stage_two.1), channel_id=1, source_target_pairs={{0,2},{1,3},{2,0},{3,1},{4,6},{5,7},{6,4},{7,5},{8,10},{9,11},{10,... | collective-permute-start | bytes 294920 | tf_op jit(solution)/shard_map/ppermute | solution.py:520
  42.8 1.5 %column_tables.1 = (bf16[512,1024]{1,0:T(8,128)(2,1)S(1)}, bf16[2,256,256]{2,1,0:T(8,128)(2,1)S(1)}, bf16[256,256]{1,0:T(8,128)(2,1)S(1)}) custom-call(f32[16,512]{1,0:T(8,128)} %constant.81.clone.cols_c, f32[16,512]{1,0:T(8,128)} %constant.82.clone.cols_s, f32[1,512]{1,0:T(1,128)} %constant.83.clone.cols_rc, f32[1,512]{1,0:T(1,128)} %constant.84.clone.cols_rs), custom_call_target="tpu_custom_call" | custom-call | flops 10000000 | bytes 10000000 | tf_op jit(solution)/shard_map/column_tables/pallas_call | solution.py:659
  44.3 1.2 %inverse_tables.1 = (bf16[512,1024]{1,0:T(8,128)(2,1)S(1)}, bf16[512,1024]{1,0:T(8,128)(2,1)S(1)}) custom-call(f32[16,512]{1,0:T(8,128)} %constant.69.clone.even_c, f32[16,512]{1,0:T(8,128)} %constant.70.clone.even_s, f32[16,512]{1,0:T(8,128)} %constant.71.clone.odd_c, f32[16,512]{1,0:T(8,128)} %constant.72.clone.odd_s, f32[1,512]{1,0:T(1,128)} %constant.73.clone.rows_rc, ...), custom_call_target="tpu_custom_call" | custom-call | flops 10000000 | bytes 20000000 | tf_op jit(solution)/shard_map/inverse_tables/pallas_call | solution.py:639
  45.5 1.8 %lift_tables.1 = (f32[512,1024]{1,0:T(8,128)S(1)}, f32[512,1024]{1,0:T(8,128)S(1)}) custom-call(f32[2,16,1024]{2,1,0:T(8,128)} %constant.75.clone.lift_c, f32[2,16,1024]{2,1,0:T(8,128)} %constant.76.clone.lift_s, f32[16,1024]{1,0:T(8,128)} %constant.77.clone.lift_rc, f32[16,1024]{1,0:T(8,128)} %constant.78.clone.lift_rs, f32[16,1024]{1,0:T(8,128)} %constant.79.clone.mid_c, ...), custom_call_target="tpu_custom_call" | custom-call | flops 10000000 | bytes 10000000 | tf_op jit(solution)/shard_map/lift_tables/pallas_call | solution.py:649
  47.3 0.1 slice.14.own
  47.4 1.6 %collective-permute-start.11 = (bf16[16,16,1024]{2,1,0:T(8,128)(2,1)S(1)}, bf16[16,16,1024]{2,1,0:T(8,128)(2,1)S(1)}, u32[]{:S(2)}, u32[]{:S(2)}) collective-permute-start(bf16[16,16,1024]{2,1,0:T(8,128)(2,1)S(1)} %slice.14.own), channel_id=1, source_target_pairs={{0,16},{16,0},{1,17},{17,1},{2,18},{18,2},{3,19},{19,3},{4,20},{20... | collective-permute-start | bytes 1572872 | tf_op jit(solution)/shard_map/ppermute | solution.py:575
  49.0 0.0 collective-permute-done
  49.0 0.6 collective-permute-start.3
  49.5 2.0 %collective-permute-start.1 = (bf16[32,1536]{1,0:T(8,128)(2,1)S(1)}, bf16[32,1536]{1,0:T(8,128)(2,1)S(1)}, u32[]{:S(2)}, u32[]{:S(2)}) collective-permute-start(bf16[32,1536]{1,0:T(8,128)(2,1)S(1)} %collective-permute-done), channel_id=1, source_target_pairs={{0,4},{1,5},{2,6},{3,7},{4,0},{5,1},{6,2},{7,3},{8,12},{9,13},{10,... | collective-permute-start | bytes 294920 | tf_op jit(solution)/shard_map/ppermute | solution.py:520
  51.6 0.0 collective-permute-done.6
  51.6 0.0 collective-permute-start.7
  51.6 0.0 collective-permute-done.9
  51.6 0.1 pad_maximum_fusion.near
  51.6 0.1 collective-permute-start.10
  51.7 2.4 %collective-permute-done.3.ten = bf16[32,1536]{1,0:T(8,128)(2,1)S(1)} collective-permute-done((bf16[32,1536]{1,0:T(8,128)(2,1)S(1)}, bf16[32,1536]{1,0:T(8,128)(2,1)S(1)}, u32[]{:S(2)}, u32[]{:S(2)}) %collective-permute-start.3) | collective-permute-done | bytes 98336 | tf_op jit(solution)/shard_map/ppermute | solution.py:520
  54.1 0.6 collective-permute-start.4
  54.7 0.0 collective-permute-done.1.far
  54.7 1.8 %collective-permute-start.2 = (bf16[16,1536]{1,0:T(8,128)(2,1)S(1)}, bf16[16,1536]{1,0:T(8,128)(2,1)S(1)}, u32[]{:S(2)}, u32[]{:S(2)}) collective-permute-start(bf16[16,1536]{1,0:T(8,128)(2,1)S(1)} %slice.12), channel_id=1, source_target_pairs={{0,2},{1,3},{2,0},{3,1},{4,6},{5,7},{6,4},{7,5},{8,10},{9,11},{10,... | collective-permute-start | bytes 147464 | tf_op jit(solution)/shard_map/ppermute | solution.py:520
  56.5 0.0 collective-permute-done.7.six
  56.6 0.1 collective-permute-start.8
  56.6 2.2 %collective-permute-done.2 = bf16[16,1536]{1,0:T(8,128)(2,1)S(1)} collective-permute-done((bf16[16,1536]{1,0:T(8,128)(2,1)S(1)}, bf16[16,1536]{1,0:T(8,128)(2,1)S(1)}, u32[]{:S(2)}, u32[]{:S(2)}) %collective-permute-start.2) | collective-permute-done | bytes 49184 | tf_op jit(solution)/shard_map/ppermute | solution.py:520
  58.9 0.0 collective-permute-done.4
  58.9 0.1 collective-permute-start.5
  59.0 1.9 %collective-permute-done.11.other = bf16[16,16,1024]{2,1,0:T(8,128)(2,1)S(1)} collective-permute-done((bf16[16,16,1024]{2,1,0:T(8,128)(2,1)S(1)}, bf16[16,16,1024]{2,1,0:T(8,128)(2,1)S(1)}, u32[]{:S(2)}, u32[]{:S(2)}) %collective-permute-start.11) | collective-permute-done | bytes 524320 | tf_op jit(solution)/shard_map/ppermute | solution.py:575
  60.9 0.0 copy-done
  60.9 0.0 copy-done.1
  60.9 1.3 %choose.1.chosen = bf16[512,1024]{1,0:T(8,128)(2,1)S(1)} custom-call(s32[16]{0:T(128)S(1)} %copy-done, s32[16]{0:T(128)S(1)} %copy-done.1, bf16[16,16,1024]{2,1,0:T(8,128)(2,1)S(1)} %slice.14.own, bf16[16,16,1024]{2,1,0:T(8,128)(2,1)S(1)} %collective-permute-done.11.other, bf16[2,256,256]{2,1,0:T(8,128)(2,1)S(1)} %get-tuple-element.23.by_rows, ...), custom_call_target="tpu_custom_call" | custom-call | flops 1000000000 | bytes 4000000 | tf_op jit(solution)/shard_map/choose/pallas_call | solution.py:709
  62.2 0.0 collective-permute-done.10.theirs
  62.2 1.0 %early.1 = (bf16[1024,1024]{1,0:T(8,128)(2,1)S(1)}, f32[16,512]{1,0:T(8,128)S(1)}) custom-call(bf16[4,32,1536]{2,1,0:T(8,128)(2,1)S(1)} %pad_maximum_fusion.near, bf16[4,32,1536]{2,1,0:T(8,128)(2,1)S(1)} %collective-permute-done.10.theirs, bf16[512,1024]{1,0:T(8,128)(2,1)S(1)} %choose.1.chosen, bf16[512,1024]{1,0:T(8,128)(2,1)S(1)} %get-tuple-element.25.refs_0_, ...), custom_call_target="tpu_custom_call" | custom-call | flops 1000000000 | bytes 4000000 | tf_op jit(solution)/shard_map/early/pallas_call | solution.py:723
  63.3 0.0 collective-permute-done.8.theirs
  63.3 0.8 %middle.1 = (bf16[1024,1024]{1,0:T(8,128)(2,1)S(1)}, f32[16,512]{1,0:T(8,128)S(1)}) custom-call(bf16[32,1536]{1,0:T(8,128)(2,1)S(1)} %collective-permute-done.7.six, bf16[32,1536]{1,0:T(8,128)(2,1)S(1)} %collective-permute-done.3.ten, bf16[32,1536]{1,0:T(8,128)(2,1)S(1)} %collective-permute-done.1.far, ...), custom_call_target="tpu_custom_call", output_to_operand_aliasing={{0}: (4, {})} | custom-call | flops 1000000000 | bytes 4000000 | tf_op jit(solution)/shard_map/middle/pallas_call | solution.py:735
  64.1 0.0 collective-permute-done.5.theirs
  64.1 2.9 %late.1 = (bf16[1,512,1024]{2,1,0:T(8,128)(2,1)}, bf16[1024,1024]{1,0:T(8,128)(2,1)S(1)}) custom-call(bf16[32,1536]{1,0:T(8,128)(2,1)S(1)} %constant_dynamic-update-slice_fusion.last, bf16[32,1536]{1,0:T(8,128)(2,1)S(1)} %collective-permute-done.5.theirs, bf16[1024,1024]{1,0:T(8,128)(2,1)S(1)} %get-tuple-element.31.early, ...), custom_call_target="tpu_custom_call", output_to_operand_aliasing={{1}: (2, {})} | custom-call | tf_op jit(solution)/shard_map/late/pallas_call | solution.py:736
  (5 shorter events, 0.1 us)
Async XLA Ops:
  3.1 31.4 %all-to-all-start = ((bf16[16,16,2176]{2,1,0:T(8,128)(2,1)}), bf16[16,16,2176]{2,1,0:T(8,128)(2,1)S(1)}, u32[]{:S(2)}, u32[]{:S(2)}) async-start(bf16[16,16,2176]{2,1,0:T(8,128)(2,1)} %bitcast.2), calls=%async_computation | async-start | bytes 2228224 | tf_op jit(solution)/shard_map/all_to_all | solution.py:571
  35.9 25.0 %copy-start = (s32[16]{0:T(128)S(1)}, s32[16]{0:T(128)}, u32[]{:S(2)}) copy-start(s32[16]{0:T(128)} %order.1) | copy-start | bytes 196
  35.9 25.0 %copy-start.1 = (s32[16]{0:T(128)S(1)}, s32[16]{0:T(128)}, u32[]{:S(2)}) copy-start(s32[16]{0:T(128)} %cuts.1) | copy-start | bytes 196
  35.9 13.1 %collective-permute-start = (bf16[32,1536]{1,0:T(8,128)(2,1)S(1)}, bf16[32,1536]{1,0:T(8,128)(2,1)S(1)}, u32[]{:S(2)}, u32[]{:S(2)}) collective-permute-start(bf16[32,1536]{1,0:T(8,128)(2,1)S(1)} %stage_two.1), channel_id=1, source_target_pairs={{0,8},{1,9},{2,10},{3,11},{4,12},{5,13},{6,14},{7,15},{8,0},{9,1},... | collective-permute-start | bytes 294920 | tf_op jit(solution)/shard_map/ppermute | solution.py:520
  41.4 10.2 %collective-permute-start.6 = (bf16[32,1536]{1,0:T(8,128)(2,1)S(1)}, bf16[32,1536]{1,0:T(8,128)(2,1)S(1)}, u32[]{:S(2)}, u32[]{:S(2)}) collective-permute-start(bf16[32,1536]{1,0:T(8,128)(2,1)S(1)} %stage_two.1), channel_id=1, source_target_pairs={{0,4},{1,5},{2,6},{3,7},{4,0},{5,1},{6,2},{7,3},{8,12},{9,13},{10,... | collective-permute-start | bytes 294920 | tf_op jit(solution)/shard_map/ppermute | solution.py:520
  41.4 10.2 %collective-permute-start.9 = (bf16[32,1536]{1,0:T(8,128)(2,1)S(1)}, bf16[32,1536]{1,0:T(8,128)(2,1)S(1)}, u32[]{:S(2)}, u32[]{:S(2)}) collective-permute-start(bf16[32,1536]{1,0:T(8,128)(2,1)S(1)} %stage_two.1), channel_id=1, source_target_pairs={{0,2},{1,3},{2,0},{3,1},{4,6},{5,7},{6,4},{7,5},{8,10},{9,11},{10,... | collective-permute-start | bytes 294920 | tf_op jit(solution)/shard_map/ppermute | solution.py:520
  47.4 13.4 %collective-permute-start.11 = (bf16[16,16,1024]{2,1,0:T(8,128)(2,1)S(1)}, bf16[16,16,1024]{2,1,0:T(8,128)(2,1)S(1)}, u32[]{:S(2)}, u32[]{:S(2)}) collective-permute-start(bf16[16,16,1024]{2,1,0:T(8,128)(2,1)S(1)} %slice.14.own), channel_id=1, source_target_pairs={{0,16},{16,0},{1,17},{17,1},{2,18},{18,2},{3,19},{19,3},{4,20},{20... | collective-permute-start | bytes 1572872 | tf_op jit(solution)/shard_map/ppermute | solution.py:575
  49.0 5.2 %collective-permute-start.3 = (bf16[32,1536]{1,0:T(8,128)(2,1)S(1)}, bf16[32,1536]{1,0:T(8,128)(2,1)S(1)}, u32[]{:S(2)}, u32[]{:S(2)}) collective-permute-start(bf16[32,1536]{1,0:T(8,128)(2,1)S(1)} %collective-permute-done), channel_id=1, source_target_pairs={{0,2},{1,3},{2,0},{3,1},{4,6},{5,7},{6,4},{7,5},{8,10},{9,11},{10,... | collective-permute-start | bytes 294920 | tf_op jit(solution)/shard_map/ppermute | solution.py:520
  49.5 5.2 %collective-permute-start.1 = (bf16[32,1536]{1,0:T(8,128)(2,1)S(1)}, bf16[32,1536]{1,0:T(8,128)(2,1)S(1)}, u32[]{:S(2)}, u32[]{:S(2)}) collective-permute-start(bf16[32,1536]{1,0:T(8,128)(2,1)S(1)} %collective-permute-done), channel_id=1, source_target_pairs={{0,4},{1,5},{2,6},{3,7},{4,0},{5,1},{6,2},{7,3},{8,12},{9,13},{10,... | collective-permute-start | bytes 294920 | tf_op jit(solution)/shard_map/ppermute | solution.py:520
  51.6 4.9 %collective-permute-start.7 = (bf16[32,1536]{1,0:T(8,128)(2,1)S(1)}, bf16[32,1536]{1,0:T(8,128)(2,1)S(1)}, u32[]{:S(2)}, u32[]{:S(2)}) collective-permute-start(bf16[32,1536]{1,0:T(8,128)(2,1)S(1)} %collective-permute-done.6), channel_id=1, source_target_pairs={{0,2},{1,3},{2,0},{3,1},{4,6},{5,7},{6,4},{7,5},{8,10},{9,11},{10,... | collective-permute-start | bytes 294920 | tf_op jit(solution)/shard_map/ppermute | solution.py:520
  51.6 10.6 %collective-permute-start.10 = (bf16[4,32,1536]{2,1,0:T(8,128)(2,1)S(1)}, bf16[4,32,1536]{2,1,0:T(8,128)(2,1)S(1)}, u32[]{:S(2)}, u32[]{:S(2)}) collective-permute-start(bf16[4,32,1536]{2,1,0:T(8,128)(2,1)S(1)} %pad_maximum_fusion.near), channel_id=1, source_target_pairs={{0,1},{1,0},{2,3},{3,2},{4,5},{5,4},{6,7},{7,6},{8,9},{9,8},{10,11... | collective-permute-start | bytes 1179656 | tf_op jit(solution)/shard_map/ppermute | solution.py:520
  54.1 4.7 %collective-permute-start.4 = (bf16[16,1536]{1,0:T(8,128)(2,1)S(1)}, bf16[16,1536]{1,0:T(8,128)(2,1)S(1)}, u32[]{:S(2)}, u32[]{:S(2)}) collective-permute-start(bf16[16,1536]{1,0:T(8,128)(2,1)S(1)} %slice.13), channel_id=1, source_target_pairs={{0,4},{1,5},{2,6},{3,7},{4,0},{5,1},{6,2},{7,3},{8,12},{9,13},{10,... | collective-permute-start | bytes 147464 | tf_op jit(solution)/shard_map/ppermute | solution.py:520
  54.7 4.2 %collective-permute-start.2 = (bf16[16,1536]{1,0:T(8,128)(2,1)S(1)}, bf16[16,1536]{1,0:T(8,128)(2,1)S(1)}, u32[]{:S(2)}, u32[]{:S(2)}) collective-permute-start(bf16[16,1536]{1,0:T(8,128)(2,1)S(1)} %slice.12), channel_id=1, source_target_pairs={{0,2},{1,3},{2,0},{3,1},{4,6},{5,7},{6,4},{7,5},{8,10},{9,11},{10,... | collective-permute-start | bytes 147464 | tf_op jit(solution)/shard_map/ppermute | solution.py:520
  56.6 6.7 %collective-permute-start.8 = (bf16[3,32,1536]{2,1,0:T(8,128)(2,1)S(1)}, bf16[3,32,1536]{2,1,0:T(8,128)(2,1)S(1)}, u32[]{:S(2)}, u32[]{:S(2)}) collective-permute-start(bf16[3,32,1536]{2,1,0:T(8,128)(2,1)S(1)} %pad_maximum_fusion.1), channel_id=1, source_target_pairs={{0,1},{1,0},{2,3},{3,2},{4,5},{5,4},{6,7},{7,6},{8,9},{9,8},{10,11... | collective-permute-start | bytes 884744 | tf_op jit(solution)/shard_map/ppermute | solution.py:520
  58.9 5.2 %collective-permute-start.5 = (bf16[32,1536]{1,0:T(8,128)(2,1)S(1)}, bf16[32,1536]{1,0:T(8,128)(2,1)S(1)}, u32[]{:S(2)}, u32[]{:S(2)}) collective-permute-start(bf16[32,1536]{1,0:T(8,128)(2,1)S(1)} %constant_dynamic-update-slice_fusion.last), channel_id=1, source_target_pairs={{0,1},{1,0},{2,3},{3,2},{4,5},{5,4},{6,7},{7,6},{8,9},{9,8},{10,11... | collective-permute-start | bytes 294920 | tf_op jit(solution)/shard_map/ppermute | solution.py:520

commit v7 on v6

--- a/solution.py
+++ b/solution.py
@@ -508,9 +508,11 @@
             total = even - odd if upper else even + odd
             power = total[:per] * total[:per] + total[per:] * total[per:]
             size = power * lax.rsqrt(jnp.maximum(power, 1e-37))
-            result[upper * per : (upper + 1) * per, at] = (size * scale).astype(BF16)
-        copies.append(pltpu.make_async_copy(result.at[:, at], out.at[0, :, at], sems.at[block]))
-        copies[-1].start()
+            row = slice(upper * per, (upper + 1) * per)
+            result[row, at] = (size * scale).astype(BF16)
+            piece = sems.at[2 * block + upper]
+            copies.append(pltpu.make_async_copy(result.at[row, at], out.at[0, row, at], piece))
+            copies[-1].start()
     for copy in copies:
         copy.wait()
 
@@ -690,7 +692,9 @@
     last_lower = swap_with(ten[rows:], 4)
     last = jnp.concatenate([last_upper, last_lower], 0)
     more = swap_with(jnp.stack([six, ten, far]), 1)
-    late = swap_with(last, 1)
+    late_lower = swap_with(last_lower, 1)
+    late_upper = swap_with(last_upper, 1)
+    late = jnp.concatenate([late_upper, late_lower], 0)
 
     choose = pl.pallas_call(
         choose_kernel,
@@ -741,7 +745,7 @@
         scratch_shapes=[
             vmem((len(LATE) * 2 * rows, 2 * half_len)),
             vmem((first_len, second_len)),
-            pltpu.SemaphoreType.DMA((second_len // 256,)),
+            pltpu.SemaphoreType.DMA((second_len // 128,)),
         ],
         input_output_aliases={2: 1},
         compiler_params=params(16),

time: 67.5 us -> 67.5 us (level)
    ppermute x11 -> x12, waiting for transfers between devices: 4.66 us -> 5.87 us  [swap_with(): return lax.ppermute(array, 'tmpl', pairs)]
    ppermute x1, waiting for transfers between devices: 1.89 us -> 0.75 us  [tiled_local(): other = lax.ppermute(own, 'grp', [(0, 1), (1, 0)])]
    ppermute x11 -> x12, starting transfers between devices: 12.1 us -> 12.1 us  [swap_with(): return lax.ppermute(array, 'tmpl', pairs)]
  transfers between devices with their start and end apart: 13 -> 14, of which waited for: 4 -> 7; matrix products, arithmetic and copies ran while one was open for 0% -> 0% of each run, Pallas kernels for 13% -> 12%
where the time goes in v7:
time: 67.5 us; the launch traced here: 67.1 us
  waiting for transfers between devices  29.2 us (43%)
  starting transfers between devices  21 us (31%)
  Pallas kernels  16.4 us (24%)
    all_to_all x1, waiting for transfers between devices, tiled_local(): lax.all_to_all(sent.reshape(dev_count, rows, lanes + 2 * half_len), 'tmpl...  22.6 us
    ppermute x12, starting transfers between devices, swap_with(): return lax.ppermute(array, 'tmpl', pairs)  12.1 us
    all_to_all x1, starting transfers between devices, tiled_local(): lax.all_to_all(sent.reshape(dev_count, rows, lanes + 2 * half_len), 'tmpl...  7.43 us
    ppermute x12, waiting for transfers between devices, swap_with(): return lax.ppermute(array, 'tmpl', pairs)  5.87 us
    pallas_call x1, Pallas kernels, tiled_local(): pl.pallas_call(functools.partial(stage_one_kernel, turns_of_eight), in_sp...  3.06 us
    pallas_call x1, Pallas kernels, tiled_local(): pl.pallas_call(late_kernel, out_shape=[pltpu.HBM((1, first_len, second_le...  2.95 us
    pallas_call x1, Pallas kernels, tiled_local(): lift_c, lift_s = lift_tables(*in_hbm(*lifts))  1.82 us
    ppermute x1, starting transfers between devices, tiled_local(): other = lax.ppermute(own, 'grp', [(0, 1), (1, 0)])  1.56 us
  transfers between devices with their start and end apart: 14, of which 7 were waited for; matrix products, arithmetic and copies ran while one was open for 0% of the time, Pallas kernels for 12%

profile of v7, /device:TPU:0, one launch (start us, length us, event | category | flops | bytes accessed | tf_op | source)
XLA Modules:
  0.0 67.1 jit_solution(10431824504643140437)
XLA Ops:
  0.0 3.1 %stage_one.1 = bf16[256,2176]{1,0:T(8,128)(2,1)} custom-call(s32[16]{0:T(128)} %order.1, f32[8,64,512]{2,1,0:T(8,128)} %bitcast.14, f32[64,512]{1,0:T(8,128)} %bitcast.15, f32[16,2,512]{2,1,0:T(2,128)} %constant.58.clone.spin_hbm, f32[2,8,512]{2,1,0:T(8,128)} %constant.59.clone.win_hbm, bf16[2,256,256]{2,1,0:T(8,128)(2,1)} %constant.60.clone.wave_hbm, ...), custom_call_target="tpu_custom_call" | custom-call | tf_op jit(solution)/shard_map/stage_one/pallas_call | solution.py:549
  3.1 7.4 %all-to-all-start = ((bf16[16,16,2176]{2,1,0:T(8,128)(2,1)}), bf16[16,16,2176]{2,1,0:T(8,128)(2,1)S(1)}, u32[]{:S(2)}, u32[]{:S(2)}) async-start(bf16[16,16,2176]{2,1,0:T(8,128)(2,1)} %bitcast.2), calls=%async_computation | async-start | bytes 2228224 | tf_op jit(solution)/shard_map/all_to_all | solution.py:573
  10.5 1.3 %forward_tables.1 = (bf16[2,512,512]{2,1,0:T(8,128)(2,1)S(1)}, f32[16,1024]{1,0:T(8,128)S(1)}, f32[16,1024]{1,0:T(8,128)S(1)}) custom-call(f32[16,512]{1,0:T(8,128)} %constant.61.clone.fore_c, f32[16,512]{1,0:T(8,128)} %constant.62.clone.fore_s, f32[1,512]{1,0:T(1,128)} %constant.63.clone.fore_rc, f32[1,512]{1,0:T(1,128)} %constant.64.clone.fore_rs, ...), custom_call_target="tpu_custom_call" | custom-call | flops 10000000 | bytes 20000000 | tf_op jit(solution)/shard_map/forward_tables/pallas_call | solution.py:598
  11.8 22.6 %all-to-all-done.moved = bf16[16,16,2176]{2,1,0:T(8,128)(2,1)S(1)} async-done(((bf16[16,16,2176]{2,1,0:T(8,128)(2,1)}), bf16[16,16,2176]{2,1,0:T(8,128)(2,1)S(1)}, u32[]{:S(2)}, u32[]{:S(2)}) %all-to-all-start) | async-done | bytes 1114144 | tf_op jit(solution)/shard_map/all_to_all | solution.py:573
  34.5 1.4 %stage_two.1 = bf16[32,1536]{1,0:T(8,128)(2,1)S(1)} custom-call(bf16[16,16,2176]{2,1,0:T(8,128)(2,1)S(1)} %all-to-all-done.moved, f32[16,1024]{1,0:T(8,128)S(1)} %get-tuple-element.20.near_c, f32[16,1024]{1,0:T(8,128)S(1)} %get-tuple-element.21.near_s, f32[1,1024]{1,0:T(1,128)} %constant.85.clone.mid_c_hbm, f32[1,1024]{1,0:T(1,128)} %constant.86.clone.mid_s_hbm, ...), custom_call_target="tpu_custom_call" | custom-call | flops 1000000000 | bytes 4000000 | tf_op jit(solution)/shard_map/stage_two/pallas_call | solution.py:681
  35.8 0.0 copy-start
  35.9 0.0 copy-start.1
  35.9 5.5 %collective-permute-start = (bf16[32,1536]{1,0:T(8,128)(2,1)S(1)}, bf16[32,1536]{1,0:T(8,128)(2,1)S(1)}, u32[]{:S(2)}, u32[]{:S(2)}) collective-permute-start(bf16[32,1536]{1,0:T(8,128)(2,1)S(1)} %stage_two.1), channel_id=1, source_target_pairs={{0,8},{1,9},{2,10},{3,11},{4,12},{5,13},{6,14},{7,15},{8,0},{9,1},... | collective-permute-start | bytes 294920 | tf_op jit(solution)/shard_map/ppermute | solution.py:522
  41.4 0.0 collective-permute-start.7
  41.4 1.4 %collective-permute-start.10 = (bf16[32,1536]{1,0:T(8,128)(2,1)S(1)}, bf16[32,1536]{1,0:T(8,128)(2,1)S(1)}, u32[]{:S(2)}, u32[]{:S(2)}) collective-permute-start(bf16[32,1536]{1,0:T(8,128)(2,1)S(1)} %stage_two.1), channel_id=1, source_target_pairs={{0,2},{1,3},{2,0},{3,1},{4,6},{5,7},{6,4},{7,5},{8,10},{9,11},{10,... | collective-permute-start | bytes 294920 | tf_op jit(solution)/shard_map/ppermute | solution.py:522
  42.8 1.5 %column_tables.1 = (bf16[512,1024]{1,0:T(8,128)(2,1)S(1)}, bf16[2,256,256]{2,1,0:T(8,128)(2,1)S(1)}, bf16[256,256]{1,0:T(8,128)(2,1)S(1)}) custom-call(f32[16,512]{1,0:T(8,128)} %constant.81.clone.cols_c, f32[16,512]{1,0:T(8,128)} %constant.82.clone.cols_s, f32[1,512]{1,0:T(1,128)} %constant.83.clone.cols_rc, f32[1,512]{1,0:T(1,128)} %constant.84.clone.cols_rs), custom_call_target="tpu_custom_call" | custom-call | flops 10000000 | bytes 10000000 | tf_op jit(solution)/shard_map/column_tables/pallas_call | solution.py:661
  44.3 1.2 %inverse_tables.1 = (bf16[512,1024]{1,0:T(8,128)(2,1)S(1)}, bf16[512,1024]{1,0:T(8,128)(2,1)S(1)}) custom-call(f32[16,512]{1,0:T(8,128)} %constant.69.clone.even_c, f32[16,512]{1,0:T(8,128)} %constant.70.clone.even_s, f32[16,512]{1,0:T(8,128)} %constant.71.clone.odd_c, f32[16,512]{1,0:T(8,128)} %constant.72.clone.odd_s, f32[1,512]{1,0:T(1,128)} %constant.73.clone.rows_rc, ...), custom_call_target="tpu_custom_call" | custom-call | flops 10000000 | bytes 20000000 | tf_op jit(solution)/shard_map/inverse_tables/pallas_call | solution.py:641
  45.5 1.8 %lift_tables.1 = (f32[512,1024]{1,0:T(8,128)S(1)}, f32[512,1024]{1,0:T(8,128)S(1)}) custom-call(f32[2,16,1024]{2,1,0:T(8,128)} %constant.75.clone.lift_c, f32[2,16,1024]{2,1,0:T(8,128)} %constant.76.clone.lift_s, f32[16,1024]{1,0:T(8,128)} %constant.77.clone.lift_rc, f32[16,1024]{1,0:T(8,128)} %constant.78.clone.lift_rs, f32[16,1024]{1,0:T(8,128)} %constant.79.clone.mid_c, ...), custom_call_target="tpu_custom_call" | custom-call | flops 10000000 | bytes 10000000 | tf_op jit(solution)/shard_map/lift_tables/pallas_call | solution.py:651
  47.3 0.1 slice.14.own
  47.4 1.6 %collective-permute-start.12 = (bf16[16,16,1024]{2,1,0:T(8,128)(2,1)S(1)}, bf16[16,16,1024]{2,1,0:T(8,128)(2,1)S(1)}, u32[]{:S(2)}, u32[]{:S(2)}) collective-permute-start(bf16[16,16,1024]{2,1,0:T(8,128)(2,1)S(1)} %slice.14.own), channel_id=1, source_target_pairs={{0,16},{16,0},{1,17},{17,1},{2,18},{18,2},{3,19},{19,3},{4,20},{20... | collective-permute-start | bytes 1572872 | tf_op jit(solution)/shard_map/ppermute | solution.py:577
  49.0 0.0 collective-permute-done
  49.0 0.6 collective-permute-start.3
  49.5 2.0 %collective-permute-start.1 = (bf16[32,1536]{1,0:T(8,128)(2,1)S(1)}, bf16[32,1536]{1,0:T(8,128)(2,1)S(1)}, u32[]{:S(2)}, u32[]{:S(2)}) collective-permute-start(bf16[32,1536]{1,0:T(8,128)(2,1)S(1)} %collective-permute-done), channel_id=1, source_target_pairs={{0,4},{1,5},{2,6},{3,7},{4,0},{5,1},{6,2},{7,3},{8,12},{9,13},{10,... | collective-permute-start | bytes 294920 | tf_op jit(solution)/shard_map/ppermute | solution.py:522
  51.6 0.0 collective-permute-done.7
  51.6 0.0 collective-permute-start.8
  51.6 0.0 collective-permute-done.10
  51.6 0.1 pad_maximum_fusion.near
  51.6 0.1 collective-permute-start.11
  51.7 2.4 %collective-permute-done.3.ten = bf16[32,1536]{1,0:T(8,128)(2,1)S(1)} collective-permute-done((bf16[32,1536]{1,0:T(8,128)(2,1)S(1)}, bf16[32,1536]{1,0:T(8,128)(2,1)S(1)}, u32[]{:S(2)}, u32[]{:S(2)}) %collective-permute-start.3) | collective-permute-done | bytes 98336 | tf_op jit(solution)/shard_map/ppermute | solution.py:522
  54.1 0.6 collective-permute-start.4
  54.7 0.0 collective-permute-done.1.far
  54.7 1.8 %collective-permute-start.2 = (bf16[16,1536]{1,0:T(8,128)(2,1)S(1)}, bf16[16,1536]{1,0:T(8,128)(2,1)S(1)}, u32[]{:S(2)}, u32[]{:S(2)}) collective-permute-start(bf16[16,1536]{1,0:T(8,128)(2,1)S(1)} %slice.12), channel_id=1, source_target_pairs={{0,2},{1,3},{2,0},{3,1},{4,6},{5,7},{6,4},{7,5},{8,10},{9,11},{10,... | collective-permute-start | bytes 147464 | tf_op jit(solution)/shard_map/ppermute | solution.py:522
  56.5 0.0 collective-permute-done.8.six
  56.5 0.1 collective-permute-start.9
  56.6 1.6 %collective-permute-done.4 = bf16[16,1536]{1,0:T(8,128)(2,1)S(1)} collective-permute-done((bf16[16,1536]{1,0:T(8,128)(2,1)S(1)}, bf16[16,1536]{1,0:T(8,128)(2,1)S(1)}, u32[]{:S(2)}, u32[]{:S(2)}) %collective-permute-start.4) | collective-permute-done | bytes 49184 | tf_op jit(solution)/shard_map/ppermute | solution.py:522
  58.2 0.0 collective-permute-start.6
  58.2 0.6 collective-permute-done.2
  58.9 0.0 collective-permute-start.5
  58.9 0.6 collective-permute-done.6
  59.5 0.6 collective-permute-done.5
  60.1 0.8 %collective-permute-done.12.other = bf16[16,16,1024]{2,1,0:T(8,128)(2,1)S(1)} collective-permute-done((bf16[16,16,1024]{2,1,0:T(8,128)(2,1)S(1)}, bf16[16,16,1024]{2,1,0:T(8,128)(2,1)S(1)}, u32[]{:S(2)}, u32[]{:S(2)}) %collective-permute-start.12) | collective-permute-done | bytes 524320 | tf_op jit(solution)/shard_map/ppermute | solution.py:577
  60.8 0.0 copy-done
  60.9 0.0 copy-done.1
  60.9 1.3 %choose.1.chosen = bf16[512,1024]{1,0:T(8,128)(2,1)S(1)} custom-call(s32[16]{0:T(128)S(1)} %copy-done, s32[16]{0:T(128)S(1)} %copy-done.1, bf16[16,16,1024]{2,1,0:T(8,128)(2,1)S(1)} %slice.14.own, bf16[16,16,1024]{2,1,0:T(8,128)(2,1)S(1)} %collective-permute-done.12.other, bf16[2,256,256]{2,1,0:T(8,128)(2,1)S(1)} %get-tuple-element.23.by_rows, ...), custom_call_target="tpu_custom_call" | custom-call | flops 1000000000 | bytes 4000000 | tf_op jit(solution)/shard_map/choose/pallas_call | solution.py:713
  62.2 0.0 collective-permute-done.11.theirs
  62.2 1.0 %early.1 = (bf16[1024,1024]{1,0:T(8,128)(2,1)S(1)}, f32[16,512]{1,0:T(8,128)S(1)}) custom-call(bf16[4,32,1536]{2,1,0:T(8,128)(2,1)S(1)} %pad_maximum_fusion.near, bf16[4,32,1536]{2,1,0:T(8,128)(2,1)S(1)} %collective-permute-done.11.theirs, bf16[512,1024]{1,0:T(8,128)(2,1)S(1)} %choose.1.chosen, bf16[512,1024]{1,0:T(8,128)(2,1)S(1)} %get-tuple-element.25.refs_0_, ...), custom_call_target="tpu_custom_call" | custom-call | flops 1000000000 | bytes 4000000 | tf_op jit(solution)/shard_map/early/pallas_call | solution.py:727
  63.3 0.0 collective-permute-done.9.theirs
  63.3 0.8 %middle.1 = (bf16[1024,1024]{1,0:T(8,128)(2,1)S(1)}, f32[16,512]{1,0:T(8,128)S(1)}) custom-call(bf16[32,1536]{1,0:T(8,128)(2,1)S(1)} %collective-permute-done.8.six, bf16[32,1536]{1,0:T(8,128)(2,1)S(1)} %collective-permute-done.3.ten, bf16[32,1536]{1,0:T(8,128)(2,1)S(1)} %collective-permute-done.1.far, ...), custom_call_target="tpu_custom_call", output_to_operand_aliasing={{0}: (4, {})} | custom-call | flops 1000000000 | bytes 4000000 | tf_op jit(solution)/shard_map/middle/pallas_call | solution.py:739
  64.1 3.0 %late.1 = (bf16[1,512,1024]{2,1,0:T(8,128)(2,1)}, bf16[1024,1024]{1,0:T(8,128)(2,1)S(1)}) custom-call(bf16[32,1536]{1,0:T(8,128)(2,1)S(1)} %pad_maximum_fusion.2.last, bf16[32,1536]{1,0:T(8,128)(2,1)S(1)} %pad_maximum_fusion.3.theirs, bf16[1024,1024]{1,0:T(8,128)(2,1)S(1)} %get-tuple-element.31.early, ...), custom_call_target="tpu_custom_call", output_to_operand_aliasing={{1}: (2, {})} | custom-call | tf_op jit(solution)/shard_map/late/pallas_call | solution.py:740
  (5 shorter events, 0.1 us)
Async XLA Ops:
  3.1 31.4 %all-to-all-start = ((bf16[16,16,2176]{2,1,0:T(8,128)(2,1)}), bf16[16,16,2176]{2,1,0:T(8,128)(2,1)S(1)}, u32[]{:S(2)}, u32[]{:S(2)}) async-start(bf16[16,16,2176]{2,1,0:T(8,128)(2,1)} %bitcast.2), calls=%async_computation | async-start | bytes 2228224 | tf_op jit(solution)/shard_map/all_to_all | solution.py:573
  35.8 25.0 %copy-start = (s32[16]{0:T(128)S(1)}, s32[16]{0:T(128)}, u32[]{:S(2)}) copy-start(s32[16]{0:T(128)} %order.1) | copy-start | bytes 196
  35.9 25.0 %copy-start.1 = (s32[16]{0:T(128)S(1)}, s32[16]{0:T(128)}, u32[]{:S(2)}) copy-start(s32[16]{0:T(128)} %cuts.1) | copy-start | bytes 196
  35.9 13.1 %collective-permute-start = (bf16[32,1536]{1,0:T(8,128)(2,1)S(1)}, bf16[32,1536]{1,0:T(8,128)(2,1)S(1)}, u32[]{:S(2)}, u32[]{:S(2)}) collective-permute-start(bf16[32,1536]{1,0:T(8,128)(2,1)S(1)} %stage_two.1), channel_id=1, source_target_pairs={{0,8},{1,9},{2,10},{3,11},{4,12},{5,13},{6,14},{7,15},{8,0},{9,1},... | collective-permute-start | bytes 294920 | tf_op jit(solution)/shard_map/ppermute | solution.py:522
  41.4 10.2 %collective-permute-start.7 = (bf16[32,1536]{1,0:T(8,128)(2,1)S(1)}, bf16[32,1536]{1,0:T(8,128)(2,1)S(1)}, u32[]{:S(2)}, u32[]{:S(2)}) collective-permute-start(bf16[32,1536]{1,0:T(8,128)(2,1)S(1)} %stage_two.1), channel_id=1, source_target_pairs={{0,4},{1,5},{2,6},{3,7},{4,0},{5,1},{6,2},{7,3},{8,12},{9,13},{10,... | collective-permute-start | bytes 294920 | tf_op jit(solution)/shard_map/ppermute | solution.py:522
  41.4 10.2 %collective-permute-start.10 = (bf16[32,1536]{1,0:T(8,128)(2,1)S(1)}, bf16[32,1536]{1,0:T(8,128)(2,1)S(1)}, u32[]{:S(2)}, u32[]{:S(2)}) collective-permute-start(bf16[32,1536]{1,0:T(8,128)(2,1)S(1)} %stage_two.1), channel_id=1, source_target_pairs={{0,2},{1,3},{2,0},{3,1},{4,6},{5,7},{6,4},{7,5},{8,10},{9,11},{10,... | collective-permute-start | bytes 294920 | tf_op jit(solution)/shard_map/ppermute | solution.py:522
  47.4 13.4 %collective-permute-start.12 = (bf16[16,16,1024]{2,1,0:T(8,128)(2,1)S(1)}, bf16[16,16,1024]{2,1,0:T(8,128)(2,1)S(1)}, u32[]{:S(2)}, u32[]{:S(2)}) collective-permute-start(bf16[16,16,1024]{2,1,0:T(8,128)(2,1)S(1)} %slice.14.own), channel_id=1, source_target_pairs={{0,16},{16,0},{1,17},{17,1},{2,18},{18,2},{3,19},{19,3},{4,20},{20... | collective-permute-start | bytes 1572872 | tf_op jit(solution)/shard_map/ppermute | solution.py:577
  49.0 5.2 %collective-permute-start.3 = (bf16[32,1536]{1,0:T(8,128)(2,1)S(1)}, bf16[32,1536]{1,0:T(8,128)(2,1)S(1)}, u32[]{:S(2)}, u32[]{:S(2)}) collective-permute-start(bf16[32,1536]{1,0:T(8,128)(2,1)S(1)} %collective-permute-done), channel_id=1, source_target_pairs={{0,2},{1,3},{2,0},{3,1},{4,6},{5,7},{6,4},{7,5},{8,10},{9,11},{10,... | collective-permute-start | bytes 294920 | tf_op jit(solution)/shard_map/ppermute | solution.py:522
  49.5 5.2 %collective-permute-start.1 = (bf16[32,1536]{1,0:T(8,128)(2,1)S(1)}, bf16[32,1536]{1,0:T(8,128)(2,1)S(1)}, u32[]{:S(2)}, u32[]{:S(2)}) collective-permute-start(bf16[32,1536]{1,0:T(8,128)(2,1)S(1)} %collective-permute-done), channel_id=1, source_target_pairs={{0,4},{1,5},{2,6},{3,7},{4,0},{5,1},{6,2},{7,3},{8,12},{9,13},{10,... | collective-permute-start | bytes 294920 | tf_op jit(solution)/shard_map/ppermute | solution.py:522
  51.6 4.9 %collective-permute-start.8 = (bf16[32,1536]{1,0:T(8,128)(2,1)S(1)}, bf16[32,1536]{1,0:T(8,128)(2,1)S(1)}, u32[]{:S(2)}, u32[]{:S(2)}) collective-permute-start(bf16[32,1536]{1,0:T(8,128)(2,1)S(1)} %collective-permute-done.7), channel_id=1, source_target_pairs={{0,2},{1,3},{2,0},{3,1},{4,6},{5,7},{6,4},{7,5},{8,10},{9,11},{10,... | collective-permute-start | bytes 294920 | tf_op jit(solution)/shard_map/ppermute | solution.py:522
  51.6 10.6 %collective-permute-start.11 = (bf16[4,32,1536]{2,1,0:T(8,128)(2,1)S(1)}, bf16[4,32,1536]{2,1,0:T(8,128)(2,1)S(1)}, u32[]{:S(2)}, u32[]{:S(2)}) collective-permute-start(bf16[4,32,1536]{2,1,0:T(8,128)(2,1)S(1)} %pad_maximum_fusion.near), channel_id=1, source_target_pairs={{0,1},{1,0},{2,3},{3,2},{4,5},{5,4},{6,7},{7,6},{8,9},{9,8},{10,11... | collective-permute-start | bytes 1179656 | tf_op jit(solution)/shard_map/ppermute | solution.py:522
  54.1 4.1 %collective-permute-start.4 = (bf16[16,1536]{1,0:T(8,128)(2,1)S(1)}, bf16[16,1536]{1,0:T(8,128)(2,1)S(1)}, u32[]{:S(2)}, u32[]{:S(2)}) collective-permute-start(bf16[16,1536]{1,0:T(8,128)(2,1)S(1)} %slice.13), channel_id=1, source_target_pairs={{0,4},{1,5},{2,6},{3,7},{4,0},{5,1},{6,2},{7,3},{8,12},{9,13},{10,... | collective-permute-start | bytes 147464 | tf_op jit(solution)/shard_map/ppermute | solution.py:522
  54.7 4.2 %collective-permute-start.2 = (bf16[16,1536]{1,0:T(8,128)(2,1)S(1)}, bf16[16,1536]{1,0:T(8,128)(2,1)S(1)}, u32[]{:S(2)}, u32[]{:S(2)}) collective-permute-start(bf16[16,1536]{1,0:T(8,128)(2,1)S(1)} %slice.12), channel_id=1, source_target_pairs={{0,2},{1,3},{2,0},{3,1},{4,6},{5,7},{6,4},{7,5},{8,10},{9,11},{10,... | collective-permute-start | bytes 147464 | tf_op jit(solution)/shard_map/ppermute | solution.py:522
  56.5 6.7 %collective-permute-start.9 = (bf16[3,32,1536]{2,1,0:T(8,128)(2,1)S(1)}, bf16[3,32,1536]{2,1,0:T(8,128)(2,1)S(1)}, u32[]{:S(2)}, u32[]{:S(2)}) collective-permute-start(bf16[3,32,1536]{2,1,0:T(8,128)(2,1)S(1)} %pad_maximum_fusion.1), channel_id=1, source_target_pairs={{0,1},{1,0},{2,3},{3,2},{4,5},{5,4},{6,7},{7,6},{8,9},{9,8},{10,11... | collective-permute-start | bytes 884744 | tf_op jit(solution)/shard_map/ppermute | solution.py:522
  58.2 1.2 %collective-permute-start.6 = (bf16[16,1536]{1,0:T(8,128)(2,1)S(1)}, bf16[16,1536]{1,0:T(8,128)(2,1)S(1)}, u32[]{:S(2)}, u32[]{:S(2)}) collective-permute-start(bf16[16,1536]{1,0:T(8,128)(2,1)S(1)} %collective-permute-done.4), channel_id=1, source_target_pairs={{0,1},{1,0},{2,3},{3,2},{4,5},{5,4},{6,7},{7,6},{8,9},{9,8},{10,11... | collective-permute-start | bytes 147464 | tf_op jit(solution)/shard_map/ppermute | solution.py:522
  58.9 1.2 %collective-permute-start.5 = (bf16[16,1536]{1,0:T(8,128)(2,1)S(1)}, bf16[16,1536]{1,0:T(8,128)(2,1)S(1)}, u32[]{:S(2)}, u32[]{:S(2)}) collective-permute-start(bf16[16,1536]{1,0:T(8,128)(2,1)S(1)} %collective-permute-done.2), channel_id=1, source_target_pairs={{0,1},{1,0},{2,3},{3,2},{4,5},{5,4},{6,7},{7,6},{8,9},{9,8},{10,11... | collective-permute-start | bytes 147464 | tf_op jit(solution)/shard_map/ppermute | solution.py:522
